TPU v7x, 32 devices: a whole 2x2x4 slice. The times are simulated.
32 devices in a mesh: dp: 2 (over x), ctx: 4 (over z), tp: 4 (over y, core).
Axes of the slice: x: 2, y: 2, z: 4, core: 2. Of those that a mesh axis runs over, the one named last changes fastest.
Arguments:
- prompt_x: bfloat16 [4, 2048, 768], P('dp', 'ctx'), may hold values from -6 to 6
- cont_x: bfloat16 [16, 256, 768], P(('dp', 'ctx')), may hold values from -6 to 6
- prompt_hist: bfloat16 [4, 4, 2048, 768], P(None, 'dp', 'ctx'), may hold values from -6 to 6
- cont_hist: bfloat16 [4, 16, 256, 768], P(None, ('dp', 'ctx')), may hold values from -6 to 6
- teacher: bfloat16 [16, 256, 768], P(('dp', 'ctx')), may hold values from -6 to 6
- valid_mask: int32 [16, 256], P(('dp', 'ctx')), may hold values 0 or 1
- cont_group: int32 [16], P(('dp', 'ctx')), may hold values from 0 to 1
- layer_ids: int32 [4], replicated, may hold values from 0 to 3, each once
- dwa_weights: float32 [5], replicated, may hold values from 0.3 to 1
- qkv_weight: bfloat16 [768, 3, 768], P('dp', None, 'tp'), may hold values from -0.21875 to 0.21875
- out_weight: bfloat16 [768, 768], P('tp', 'dp'), may hold values from -1.75 to 1.75
- up_weight: bfloat16 [768, 3072], P('dp', 'tp'), may hold values from -0.21875 to 0.21875
- down_weight: bfloat16 [3072, 768], P('tp', 'dp'), may hold values from -0.109375 to 0.109375
- ln1_gain: bfloat16 [768], P('dp'), may hold values from 0.5 to 1.5
- ln1_bias: bfloat16 [768], P('dp'), may hold values from -1.5 to 1.5
- ln2_gain: bfloat16 [768], P('dp'), may hold values from 0.5 to 1.5
- ln2_bias: bfloat16 [768], P('dp'), may hold values from -1.5 to 1.5
Outputs:
- prompt_out: bfloat16 [4, 2048, 768], P('dp', 'ctx')
- cont_out: bfloat16 [16, 256, 768], P(('dp', 'ctx'))
- loss: float32 [], replicated
- prompt_grad: bfloat16 [4, 2048, 768], P('dp', 'ctx')
- cont_grad: bfloat16 [16, 256, 768], P(('dp', 'ctx'))
- qkv_grad: float32 [768, 3, 768], P('dp', None, 'tp')
- out_grad: float32 [768, 768], P('tp', 'dp')
- up_grad: float32 [768, 3072], P('dp', 'tp')
- down_grad: float32 [3072, 768], P('tp', 'dp')
- ln1_gain_grad: float32 [768], P('dp')
- ln1_bias_grad: float32 [768], P('dp')
- ln2_gain_grad: float32 [768], P('dp')
- ln2_bias_grad: float32 [768], P('dp')
- dwa_grad: float32 [5], replicated
Inputs may be any that keep to these rules, and one draw needn't show every extreme that they name: `cont_group`: each continuation names one of the 2 prompts held at its own dp index. `layer_ids`: each depth 0 to 3 is stored exactly once.
All inputs are finite; a program needn't handle non-finite values. No bound on the sum of `valid_mask` on one device may be relied on, other than what follows from the above.
Results may differ from a plain program's by a relative error of at most 0.015.
Values may be sent and summed in bfloat16 or wider, within the bound.
A program may use at most 512 MiB of HBM per device.

v0:
```python
import math

import jax
import jax.numpy as jnp
from jax import lax
from jax.sharding import PartitionSpec as P

HEAD_DIM = 64


EPS = 1e-05
NEG = -1e30
HIGH = lax.Precision.HIGHEST


def norm_pieces(x, norm_gain, norm_bias):
    row_mean = jnp.mean(x, -1, keepdims=True)
    centered_input = x - row_mean
    var = jnp.mean(centered_input * centered_input, -1, keepdims=True)
    inverse_deviation = lax.rsqrt(var + EPS)
    whitened_input = centered_input * inverse_deviation
    return (whitened_input * norm_gain + norm_bias, whitened_input, inverse_deviation)


def norm_backward(normalized_gradient, whitened_input, inverse_deviation, norm_gain):
    whitened_gradient = normalized_gradient * norm_gain
    return inverse_deviation * (
        whitened_gradient
        - jnp.mean(whitened_gradient, -1, keepdims=True)
        - whitened_input * jnp.mean(whitened_gradient * whitened_input, -1, keepdims=True)
    )


def rope_tables(positions):
    half = HEAD_DIM // 2
    freq = jnp.exp(jnp.arange(half, dtype=jnp.float32) * (-2.0 * math.log(10000.0) / HEAD_DIM))
    angle = positions.astype(jnp.float32)[:, None] * freq[None, :]
    cosine = jnp.cos(angle)
    sine = jnp.sin(angle)
    return (jnp.concatenate([cosine, cosine], -1), jnp.concatenate([sine, sine], -1))


def rotate_rows(x, cosine, sine):
    half = x.shape[-1] // 2
    turned = jnp.concatenate([-x[..., half:], x[..., :half]], -1)
    return x * cosine + turned * sine


def gelu_tanh(value):
    return jax.nn.gelu(value, approximate=True)


def token_major(x):
    batch, heads, length, size = x.shape
    return x.transpose(0, 2, 1, 3).reshape(batch * length, heads * size)


def per_device(
    prompt_x,
    cont_x,
    prompt_hist,
    cont_hist,
    teacher,
    valid_mask,
    cont_group,
    layer_ids,
    dwa_weights,
    qkv_weight,
    out_weight,
    up_weight,
    down_weight,
    ln1_gain,
    ln1_bias,
    ln2_gain,
    ln2_bias,
):
    f32 = jnp.float32
    bfloat16_cast = jnp.bfloat16
    qkv_w, out_w, up_w, down_w, first_gain, first_bias, second_gain, second_bias = (
        lax.all_gather(qkv_weight, "dp", axis=0, tiled=True),
        lax.all_gather(out_weight, "dp", axis=1, tiled=True),
        lax.all_gather(up_weight, "dp", axis=0, tiled=True),
        lax.all_gather(down_weight, "dp", axis=1, tiled=True),
        lax.all_gather(ln1_gain, "dp", axis=0, tiled=True),
        lax.all_gather(ln1_bias, "dp", axis=0, tiled=True),
        lax.all_gather(ln2_gain, "dp", axis=0, tiled=True),
        lax.all_gather(ln2_bias, "dp", axis=0, tiled=True),
    )
    first_gain = first_gain.astype(f32)
    first_bias = first_bias.astype(f32)
    second_gain = second_gain.astype(f32)
    second_bias = second_bias.astype(f32)
    prompt_groups, prompt_length, model_width = prompt_x.shape
    continuation_rows, continuation_length, _ = cont_x.shape
    local_width = qkv_w.shape[2]
    heads = local_width // HEAD_DIM
    scale = 1.0 / math.sqrt(HEAD_DIM)
    qkv_flat = qkv_w.reshape(model_width, 3 * local_width)
    prompt_pos = lax.axis_index("ctx") * prompt_length + jnp.arange(prompt_length, dtype=jnp.int32)
    p_cos, p_sin = rope_tables(prompt_pos)
    prompt_input = prompt_x.astype(f32).reshape(prompt_groups * prompt_length, model_width)
    prompt_normalized, prompt_first_whitened, prompt_first_inverse = norm_pieces(
        prompt_input, first_gain, first_bias
    )
    xn1_p = prompt_normalized.astype(bfloat16_cast)
    proj_p = (
        jnp.dot(xn1_p, qkv_flat, preferred_element_type=f32)
        .reshape(prompt_groups, prompt_length, 3, heads, HEAD_DIM)
        .transpose(2, 0, 3, 1, 4)
    )
    q_p = rotate_rows(proj_p[0], p_cos, p_sin).astype(bfloat16_cast)
    k_p = rotate_rows(proj_p[1], p_cos, p_sin).astype(bfloat16_cast)
    v_p = proj_p[2].astype(bfloat16_cast)
    prompt_keys, prompt_values = (
        lax.all_gather(k_p, "ctx", axis=2, tiled=True),
        lax.all_gather(v_p, "ctx", axis=2, tiled=True),
    )
    ptotal = prompt_keys.shape[2]
    scores_p = jnp.einsum("ghqd,ghkd->ghqk", q_p, prompt_keys, preferred_element_type=f32) * scale
    allowed_p = jnp.arange(ptotal, dtype=jnp.int32)[None, :] <= prompt_pos[:, None]
    masked_p = jnp.where(allowed_p[None, None], scores_p, NEG)
    top_p = jnp.max(masked_p, -1, keepdims=True)
    total_p = top_p + jnp.log(jnp.sum(jnp.exp(masked_p - top_p), -1, keepdims=True))
    probs_p = jnp.exp(masked_p - total_p)
    o_p = token_major(
        jnp.einsum(
            "ghqk,ghkd->ghqd",
            probs_p.astype(bfloat16_cast),
            prompt_values,
            preferred_element_type=f32,
        ).astype(bfloat16_cast)
    )
    cont_pos = ptotal + jnp.arange(continuation_length, dtype=jnp.int32)
    c_cos, c_sin = rope_tables(cont_pos)
    continuation_input = cont_x.astype(f32).reshape(
        continuation_rows * continuation_length, model_width
    )
    continuation_normalized, continuation_first_whitened, continuation_first_inverse = norm_pieces(
        continuation_input, first_gain, first_bias
    )
    xn1_c = continuation_normalized.astype(bfloat16_cast)
    proj_c = (
        jnp.dot(xn1_c, qkv_flat, preferred_element_type=f32)
        .reshape(continuation_rows, continuation_length, 3, heads, HEAD_DIM)
        .transpose(2, 0, 3, 1, 4)
    )
    q_c = rotate_rows(proj_c[0], c_cos, c_sin).astype(bfloat16_cast)
    k_c = rotate_rows(proj_c[1], c_cos, c_sin).astype(bfloat16_cast)
    v_c = proj_c[2].astype(bfloat16_cast)
    picked_keys = jnp.take(prompt_keys, cont_group, axis=0)
    picked_values = jnp.take(prompt_values, cont_group, axis=0)
    steps_idx = jnp.arange(continuation_length, dtype=jnp.int32)
    causal = steps_idx[None, :] <= steps_idx[:, None]
    self_ok = (causal[None] & (valid_mask[:, None, :] == 1))[:, None]

    def cont_scores():
        outer = jnp.einsum("chqd,chkd->chqk", q_c, picked_keys, preferred_element_type=f32) * scale
        inner = jnp.where(
            self_ok,
            jnp.einsum("chqd,chkd->chqk", q_c, k_c, preferred_element_type=f32) * scale,
            NEG,
        )
        return (outer, inner)

    outer_scores, inner_scores = cont_scores()
    top_c = jnp.maximum(
        jnp.max(outer_scores, -1, keepdims=True), jnp.max(inner_scores, -1, keepdims=True)
    )
    total_c = top_c + jnp.log(
        jnp.sum(jnp.exp(outer_scores - top_c), -1, keepdims=True)
        + jnp.sum(jnp.exp(inner_scores - top_c), -1, keepdims=True)
    )
    outer_probs = jnp.exp(outer_scores - total_c)
    inner_probs = jnp.exp(inner_scores - total_c)
    o_heads = jnp.einsum(
        "chqk,chkd->chqd",
        outer_probs.astype(bfloat16_cast),
        picked_values,
        preferred_element_type=f32,
    ) + jnp.einsum(
        "chqk,chkd->chqd", inner_probs.astype(bfloat16_cast), v_c, preferred_element_type=f32
    )
    o_c = token_major(o_heads.astype(bfloat16_cast))
    part_p = jnp.dot(o_p, out_w, preferred_element_type=f32)
    part_c = jnp.dot(o_c, out_w, preferred_element_type=f32)
    hist_p = prompt_hist.reshape(4, -1, model_width)
    hist_c = cont_hist.reshape(4, -1, model_width)
    teach = teacher.reshape(-1, model_width)
    mask_rows = valid_mask.reshape(-1, 1)
    attn_p, attn_c = lax.psum((part_p, part_c), "tp")
    h1_p = prompt_input + attn_p
    continuation_hidden_first = continuation_input + attn_c
    normed2_p, _, _ = norm_pieces(h1_p, second_gain, second_bias)
    continuation_second_normalized, continuation_second_whitened, continuation_second_inverse = (
        norm_pieces(continuation_hidden_first, second_gain, second_bias)
    )
    xn2_p = normed2_p.astype(bfloat16_cast)
    xn2_c = continuation_second_normalized.astype(bfloat16_cast)
    upper_p = jnp.dot(xn2_p, up_w, preferred_element_type=f32)
    upper_c = jnp.dot(xn2_c, up_w, preferred_element_type=f32)
    hid_p = gelu_tanh(upper_p).astype(bfloat16_cast)
    hid_c = gelu_tanh(upper_c).astype(bfloat16_cast)
    mpart_p = jnp.dot(hid_p, down_w, preferred_element_type=f32)
    mpart_c = jnp.dot(hid_c, down_w, preferred_element_type=f32)
    mlp_p, mlp_c = (
        lax.psum(mpart_p.astype(jnp.bfloat16), "tp").astype(jnp.float32),
        lax.psum(mpart_c.astype(jnp.bfloat16), "tp").astype(jnp.float32),
    )
    y_p = h1_p + mlp_p
    y_c = continuation_hidden_first + mlp_c
    slot_pick = (layer_ids[:, None] == jnp.arange(4, dtype=jnp.int32)[None, :]).astype(f32)
    slot_w = jnp.sum(slot_pick * dwa_weights[None, :4], 1)
    mixed_p = dwa_weights[4] * y_p
    mixed_c = dwa_weights[4] * y_c
    for slot in range(4):
        mixed_p = mixed_p + slot_w[slot] * hist_p[slot].astype(f32)
        mixed_c = mixed_c + slot_w[slot] * hist_c[slot].astype(f32)
    maskf = mask_rows.astype(f32)
    diff = mixed_c - teach.astype(f32)
    weighted = maskf * diff
    err = jnp.sum(weighted * diff)
    count = jnp.sum(maskf)
    slot_terms = jnp.stack([jnp.sum(weighted * hist_c[slot].astype(f32)) for slot in range(4)])
    raw_dwa = jnp.concatenate(
        [jnp.sum(slot_pick * slot_terms[:, None], 0), jnp.sum(weighted * y_c)[None]]
    )
    err_all, count_all, dwa_all = lax.psum((err, count, raw_dwa), ("dp", "ctx"))
    denom = jnp.maximum(count_all, 1.0) * model_width
    loss = err_all / denom
    dwa_grad = dwa_all * (2.0 / denom)
    output_gradient = weighted * (2.0 * dwa_weights[4] / denom)
    out_p_r = mixed_p.astype(bfloat16_cast)
    out_c_r = mixed_c.astype(bfloat16_cast)
    dm_r = output_gradient.astype(bfloat16_cast)
    down_g = jnp.einsum("rf,rd->fd", hid_c, dm_r, preferred_element_type=f32)
    dhid = jnp.einsum("rd,fd->rf", dm_r, down_w, preferred_element_type=f32)
    _, gelu_back = jax.vjp(gelu_tanh, upper_c)
    du_r = gelu_back(dhid)[0].astype(bfloat16_cast)
    up_g = jnp.einsum("rd,rf->df", xn2_c, du_r, preferred_element_type=f32)
    part2 = jnp.einsum("rf,df->rd", du_r, up_w, preferred_element_type=f32)
    second_norm_gradient = lax.psum(part2.astype(jnp.bfloat16), "tp").astype(jnp.float32)
    hidden_first_gradient = output_gradient + norm_backward(
        second_norm_gradient, continuation_second_whitened, continuation_second_inverse, second_gain
    )
    da_r = hidden_first_gradient.astype(bfloat16_cast)
    second_gain_gradient = jnp.sum(second_norm_gradient * continuation_second_whitened, 0)
    bias2_g = jnp.sum(second_norm_gradient, 0)
    out_g = jnp.einsum("rf,rd->fd", o_c, da_r, preferred_element_type=f32)
    do_heads = (
        jnp.einsum("rd,fd->rf", da_r, out_w, preferred_element_type=f32)
        .astype(bfloat16_cast)
        .reshape(continuation_rows, continuation_length, heads, HEAD_DIM)
        .transpose(0, 2, 1, 3)
    )
    outer_again, inner_again = cont_scores()
    outer_probs = jnp.exp(outer_again - total_c)
    inner_probs = jnp.exp(inner_again - total_c)
    outer_dprobs = jnp.einsum(
        "chqd,chkd->chqk", do_heads, picked_values, preferred_element_type=f32
    )
    inner_dprobs = jnp.einsum("chqd,chkd->chqk", do_heads, v_c, preferred_element_type=f32)
    row_total = jnp.sum(outer_probs * outer_dprobs, -1, keepdims=True) + jnp.sum(
        inner_probs * inner_dprobs, -1, keepdims=True
    )
    outer_dscores = (outer_probs * (outer_dprobs - row_total)).astype(bfloat16_cast)
    inner_dscores = (inner_probs * (inner_dprobs - row_total)).astype(bfloat16_cast)
    dq = (
        jnp.einsum("chqk,chkd->chqd", outer_dscores, picked_keys, preferred_element_type=f32)
        + jnp.einsum("chqk,chkd->chqd", inner_dscores, k_c, preferred_element_type=f32)
    ) * scale
    dk_inner = jnp.einsum("chqk,chqd->chkd", inner_dscores, q_c, preferred_element_type=f32) * scale
    dv_inner = jnp.einsum(
        "chqk,chqd->chkd", inner_probs.astype(bfloat16_cast), do_heads, preferred_element_type=f32
    )
    dk_outer = jnp.einsum("chqk,chqd->chkd", outer_dscores, q_c, preferred_element_type=f32) * scale
    dv_outer = jnp.einsum(
        "chqk,chqd->chkd", outer_probs.astype(bfloat16_cast), do_heads, preferred_element_type=f32
    )
    dq_r = token_major(rotate_rows(dq, c_cos, -c_sin).astype(bfloat16_cast))
    dk_self = token_major(rotate_rows(dk_inner, c_cos, -c_sin).astype(bfloat16_cast))
    dv_self = token_major(dv_inner.astype(bfloat16_cast))
    pick = (cont_group[:, None] == jnp.arange(prompt_groups, dtype=jnp.int32)[None, :]).astype(f32)
    dk_groups = jnp.einsum("cg,chkd->ghkd", pick, dk_outer, precision=HIGH)
    dv_groups = jnp.einsum("cg,chkd->ghkd", pick, dv_outer, precision=HIGH)
    dk_own, dv_own = (
        lax.psum_scatter(
            dk_groups.astype(jnp.bfloat16), "ctx", scatter_dimension=2, tiled=True
        ).astype(jnp.float32),
        lax.psum_scatter(
            dv_groups.astype(jnp.bfloat16), "ctx", scatter_dimension=2, tiled=True
        ).astype(jnp.float32),
    )
    dk_pr = token_major(rotate_rows(dk_own, p_cos, -p_sin).astype(bfloat16_cast))
    dv_pr = token_major(dv_own.astype(bfloat16_cast))
    dcat_c = jnp.concatenate([dq_r, dk_self, dv_self], 1)
    dkv_p = jnp.concatenate([dk_pr, dv_pr], 1)
    qkv_c = jnp.einsum("rd,rf->df", xn1_c, dcat_c, preferred_element_type=f32)
    kv_p = jnp.einsum("rd,rf->df", xn1_p, dkv_p, preferred_element_type=f32)
    qkv_g = (
        qkv_c + jnp.concatenate([jnp.zeros((model_width, local_width), f32), kv_p], 1)
    ).reshape(model_width, 3, local_width)
    part1_c = jnp.einsum("rf,df->rd", dcat_c, qkv_flat, preferred_element_type=f32)
    part1_p = jnp.einsum("rf,df->rd", dkv_p, qkv_flat[:, local_width:], preferred_element_type=f32)
    first_norm_continuation_gradient, first_norm_prompt_gradient = (
        lax.psum(part1_c.astype(jnp.bfloat16), "tp").astype(jnp.float32),
        lax.psum(part1_p.astype(jnp.bfloat16), "tp").astype(jnp.float32),
    )
    first_gain_gradient = jnp.sum(
        first_norm_continuation_gradient * continuation_first_whitened, 0
    ) + jnp.sum(first_norm_prompt_gradient * prompt_first_whitened, 0)
    bias1_g = jnp.sum(first_norm_continuation_gradient, 0) + jnp.sum(first_norm_prompt_gradient, 0)
    cont_grad = (
        (
            hidden_first_gradient
            + norm_backward(
                first_norm_continuation_gradient,
                continuation_first_whitened,
                continuation_first_inverse,
                first_gain,
            )
        )
        .astype(bfloat16_cast)
        .reshape(continuation_rows, continuation_length, model_width)
    )
    prompt_grad = (
        norm_backward(
            first_norm_prompt_gradient, prompt_first_whitened, prompt_first_inverse, first_gain
        )
        .astype(bfloat16_cast)
        .reshape(prompt_groups, prompt_length, model_width)
    )
    s_qkv, s_out, s_up, s_down, s_g1, s_b1, s_g2, s_b2 = (
        lax.psum_scatter(qkv_g.astype(jnp.bfloat16), "dp", scatter_dimension=0, tiled=True).astype(
            jnp.float32
        ),
        lax.psum_scatter(out_g.astype(jnp.bfloat16), "dp", scatter_dimension=1, tiled=True).astype(
            jnp.float32
        ),
        lax.psum_scatter(up_g.astype(jnp.bfloat16), "dp", scatter_dimension=0, tiled=True).astype(
            jnp.float32
        ),
        lax.psum_scatter(down_g.astype(jnp.bfloat16), "dp", scatter_dimension=1, tiled=True).astype(
            jnp.float32
        ),
        lax.psum_scatter(
            first_gain_gradient.astype(jnp.bfloat16), "dp", scatter_dimension=0, tiled=True
        ).astype(jnp.float32),
        lax.psum_scatter(
            bias1_g.astype(jnp.bfloat16), "dp", scatter_dimension=0, tiled=True
        ).astype(jnp.float32),
        lax.psum_scatter(
            second_gain_gradient.astype(jnp.bfloat16), "dp", scatter_dimension=0, tiled=True
        ).astype(jnp.float32),
        lax.psum_scatter(
            bias2_g.astype(jnp.bfloat16), "dp", scatter_dimension=0, tiled=True
        ).astype(jnp.float32),
    )
    r_qkv, r_out, r_up, r_down, r_g1, r_b1, r_g2, r_b2 = (
        lax.psum(s_qkv.astype(jnp.bfloat16), "ctx").astype(jnp.float32),
        lax.psum(s_out.astype(jnp.bfloat16), "ctx").astype(jnp.float32),
        lax.psum(s_up.astype(jnp.bfloat16), "ctx").astype(jnp.float32),
        lax.psum(s_down.astype(jnp.bfloat16), "ctx").astype(jnp.float32),
        lax.psum(s_g1.astype(jnp.bfloat16), "ctx").astype(jnp.float32),
        lax.psum(s_b1.astype(jnp.bfloat16), "ctx").astype(jnp.float32),
        lax.psum(s_g2.astype(jnp.bfloat16), "ctx").astype(jnp.float32),
        lax.psum(s_b2.astype(jnp.bfloat16), "ctx").astype(jnp.float32),
    )
    prompt_out = out_p_r.reshape(prompt_groups, prompt_length, model_width)
    cont_out = out_c_r.reshape(continuation_rows, continuation_length, model_width)
    return (
        prompt_out,
        cont_out,
        loss,
        prompt_grad,
        cont_grad,
        r_qkv,
        r_out,
        r_up,
        r_down,
        r_g1,
        r_b1,
        r_g2,
        r_b2,
        dwa_grad,
    )


def solution(mesh):
    in_specs = (
        P("dp", "ctx", None),
        P(("dp", "ctx"), None, None),
        P(None, "dp", "ctx", None),
        P(None, ("dp", "ctx"), None, None),
        P(("dp", "ctx"), None, None),
        P(("dp", "ctx"), None),
        P(("dp", "ctx")),
        P(),
        P(),
        P("dp", None, "tp"),
        P("tp", "dp"),
        P("dp", "tp"),
        P("tp", "dp"),
        P("dp"),
        P("dp"),
        P("dp"),
        P("dp"),
    )
    out_specs = (
        P("dp", "ctx", None),
        P(("dp", "ctx"), None, None),
        P(),
        P("dp", "ctx", None),
        P(("dp", "ctx"), None, None),
        P("dp", None, "tp"),
        P("tp", "dp"),
        P("dp", "tp"),
        P("tp", "dp"),
        P("dp"),
        P("dp"),
        P("dp"),
        P("dp"),
        P(),
    )
    return jax.shard_map(
        per_device, mesh=mesh, in_specs=in_specs, out_specs=out_specs, check_vma=False
    )
```

profile of v0, /device:TPU:0, one launch (start us, length us, event | category | flops | bytes accessed | tf_op | source)
XLA Modules:
  0.0 1058.1 jit_solution(7776467773823273445)
XLA Ops:
  19.2 10.8 %all_gather.32 = bf16[768,3,192]{0,2,1:T(8,128)(2,1)S(1)} all-gather(bf16[384,3,192]{0,2,1:T(8,128)(2,1)} %param.28), channel_id=1, replica_groups=mesh['dp'=2,'ctx'=4,'tp'=4] {'dp'}, dimensions={0}, use_global_device_ids=true | all-gather | bytes 1327104 | tf_op jit(solution)/shard_map/all_gather | solution.py:80
  55.7 22.9 %all-gather.10.cloned.1.call-done = bf16[2,3,2048,64]{2,3,1,0:T(8,128)(2,1)} async-done(((bf16[2,3,512,64]{2,3,1,0:T(8,128)(2,1)}), bf16[2,3,2048,64]{2,3,1,0:T(8,128)(2,1)}) %all-gather.10.cloned.1.call-update) | async-done | bytes 1572880 | tf_op jit(solution)/shard_map/all_gather | solution.py:115
  91.9 24.9 %all-gather.16.cloned.1.call-done = bf16[1,2,3,2048,64]{3,4,2,0,1:T(8,128)(2,1)} async-done(((bf16[1,2,3,512,64]{3,4,2,0,1:T(8,128)(2,1)}), bf16[1,2,3,2048,64]{3,4,2,0,1:T(8,128)(2,1)}) %all-gather.16.cloned.1.call-update) | async-done | bytes 1572880 | tf_op jit(solution)/shard_map/all_gather | solution.py:116
  127.9 11.8 %fusion = (f32[2,3,512]{2,1,0:T(4,128)S(1)}, f32[2,3,512,2048]{3,2,1,0:T(8,128)}) fusion(pred[512,2048]{1,0:T(8,128)(4,1)S(1)} %iota_compare_fusion, bf16[2,3,2048,64]{2,3,1,0:T(8,128)(2,1)S(1)} %copy-done.9, f32[2,3,512,32]{2,3,1,0:T(8,128)S(1)} %copy-done.29, f32[2,3,512,32]{2,3,1,0:T(8,128)S(1)} %copy-done.28, f32[512,64]{0,1:T(8,128)S(1)} %get-tuple-element.92, ...), kind=kOutput, calls=%fused_computation.5 | convolution fusion | flops 825160704 | bytes 29634560 | tf_op jit(solution)/shard_map/ghqd,ghkd->ghqk/dot_general | solution.py:119
  139.7 12.1 %exponential_reduce_fusion = f32[2,3,512]{2,1,0:T(4,128)S(1)} fusion(f32[2,3,512,2048]{3,2,1,0:T(8,128)} %get-tuple-element.114, f32[2,3,512]{2,1,0:T(4,128)S(1)} %get-tuple-element.113, pred[512,2048]{1,0:T(8,128)(4,1)S(1)} %iota_compare_fusion), kind=kLoop, calls=%fused_computation.3 | loop fusion | flops 25162752 | bytes 26238976 | tf_op jit(solution)/shard_map/reduce_sum | solution.py:123
  151.8 11.2 %fusion.97 = bf16[2,512,3,64]{1,3,2,0:T(8,128)(2,1)S(1)} fusion(f32[2,3,512,2048]{3,2,1,0:T(8,128)} %get-tuple-element.114, f32[2,3,512]{2,1,0:T(4,128)S(1)} %log_add_fusion, pred[512,2048]{1,0:T(8,128)(4,1)S(1)} %iota_compare_fusion, bf16[1,2,3,2048,64]{3,4,2,0,1:T(8,128)(2,1)S(1)} %copy-done.18), kind=kOutput, calls=%fused_computation.173 | convolution fusion | flops 830668800 | bytes 28192768 | tf_op jit(solution)/shard_map/ghqk,ghkd->ghqd/dot_general | solution.py:126
  174.1 16.1 %all-gather.4 = bf16[2,1,384]{2,1,0:T(2,128)(2,1)S(1)} all-gather(bf16[1,1,384]{2,1,0:T(2,128)(2,1)S(1)} %reshape.491), channel_id=1, replica_groups=mesh['dp'=2,'ctx'=4,'tp'=4] {'dp'}, dimensions={0}, use_global_device_ids=true | all-gather | bytes 2304 | tf_op jit(solution)/shard_map/all_gather | solution.py:87
  190.8 20.3 %psum.131 = f32[]{:T(128)} all-reduce(f32[]{:T(128)} %convert_reduce_fusion.8), channel_id=1, replica_groups=mesh['dp'=2,'ctx'=4,'tp'=4] {'dp','ctx'}, use_global_device_ids=true, to_apply=%region_22.24 | all-reduce | flops 1 | bytes 8 | tf_op jit(solution)/shard_map/psum | solution.py:227
  212.5 48.5 %all-reduce.24.cloned.1.call-done = (f32[1024,768]{1,0:T(8,128)}, f32[512,768]{1,0:T(8,128)}) async-done(((f32[1024,768]{1,0:T(8,128)}, f32[512,768]{1,0:T(8,128)}), (f32[1024,768]{1,0:T(8,128)}, f32[512,768]{1,0:T(8,128)})) %all-reduce.24.cloned.1.call-update) | async-done | bytes 4718608 | tf_op jit(solution)/shard_map/psum | solution.py:190
  274.5 30.7 %all-reduce.18.cloned.1.call-done = bf16[512,768]{1,0:T(8,128)(2,1)} async-done(((bf16[512,768]{1,0:T(8,128)(2,1)}), bf16[512,768]{1,0:T(8,128)(2,1)}) %all-reduce.18.cloned.1.call-update) | async-done | bytes 786448 | tf_op jit(solution)/shard_map/psum | solution.py:207
  318.7 34.8 %all-reduce.20.cloned.1.call-done = bf16[512,768]{1,0:T(8,128)(2,1)} async-done(((bf16[512,768]{1,0:T(8,128)(2,1)}), bf16[512,768]{1,0:T(8,128)(2,1)}) %all-reduce.20.cloned.1.call-update) | async-done | bytes 786448 | tf_op jit(solution)/shard_map/psum | solution.py:241
  379.5 153.4 %copy.92 = bf16[2,3,2048,64]{0,3,1,2:T(8,128)(2,1)} copy(bf16[2,3,2048,64]{2,0,3,1:T(2,128)(2,1)} %fusion.36) | data formatting | bytes 3145728
  532.9 135.2 %reshape.505 = bf16[2048,384]{1,0:T(8,128)(2,1)} reshape(bf16[2048,3,64,2]{3,2,1,0:T(8,128)(2,1)} %bitcast.61) | data formatting | bytes 3145728
  706.4 55.1 %reshape.506 = bf16[512,3,64,2]{3,2,1,0:T(8,128)(2,1)} reshape(bf16[512,384]{1,0:T(8,128)(2,1)} %reduce-scatter.19.cloned.1.call-done) | data formatting | bytes 786432
  761.5 26.2 %copy.93 = bf16[2,3,512,64]{2,0,3,1:T(2,128)(2,1)} copy(bf16[2,3,512,64]{0,3,1,2:T(8,128)(2,1)} %bitcast.286) | data formatting | bytes 786432
  798.8 39.3 %all-reduce.22.cloned.1.call-done = bf16[1024,768]{1,0:T(8,128)(2,1)} async-done(((bf16[1024,768]{1,0:T(8,128)(2,1)}), bf16[1024,768]{1,0:T(8,128)(2,1)}) %all-reduce.22.cloned.1.call-update) | async-done | bytes 1572880 | tf_op jit(solution)/shard_map/psum | solution.py:306
  863.5 10.2 convert_multiply_fusion.5
  873.8 33.6 %all-reduce.26.cloned.1.call-done = (bf16[1024,768]{1,0:T(8,128)(2,1)}, bf16[512,768]{1,0:T(8,128)(2,1)}) async-done(((bf16[1024,768]{1,0:T(8,128)(2,1)}, bf16[512,768]{1,0:T(8,128)(2,1)}), (bf16[1024,768]{1,0:T(8,128)(2,1)}, bf16[512,768]{1,0:T(8,128)(2,1)})) %all-reduce.26.cloned.1.call-update) | async-done | bytes 2359312 | tf_op jit(solution)/shard_map/psum | solution.py:206
  909.9 9.4 fusion.31
  930.8 11.2 %reduce-scatter.21.cloned.1.call-done = bf16[384,576]{1,0:T(8,128)(2,1)} async-done(((bf16[768,576]{1,0:T(8,128)(2,1)}), bf16[384,576]{1,0:T(8,128)(2,1)}) %reduce-scatter.21.cloned.1.call-update) | async-done | bytes 442384
  944.0 22.6 %reduce-scatter.17.cloned.1.call-done = bf16[384,768]{1,0:T(8,128)(2,1)} async-done(((bf16[768,768]{1,0:T(8,128)(2,1)}), bf16[384,768]{1,0:T(8,128)(2,1)}) %reduce-scatter.17.cloned.1.call-update) | async-done | bytes 589840 | tf_op jit(solution)/shard_map/reduce_scatter | solution.py:339
  970.1 22.4 %all-reduce.5 = (f32[]{:T(128)}, f32[5]{0:T(128)S(1)}) all-reduce(f32[]{:T(128)} %get-tuple-element.27, f32[5]{0:T(128)S(1)} %pad_maximum_fusion.5), channel_id=1, replica_groups=mesh['dp'=2,'ctx'=4,'tp'=4] {'dp','ctx'}, use_global_device_ids=true, to_apply=%region_20.22 | all-reduce | flops 6 | bytes 48 | tf_op jit(solution)/shard_map/psum | solution.py:227
  999.1 8.7 all-reduce.8
  1012.7 31.5 %all-reduce.28.cloned.1.call-done = (bf16[384,3,192]{0,2,1:T(8,128)(2,1)}, bf16[192,384]{1,0:T(8,128)(2,1)}, bf16[384,768]{1,0:T(8,128)(2,1)}, bf16[768,384]{1,0:T(8,128)(2,1)}) async-done(((bf16[384,3,192]{0,2,1:T(8,128)(2,1)}, bf16[192,384]{1,0:T(8,128)(2,1)}, bf16[384,768]{1,0:T(8,128)(2,1)}, bf16[768,384]{1,0:T(8,128)(2,1)}), (bf16[384,3,192]{0,2,1:T(8,128)(2,1)}, bf16[192,384]{1,0:T(8,128)(2,1)}, ...) | async-done | bytes 1769488 | tf_op jit(solution)/shard_map/psum | solution.py:359
  (380 shorter events, 234.1 us)
Async XLA Ops:
  8.0 70.6 %all-gather.10.cloned.1.call-start = ((), (), s32[]{:S(2)}) async-start(), calls=%async_computation.6 | async-start | bytes 1966080 | tf_op jit(solution)/shard_map/all_gather | solution.py:115
  37.7 90.1 %copy-start.15 = (f32[512,64]{0,1:T(8,128)}, f32[512,64]{0,1:T(8,128)S(1)}, u32[]{:S(2)}) copy-start(f32[512,64]{0,1:T(8,128)S(1)} %pad_maximum_fusion) | copy-start | bytes 393220
  39.9 76.8 %all-gather.16.cloned.1.call-start = ((), (), s32[]{:S(2)}) async-start(), calls=%async_computation.14 | async-start | bytes 1966080 | tf_op jit(solution)/shard_map/all_gather | solution.py:116
  41.9 219.1 %all-reduce.24.cloned.1.call-start = ((), (), s32[]{:S(2)}) async-start(), calls=%async_computation.19 | async-start | bytes 9437184 | tf_op jit(solution)/shard_map/psum | solution.py:190
  42.1 626.4 %copy-start.64 = (pred[2]{0:T(512)(128)(4,1)}, pred[2]{0:T(512)(128)(4,1)S(1)}, u32[]{:S(2)}) copy-start(pred[2]{0:T(512)(128)(4,1)S(1)} %compare_and_fusion) | copy-start | bytes 10
  167.8 95.4 %all-gather.12.cloned.1.call-start = ((), (), s32[]{:S(2)}) async-start(), calls=%async_computation.7 | async-start | bytes 1769472 | tf_op jit(solution)/shard_map/all_gather | solution.py:82
  168.4 98.2 %all-gather.14.cloned.1.call-start = ((), (), s32[]{:S(2)}) async-start(), calls=%async_computation.8 | async-start | bytes 1769472 | tf_op jit(solution)/shard_map/all_gather | solution.py:83
  169.0 136.2 %all-reduce.18.cloned.1.call-start = ((), (), s32[]{:S(2)}) async-start(), calls=%async_computation.9 | async-start | bytes 1572864 | tf_op jit(solution)/shard_map/psum | solution.py:207
  174.1 184.3 %copy-start.52 = (f32[768]{0:T(1024)}, f32[768]{0:T(1024)S(1)}, u32[]{:S(2)}) copy-start(f32[768]{0:T(1024)S(1)} %reshape.495) | copy-start | bytes 9220
  190.2 73.0 %copy-start.69 = (f32[768]{0:T(1024)}, f32[768]{0:T(1024)S(1)}, u32[]{:S(2)}) copy-start(f32[768]{0:T(1024)S(1)} %reshape.496) | copy-start | bytes 9220
  211.1 147.2 %copy-start.61 = (f32[1,2,2,128]{3,1,2,0:T(2,128)}, f32[1,2,2,128]{3,1,2,0:T(2,128)S(1)}, u32[]{:S(2)}) copy-start(f32[1,2,2,128]{3,1,2,0:T(2,128)S(1)} %copy.106) | copy-start | bytes 6148
  262.9 95.4 %copy-start.56 = (f32[512]{0:T(512)}, f32[512]{0:T(512)S(1)}, u32[]{:S(2)}) copy-start(f32[512]{0:T(512)S(1)} %broadcast_multiply_fusion.11) | copy-start | bytes 6148
  263.2 95.1 %copy-start.59 = (f32[512]{0:T(512)}, f32[512]{0:T(512)S(1)}, u32[]{:S(2)}) copy-start(f32[512]{0:T(512)S(1)} %add_rsqrt_fusion.2) | copy-start | bytes 6148
  270.3 83.2 %all-reduce.20.cloned.1.call-start = ((), (), s32[]{:S(2)}) async-start(), calls=%async_computation.10 | async-start | bytes 1572864 | tf_op jit(solution)/shard_map/psum | solution.py:241
  318.7 387.7 %reduce-scatter.19.cloned.1.call-start = ((), (), s32[]{:S(2)}) async-start(), calls=%async_computation.15 | async-start | bytes 1966080
  668.2 121.3 %reduce-scatter.15.cloned.1.call-start = ((), (), s32[]{:S(2)}) async-start(), calls=%async_computation.11 | async-start | bytes 1966080 | tf_op jit(solution)/shard_map/reduce_scatter | solution.py:286
  693.5 144.6 %all-reduce.22.cloned.1.call-start = ((), (), s32[]{:S(2)}) async-start(), calls=%async_computation.12 | async-start | bytes 3145728 | tf_op jit(solution)/shard_map/psum | solution.py:306
  795.0 112.3 %all-reduce.26.cloned.1.call-start = ((), (), s32[]{:S(2)}) async-start(), calls=%async_computation.20 | async-start | bytes 4718592 | tf_op jit(solution)/shard_map/psum | solution.py:206
  851.4 75.6 %reduce-scatter.23.cloned.1.call-start = ((), (), s32[]{:S(2)}) async-start(), calls=%async_computation.17 | async-start | bytes 589824
  856.6 72.1 %reduce-scatter.25.cloned.1.call-start = ((), (), s32[]{:S(2)}) async-start(), calls=%async_computation.18 | async-start | bytes 1769472
  863.2 78.8 %reduce-scatter.21.cloned.1.call-start = ((), (), s32[]{:S(2)}) async-start(), calls=%async_computation.16 | async-start | bytes 1474560
  922.4 44.3 %reduce-scatter.17.cloned.1.call-start = ((), (), s32[]{:S(2)}) async-start(), calls=%async_computation.13 | async-start | bytes 1769472 | tf_op jit(solution)/shard_map/reduce_scatter | solution.py:339
  925.6 118.7 %all-reduce.28.cloned.1.call-start = ((), (), s32[]{:S(2)}) async-start(), calls=%async_computation.21 | async-start | bytes 3538944 | tf_op jit(solution)/shard_map/psum | solution.py:359
  944.0 66.1 %copy-start.8 = (bf16[2,256,768]{2,1,0:T(8,128)(2,1)S(1)}, bf16[2,256,768]{2,1,0:T(8,128)(2,1)}, u32[]{:S(2)}) copy-start(bf16[2,256,768]{2,1,0:T(8,128)(2,1)} %param.20) | copy-start | bytes 2359300
  (76 other events, 824.2 us)
Sparse Core Ops, SparseCore 0:
  40.1 38.5 all-gather.9
  80.8 35.9 all-gather.15
  168.0 93.0 all-reduce.23
  270.5 34.7 all-reduce.17
  318.8 34.6 all-reduce.19
  668.3 35.3 reduce-scatter.18
  706.6 34.2 reduce-scatter.14
  795.1 42.9 all-reduce.21
  851.5 55.8 all-reduce.25
  966.8 77.4 all-reduce.27
Sparse Core Ops, SparseCore 1:
  169.9 21.5 all-gather.11
  192.8 22.8 all-gather.13
  856.7 13.1 reduce-scatter.22
  872.7 21.6 reduce-scatter.24
  922.4 19.5 reduce-scatter.20
  944.9 21.6 reduce-scatter.16
where the time goes:
time: 1070 us; the launch traced here: 1060 us
  local copies, waits for them, and re-layouts  421 us (39%)
  waiting for transfers between devices  302 us (28%)
  matrix products  115 us (11%)
  blocking collectives  103 us (10%)
  other arithmetic  94.8 us (9%)
  between operations  20.9 us (2%)
    unnamed x202, local copies, waits for them, and re-layouts  403 us
    psum x1, waiting for transfers between devices, per_device(): attn_p, attn_c = lax.psum((part_p, part_c), 'tp')  48.5 us
    psum x2, blocking collectives, per_device(): err_all, count_all, dwa_all = lax.psum((err, count, raw_dwa), ('dp', 'ctx'))  42.6 us
    psum x1, waiting for transfers between devices, per_device(): lax.psum(part1_p.astype(jnp.bfloat16), 'tp').astype(jnp.float32)  39.3 us
    psum x1, waiting for transfers between devices, per_device(): lax.psum(part2.astype(jnp.bfloat16), 'tp').astype(jnp.float32)  34.8 us
    psum x1, waiting for transfers between devices, per_device(): lax.psum(mpart_p.astype(jnp.bfloat16), 'tp').astype(jnp.float32)  33.6 us
    psum x1, waiting for transfers between devices, per_device(): lax.psum(s_qkv.astype(jnp.bfloat16), 'ctx').astype(jnp.float32)  31.5 us
    psum x1, waiting for transfers between devices, per_device(): lax.psum(mpart_c.astype(jnp.bfloat16), 'tp').astype(jnp.float32)  30.7 us
  transfers between devices with their start and end apart: 16, of which 10 were waited for; matrix products, arithmetic and copies ran while one was open for 20% of the time, Pallas kernels for 0%

commit v1 on v0

v1 whole, which is shorter than its diff:
```python
import functools
import math

import jax
import jax.numpy as jnp
from jax import lax
from jax.experimental import pallas as pl
from jax.experimental.pallas import tpu as pltpu
from jax.sharding import PartitionSpec as P

HEAD_DIM = 64
EPS = 1e-05
NEG = -1e30
MESH = pl.DeviceIdType.MESH
f32 = jnp.float32
bf16 = jnp.bfloat16
VMEM_SPEC = pl.BlockSpec(memory_space=pltpu.VMEM)
SMEM_SPEC = pl.BlockSpec(memory_space=pltpu.SMEM)
HBM_SPEC = pl.BlockSpec(memory_space=pl.ANY)
DMA = pltpu.SemaphoreType.DMA
LIMIT = 56 << 20
NT = (((1,), (1,)), ((), ()))
TN = (((0,), (0,)), ((), ()))
CH = 128
BIG = 256


def dot(a, b):
    return jnp.dot(a, b, preferred_element_type=f32)


def dot_nt(a, b):
    return lax.dot_general(a, b, NT, preferred_element_type=f32)


def dot_tn(a, b):
    return lax.dot_general(a, b, TN, preferred_element_type=f32)


def rows(start, size):
    return pl.ds(pl.multiple_of(start, size), size)


def loop(count, body):
    def step(i, carry):
        body(i)
        return carry

    lax.fori_loop(0, count, step, 0)


def kernel_call(body, outs, scratch, cid, specs, args, flops=0, name=None):
    return pl.pallas_call(
        body,
        out_shape=[jax.ShapeDtypeStruct(s, d) for s, d in outs],
        in_specs=specs,
        out_specs=[VMEM_SPEC] * len(outs),
        scratch_shapes=scratch,
        compiler_params=pltpu.CompilerParams(
            collective_id=cid, has_side_effects=True, vmem_limit_bytes=LIMIT
        ),
        cost_estimate=pl.CostEstimate(flops=flops, bytes_accessed=30 << 20, transcendentals=0),
        name=name,
    )(*args)


def greet(partners):
    barrier = pltpu.get_barrier_semaphore()
    for device in partners:
        pl.semaphore_signal(barrier, inc=1, device_id=device, device_id_type=MESH)
    pl.semaphore_wait(barrier, len(partners))


def remote(src, dst, send, recv, device):
    return pltpu.make_async_remote_copy(
        src_ref=src,
        dst_ref=dst,
        send_sem=send,
        recv_sem=recv,
        device_id=device,
        device_id_type=MESH,
    )


def axis_peers(axis, count):
    me = lax.axis_index(axis)
    return [{axis: lax.rem(me + d, count)} for d in range(1, count)]


def tp_place():
    tp = lax.axis_index("tp")
    core = lax.rem(tp, 2)
    mate = {"tp": tp + 1 - 2 * core}
    across = {"tp": lax.rem(tp + 2, 4)}
    return core, mate, across


def norm_rows(x):
    mean = jnp.mean(x, -1, keepdims=True)
    centered = x - mean
    var = jnp.mean(centered * centered, -1, keepdims=True)
    inverse = lax.rsqrt(var + EPS)
    return centered * inverse, inverse


def norm_back(gradient, whitened, inverse, gain):
    e = gradient * gain
    return inverse * (
        e - jnp.mean(e, -1, keepdims=True) - whitened * jnp.mean(e * whitened, -1, keepdims=True)
    )


def lanes_below(shape, bound):
    return lax.broadcasted_iota(jnp.int32, shape, len(shape) - 1) < bound


def turn(y, tab, sign, half):
    cos, low, high = tab[:, :128], tab[:, 128:256], tab[:, 256:384]
    turned = sign * (pltpu.roll(y, 96, 1) * low + pltpu.roll(y, 32, 1) * high)
    if not half:
        return y * cos + turned
    return jnp.where(lanes_below(y.shape, 64), y * cos + turned, y)


COLS = ((0, 256), (256, 512), (512, 640))


def project_body(
    n_dp, n_ctx, plen, clen,
    px, cx, w, g1, b1, g2, b2, valid,
    q, kv, xn, gains, tab, cnt_out, w_full,
    gb, gbs, cnt, cnts, send, recv,
):
    me = lax.axis_index("dp")
    depth = w.shape[0]
    width = px.shape[1]
    peers = axis_peers("dp", n_dp)
    for i, vector in enumerate((g1, b1, g2, b2)):
        gb[i:i + 1] = vector[...].astype(f32)
    gb[4:8] = jnp.zeros((4, depth), f32)
    cnt[...] = jnp.zeros(cnt.shape, f32) + jnp.sum(valid[...].astype(f32))
    greet(peers)
    here = rows(me * depth, depth)
    copies = []
    for d, device in enumerate(peers):
        pairs = [(gb, gbs.at[me]), (cnt, cnts.at[me])]
        pairs += [(w.at[:, a:b], w_full.at[here, a:b]) for a, b in COLS]
        copies.append(
            [remote(s, t, send.at[d, i], recv.at[d, i], device) for i, (s, t) in enumerate(pairs)]
        )
    for i in range(5):
        for group in copies:
            group[i].start()
    gbs[me] = gb[...]
    cnts[me] = cnt[...]
    w_full[here] = w[...]

    first = lax.axis_index("ctx") * plen

    def table(count, base, start):
        def body(i):
            shape = (CH, 128)
            lane = lax.broadcasted_iota(jnp.int32, shape, 1)
            row = lax.broadcasted_iota(jnp.int32, shape, 0)
            turns = lax.rem(lane, 32).astype(f32) * (-2.0 * math.log(10000.0) / HEAD_DIM)
            angle = (row + (start + i * CH)).astype(f32) * jnp.exp(turns)
            sin = jnp.sin(angle)
            left = lax.rem(lane, 64) < 32
            at = rows(base + i * CH, CH)
            tab[at, 0:128] = jnp.cos(angle)
            tab[at, 128:256] = jnp.where(left, -sin, 0.0)
            tab[at, 256:384] = jnp.where(left, 0.0, sin)

        loop(count // CH, body)

    table(plen, 0, first)
    table(clen, plen, n_ctx * plen)
    for group in copies:
        group[0].wait_recv()
        group[1].wait_recv()
    total = jnp.zeros(gains.shape, f32)
    count = jnp.zeros(cnt.shape, f32)
    for d in range(n_dp):
        row = lax.broadcasted_iota(jnp.int32, (depth, width), 0) + d * depth
        col = lax.broadcasted_iota(jnp.int32, (depth, width), 1)
        total += dot(gbs[d].astype(bf16), (row == col).astype(f32).astype(bf16))
        count += cnts[d]
    gains[...] = total
    cnt_out[...] = count
    n_prompt = px.shape[0]

    def norm_part(x, base):
        def body(i):
            whitened, _ = norm_rows(x[rows(i * CH, CH)].astype(f32))
            xn[rows(base + i * CH, CH)] = (whitened * gains[0:1] + gains[1:2]).astype(bf16)

        loop(x.shape[0] // CH, body)

    norm_part(px, 0)
    norm_part(cx, n_prompt)

    def project_part(store, lo, hi):
        def part(count, base, tab_base, period):
            def body(i):
                at = rows(base + i * BIG, BIG)
                t = tab[rows(tab_base + lax.rem(i * BIG, period), BIG)]
                store(at, t, dot(xn[at], w_full[:, lo:hi]))

            loop(count // BIG, body)

        part(n_prompt, 0, 0, plen)
        part(cx.shape[0], n_prompt, plen, clen)

    def store_q(at, t, y):
        q[at, 0:128] = (turn(y[:, 0:128], t, 1.0, False) * 0.125).astype(bf16)
        q[at, 128:256] = (turn(y[:, 128:256], t, 1.0, True) * 0.125).astype(bf16)

    def store_pair(at, t, y):
        kv[at, 0:128] = turn(y[:, 0:128], t, 1.0, False).astype(bf16)
        kv[at, 128:256] = y[:, 128:256].astype(bf16)

    def store_third(at, t, y):
        kv[at, 256:384] = turn(y, t, 1.0, True).astype(bf16)

    for i, store in enumerate((store_q, store_pair, store_third)):
        for group in copies:
            group[2 + i].wait_recv()
        project_part(store, *COLS[i])
    for group in copies:
        for copy in group:
            copy.wait_send()


def attend_body(
    n_ctx, n_dp, share, plen, clen, groups, conts,
    sel, q, kv, bias, cnt, *refs,
):
    if share:
        wo, wu, wd = refs[:3]
        refs = refs[3:]
        o, lse, msgs, wo_full, wu_full, wd_full = refs[:6]
        refs = refs[6:]
        kvs, cnts, m_s, l_s, acc_s, s_kv, r_kv, s_c, r_c, s_w, r_w = refs
    else:
        o, lse, msgs = refs[:3]
        kvs, cnts, m_s, l_s, acc_s, s_kv, r_kv, s_c, r_c = refs[3:]
    me = lax.axis_index("ctx")
    last = n_ctx - 1
    n_prompt = groups * plen
    tile = clen
    peers = axis_peers("ctx", n_ctx)
    greet(peers + (axis_peers("dp", n_dp) if share else []))

    def hop(slot, step, side):
        there = kvs.at[slot]
        return remote(there, there, s_kv.at[side, slot], r_kv.at[slot], {"ctx": me + step})

    kvs[me] = kv[0:n_prompt]

    @pl.when(me < last)
    def _():
        hop(me, 1, 0).start()

    @pl.when(me > 0)
    def _():
        hop(me, -1, 1).start()

    note = cnts.at[me]
    cnts[me] = cnt[...]
    for i in range(conts):
        cnts[me, 1 + i:2 + i] = jnp.zeros((1, 128), f32) + sel[i].astype(f32)
    counts = [remote(note, note, s_c.at[d], r_c.at[d], device) for d, device in enumerate(peers)]
    for copy in counts:
        copy.start()
    weights = []
    if share:
        mine = lax.axis_index("dp")
        depth = wu.shape[0]
        cols = pl.ds(pl.multiple_of(mine * depth, 128), depth)
        here = rows(mine * depth, depth)
        top = 2 * HEAD_DIM
        gap = top + HEAD_DIM
        for d, device in enumerate(axis_peers("dp", n_dp)):
            for i, (s, t) in enumerate((
                (wo.at[0:top], wo_full.at[0:top, cols]),
                (wo.at[top:gap], wo_full.at[gap:gap + HEAD_DIM, cols]),
                (wu, wu_full.at[here]),
                (wd, wd_full.at[:, cols]),
            )):
                weights.append(remote(s, t, s_w.at[d, i], r_w.at[d, i], device))
        for copy in weights:
            copy.start()
        wo_full[top:gap] = jnp.zeros((HEAD_DIM, wo_full.shape[1]), bf16)
        wo_full[0:top, cols] = wo[0:top]
        wo_full[gap:gap + HEAD_DIM, cols] = wo[top:gap]
        wu_full[here] = wu[...]
        wd_full[:, cols] = wd[...]

    def update(at, q_rows, k, v, mask, first):
        s = dot_nt(q_rows, k)
        if mask is not None:
            s = mask(s)
        top = jnp.max(s, -1, keepdims=True)
        if first:
            m_new = jnp.broadcast_to(top, (s.shape[0], 128))
        else:
            m_old = m_s[at]
            m_new = jnp.maximum(m_old, top)
        total = None
        parts = []
        for j in range(s.shape[1] // 128):
            p = jnp.exp(s[:, 128 * j:128 * j + 128] - m_new)
            total = p if total is None else total + p
            parts.append(p.astype(bf16))
        pv = dot(jnp.concatenate(parts, 1), v)
        m_s[at] = m_new
        if first:
            l_s[at] = total
            acc_s[at] = pv
        else:
            fade = jnp.exp(m_old - m_new)
            l_s[at] = l_s[at] * fade + total
            acc_s[at] = acc_s[at] * fade + pv

    low = lanes_below((tile, 128), 64)

    def heads(q_at, state, k_b, k_c, k_d, mask, first):
        a = q[q_at, 0:128]
        zero = jnp.zeros_like(a)
        update(state, jnp.where(low, a, zero), k_b, k_c, mask, first)
        update(state + 1, jnp.where(low, zero, a), k_b, k_c, mask, first)
        update(state + 2, q[q_at, 128:256], k_d, k_d, mask, first)

    tiles = plen // tile

    def prompt_part(slot, diagonal):
        def body(i):
            group = i // tiles
            t = lax.rem(i, tiles)
            at = rows(group * plen, plen)
            b = kvs[slot, at, 0:128]
            c = kvs[slot, at, 128:256]
            d = kvs[slot, at, 256:384]
            mask = None
            if diagonal:
                def mask(s):
                    row = lax.broadcasted_iota(jnp.int32, s.shape, 0) + t * tile
                    col = lax.broadcasted_iota(jnp.int32, s.shape, 1)
                    return jnp.where(col <= row, s, NEG)
            heads(rows(i * tile, tile), 3 * i, b, c, d, mask, diagonal)

        loop(groups * tiles, body)

    def cont_part(slot, first):
        def body(i):
            k = kvs[slot, 0:plen]
            for g in range(1, groups):
                k = jnp.where(sel[i] == g, kvs[slot, g * plen:(g + 1) * plen], k)
            heads(
                rows(n_prompt + i * tile, tile),
                3 * (groups * tiles + i),
                k[:, 0:128], k[:, 128:256], k[:, 256:384],
                None, first,
            )

        loop(conts, body)

    def self_part():
        def body(i):
            at = rows(n_prompt + i * tile, tile)

            def mask(s):
                row = lax.broadcasted_iota(jnp.int32, s.shape, 0)
                col = lax.broadcasted_iota(jnp.int32, s.shape, 1)
                return jnp.where(col <= row, s + bias[pl.ds(i, 1)], NEG)

            heads(
                at, 3 * (groups * tiles + i),
                kv[at, 0:128], kv[at, 128:256], kv[at, 256:384],
                mask, False,
            )

        loop(conts, body)

    cont_part(me, True)
    prompt_part(me, True)
    self_part()

    def ring(e):
        d = e + 1

        @pl.when(me - d >= 0)
        def _():
            hop(me - d, 1, 0).wait_recv()

            @pl.when(me < last)
            def _():
                hop(me - d, 1, 0).start()

        @pl.when(me + d <= last)
        def _():
            hop(me + d, -1, 1).wait_recv()

            @pl.when(me > 0)
            def _():
                hop(me + d, -1, 1).start()

        @pl.when(me - d >= 0)
        def _():
            prompt_part(me - d, False)
            cont_part(me - d, False)

        @pl.when(me + d <= last)
        def _():
            cont_part(me + d, False)

    loop(last, ring)

    for copy in counts:
        copy.wait()
    for d in range(n_ctx):
        msgs[8 * d:8 * d + 8] = cnts[d]

    def finish(at, state):
        l0 = jnp.sum(l_s[state], -1, keepdims=True)
        l1 = jnp.sum(l_s[state + 1], -1, keepdims=True)
        l2 = jnp.sum(l_s[state + 2], -1, keepdims=True)
        o[at, 0:128] = jnp.where(low, acc_s[state] / l0, acc_s[state + 1] / l1).astype(bf16)
        o[at, 128:256] = jnp.where(low, 0.0, acc_s[state + 2] / l2).astype(bf16)
        return (l0, l1, l2)

    def finish_prompt(i):
        finish(rows(i * tile, tile), 3 * i)

    loop(groups * tiles, finish_prompt)
    for i in range(conts):
        state = 3 * (groups * tiles + i)
        sums = finish(rows(n_prompt + i * tile, tile), state)
        lse[8 * i:8 * i + 8] = jnp.zeros((8, tile), f32)
        for h in range(3):
            value = m_s[state + h] + jnp.log(sums[h])
            lse[8 * i + h:8 * i + h + 1] = jnp.transpose(value)[0:1]

    for slot in range(n_ctx):
        @pl.when((slot <= me) & (me < last))
        def _():
            hop(slot, 1, 0).wait_send()

        @pl.when((slot >= me) & (me > 0))
        def _():
            hop(slot, -1, 1).wait_send()

    for copy in weights:
        copy.wait()


def full_at(a, core, split, c_split):
    b = a // split
    return a + core * split * (1 - b) + b * (split + core * c_split)


class TpSum:
    @staticmethod
    def scratch(half, width):
        n = half // CH
        return [
            pltpu.VMEM((half, width), bf16), pltpu.VMEM((half, width), bf16),
            pltpu.VMEM((half, width), bf16), pltpu.VMEM((half, width), bf16),
            pltpu.VMEM((half, width), f32), DMA((2, n)), DMA((2, n)),
        ]

    def __init__(self, half, start, place, scratch, compute):
        self.half, self.start, self.place, self.compute = half, start, place, compute
        self.snd1, self.rcv1, self.snd2, self.rcv2, self.own, self.send, self.recv = scratch
        self.core, self.mate, self.across = tp_place()
        self.n = half // CH

    def row(self, i):
        return lax.rem(self.start + i * CH, self.half)

    def pair(self, i):
        at = rows(self.row(i), CH)
        return remote(
            self.snd1.at[at], self.rcv1.at[at], self.send.at[0, i], self.recv.at[0, i], self.mate
        )

    def link(self, i):
        at = rows(self.row(i), CH)
        return remote(
            self.snd2.at[at], self.rcv2.at[at], self.send.at[1, i], self.recv.at[1, i], self.across
        )

    def second(self, i):
        at = rows(self.row(i), CH)
        self.pair(i).wait_recv()
        self.snd2[at] = (self.own[at] + self.rcv1[at].astype(f32)).astype(bf16)
        self.link(i).start()

    def begin(self):
        per = BIG // CH

        def block(b):
            a = self.row(b * per)
            at = rows(a, BIG)
            self.snd1[at] = self.compute(self.place(a, 1 - self.core)).astype(bf16)
            for s in range(per):
                self.pair(b * per + s).start()
            self.own[at] = self.compute(self.place(a, self.core))

            @pl.when(b > 0)
            def _():
                for s in range(per):
                    self.second((b - 1) * per + s)

        loop(self.n // per, block)
        for s in range(per):
            self.second(self.n - per + s)

    def take(self, i):
        at = rows(self.row(i), CH)
        self.link(i).wait_recv()
        return self.snd2[at].astype(f32) + self.rcv2[at].astype(f32)

    def close(self):
        def body(i):
            self.pair(i).wait_send()
            self.link(i).wait_send()

        loop(self.n, body)


class Share:
    def __init__(self, ref, place, sems):
        self.ref, self.place = ref, place
        self.send, self.recv = sems
        _, self.mate, _ = tp_place()

    def copy(self, i, a):
        at = rows(self.place(a), CH)
        return remote(self.ref.at[at], self.ref.at[at], self.send.at[i], self.recv.at[i], self.mate)


def share_scratch(half):
    return [DMA((half // CH,)), DMA((half // CH,))]


GELU = 0.7978845608028654


def gelu_tanh(u):
    return jnp.tanh(GELU * (u + 0.044715 * (u * u * u)))


def mixed_states(sc, hist, at, y):
    mixed = sc[4] * y
    for j in range(4):
        mixed += sc[j] * hist[j, at].astype(f32)
    return mixed


def middle_body(
    n_ctx, n_prompt, clen,
    sc, o, q, msgs, wo, wu, wd, cx, gains, mask, hist, teach,
    out, dm, hid, xn, du, da, do, dh1, stat, qs,
    hc, tc, slope, h1, dy, hsem, s_q, r_q, *scratch,
):
    core, mate, across = tp_place()
    ctx = lax.axis_index("ctx")
    half = clen
    n_cont = 2 * half
    mine = rows(core * half, half)
    loads = [
        pltpu.make_async_copy(hist.at[:, mine], hc, hsem.at[0]),
        pltpu.make_async_copy(teach.at[mine], tc, hsem.at[1]),
    ]
    for copy in loads:
        copy.start()
    low = lanes_below((clen, 128), 64)
    e0 = q[n_prompt:n_prompt + clen, 128:256].astype(f32)
    e1 = q[n_prompt + clen:n_prompt + n_cont, 128:256].astype(f32)
    qs[ctx, 0:n_cont] = q[n_prompt:n_prompt + n_cont, 0:128]
    qs[ctx, n_cont:n_cont + clen] = jnp.where(low, e0, pltpu.roll(e1, 64, 1)).astype(bf16)
    stat[...] = jnp.zeros(stat.shape, f32)
    others = axis_peers("ctx", n_ctx)
    greet([mate, across] + others)
    s1, s2, s3 = scratch[0:7], scratch[7:14], scratch[14:21]
    shares = scratch[21:]

    def place(a, c):
        return a + c * half

    def home(a):
        return a + core * half

    def each(body):
        loop(half // CH, body)

    def attn(at):
        return dot(o[rows(n_prompt + at, BIG)], wo[...])

    first = TpSum(half, 0, place, s1, attn)
    first.begin()
    moves = [
        remote(qs.at[ctx], qs.at[ctx], s_q.at[d], r_q.at[d], device)
        for d, device in enumerate(others)
    ]
    for copy in moves:
        copy.start()
    give_xn = Share(xn, home, shares[0:2])

    def normed(i):
        a = first.row(i)
        h = cx[rows(home(a), CH)].astype(f32) + first.take(i)
        h1[rows(a, CH)] = h
        whitened, _ = norm_rows(h)
        xn[rows(home(a), CH)] = (whitened * gains[2:3] + gains[3:4]).astype(bf16)
        give_xn.copy(i, a).start()

    each(normed)
    each(lambda i: give_xn.copy(i, first.row(i)).wait())

    def hidden(at):
        here = rows(at, BIG)
        u = dot(xn[here], wu[...])
        t = gelu_tanh(u)
        g = (0.5 * u * (1.0 + t)).astype(bf16)
        hid[here] = g
        slope[here] = 0.5 * (1.0 + t) + (0.5 * GELU) * u * (1.0 - t * t) * (
            1.0 + (3.0 * 0.044715) * (u * u)
        )
        return dot(g, wd[...])

    second = TpSum(half, 0, place, s2, hidden)
    second.begin()
    for copy in loads:
        copy.wait()
    give_dm = Share(dm, home, shares[2:4])
    give_out = Share(out, home, shares[4:6])
    count = msgs[0:1]
    for j in range(1, n_ctx):
        count += msgs[8 * j:8 * j + 1]
    coef = (2.0 * sc[4]) / (jnp.maximum(count, 1.0) * (1.0 * cx.shape[1]))

    def add(row, value):
        stat[row:row + 1] += jnp.sum(value, 0, keepdims=True)

    def lossy(i):
        a = second.row(i)
        here, there = rows(a, CH), rows(home(a), CH)
        y = h1[here] + second.take(i)
        mixed = mixed_states(sc, hc, here, y)
        diff = mixed - tc[here].astype(f32)
        weighted = diff * mask[there][:, 0:1]
        grad = weighted * coef[:, 0:1]
        dy[here] = grad
        dm[there] = grad.astype(bf16)
        give_dm.copy(i, a).start()
        out[there] = mixed.astype(bf16)
        give_out.copy(i, a).start()
        add(4, weighted * diff)
        for j in range(4):
            add(5 + j, weighted * hc[j, here].astype(f32))
        add(9, weighted * y)

    each(lossy)
    each(lambda i: give_dm.copy(i, second.row(i)).wait())

    def back(at):
        here = rows(at, BIG)
        d = (dot_nt(dm[here], wd[...]) * slope[here]).astype(bf16)
        du[here] = d
        return dot_nt(d, wu[...])

    third = TpSum(half, 0, place, s3, back)
    third.begin()
    give_da = Share(da, home, shares[6:8])

    def grads(i):
        a = third.row(i)
        here = rows(a, CH)
        total = third.take(i)
        whitened, inverse = norm_rows(h1[here])
        grad = dy[here] + norm_back(total, whitened, inverse, gains[2:3])
        dh1[here] = grad
        da[rows(home(a), CH)] = grad.astype(bf16)
        give_da.copy(i, a).start()
        add(2, total * whitened)
        add(3, total)

    each(grads)
    each(lambda i: give_da.copy(i, third.row(i)).wait())

    def last(i):
        at = rows(i * BIG, BIG)
        do[at] = dot_nt(da[at], wo[...]).astype(bf16)

    loop(n_cont // BIG, last)
    each(lambda i: give_out.copy(i, second.row(i)).wait())
    for part in (first, second, third):
        part.close()
    for copy in moves:
        copy.wait()


def weight_grads(hid, dm, xn, du, o, da, cols, store):
    ff = hid.shape[1]
    size = cols.size
    for j in range(ff // 256):
        store(j * 256, dot_tn(hid[:, 256 * j:256 * j + 256], dm[:, cols]))
    for j in range(ff // size):
        store(ff + j * size, dot_tn(xn[:, cols], du[:, size * j:size * j + size]))
    g = dot_tn(o[...], da[:, cols])
    store(ff + ff, g[0:128])
    store(ff + ff + 128, g[192:256])


def attend_back_body(
    n_ctx, n_dp, share, plen, clen, groups, conts, depth,
    sc, msgs, qs, do, o, lse, kv, valid, tab, gains, hid_h, dm_h, xn2_h, du_h, da_h,
    wo_h, wu_h, wd_h, px_h, hist_h, *refs,
):
    if share:
        dcat, out, gsh = refs[:3]
        refs = refs[3:]
    else:
        dcat, out, g_down, g_up, g_out = refs[:5]
        refs = refs[5:]
    (
        hid, dm, xn2, du, da, wo, wu, wd, px, hist, lsem,
        dos, sts, dqs, kd, acc_k, acc_v, acc_kd, acc_vd, dq_f, send, recv,
        xp, h1,
    ) = refs[:24]
    s1, s2 = refs[24:31], refs[31:38]
    shares = refs[38:42]
    core, mate, across = tp_place()
    me = lax.axis_index("ctx")
    dp = lax.axis_index("dp")
    peers = axis_peers("ctx", n_ctx)
    dp_peers = axis_peers("dp", n_dp) if share else []
    n_prompt = groups * plen
    n_cont = conts * clen
    half = plen
    own_rows = rows(core * half, half)
    pairs = [
        (wo_h, wo), (px_h.at[own_rows], px), (hid_h, hid), (dm_h, dm), (xn2_h, xn2), (du_h, du),
        (da_h, da), (wu_h, wu), (wd_h, wd), (hist_h.at[:, own_rows], hist),
    ]
    loads = [
        pltpu.make_async_copy(s, t, lsem.at[i]) for i, (s, t) in enumerate(pairs)
    ]
    for copy in loads:
        copy.start()
    low = lanes_below((clen, 128), 64)
    zero = jnp.zeros((clen, 128), bf16)

    g0 = do[0:clen, 128:256].astype(f32)
    g1 = do[clen:2 * clen, 128:256].astype(f32)
    dos[me, 0:n_cont] = do[:, 0:128]
    dos[me, n_cont:n_cont + clen] = jnp.where(low, pltpu.roll(g0, 64, 1), g1).astype(bf16)
    for c in range(conts):
        at = slice(c * clen, (c + 1) * clen)
        full = slice(n_prompt + c * clen, n_prompt + (c + 1) * clen)
        pa = do[at, 0:128].astype(f32) * o[full, 0:128].astype(f32)
        pe = do[at, 128:256].astype(f32) * o[full, 128:256].astype(f32)
        ta = jnp.transpose(pa)
        te = jnp.transpose(pe)
        st = 16 * c
        sts[me, st:st + 8] = lse[8 * c:8 * c + 8]
        sts[me, st + 8:st + 9] = jnp.sum(ta[0:64], 0, keepdims=True)
        sts[me, st + 9:st + 10] = jnp.sum(ta[64:128], 0, keepdims=True)
        sts[me, st + 10:st + 11] = jnp.sum(te[64:128], 0, keepdims=True)
        sts[me, st + 11:st + 16] = jnp.zeros((5, clen), f32)
    greet(peers + [mate, across] + dp_peers)
    sends = []
    for d, device in enumerate(peers):
        for i, ref in enumerate((sts, dos)):
            sends.append(remote(ref.at[me], ref.at[me], send.at[d, i], recv.at[d, i], device))
    for copy in sends:
        copy.start()

    def place(a, c):
        return a + c * half

    def home(a):
        return a + core * half

    loads[0].wait()
    loads[1].wait()

    def attn(at):
        return dot(o[rows(at, BIG)], wo[...])

    first = TpSum(half, 0, place, s1, attn)
    first.begin()

    for copy in loads[2:7]:
        copy.wait()
    gives = []
    if share:
        gsnd, grcv, gown, s_g, r_g = refs[42:47]
        for d in range(n_dp - 1):
            other = lax.rem(dp + d + 1, n_dp)

            def keep(at, value, d=d):
                gsnd[d, at:at + value.shape[0]] = value.astype(bf16)

            cols = pl.ds(pl.multiple_of(other * depth, 128), depth)
            weight_grads(hid, dm, xn2, du, o.at[n_prompt:n_prompt + n_cont], da, cols, keep)
            copy = remote(
                gsnd.at[d], grcv.at[d], s_g.at[d], r_g.at[d], {"dp": other}
            )
            copy.start()
            gives.append(copy)
    else:
        width = dm.shape[1]
        for j in range(width // 256):
            cols = pl.ds(256 * j, 256)

            def keep(at, value, j=j):
                ff = hid.shape[1]
                span = slice(256 * j, 256 * j + 256)
                if at < ff:
                    g_down[at:at + 256, span] = value.astype(bf16)
                elif at < 2 * ff:
                    g_up[span, at - ff:at - ff + 256] = value.astype(bf16)
                else:
                    g_out[at - 2 * ff:at - 2 * ff + value.shape[0], span] = value.astype(bf16)

            weight_grads(hid, dm, xn2, du, o.at[n_prompt:n_prompt + n_cont], da, cols, keep)

    kd[...] = pltpu.roll(kv[0:n_prompt, 256:384].astype(f32), 64, 1).astype(bf16)
    for acc in (acc_k, acc_v, acc_kd, acc_vd):
        acc[...] = jnp.zeros(acc.shape, f32)

    def one_head(q_rows, do_rows, k, v, lse_row, delta_row, mask):
        s = dot_nt(k, q_rows)
        p = jnp.exp(s - lse_row)
        if mask is not None:
            p = mask(p)
        dp_ = dot_nt(v, do_rows)
        ds = (p * (dp_ - delta_row)).astype(bf16)
        return p.astype(bf16), ds

    def halves(a):
        return jnp.where(low, a, zero), jnp.where(low, zero, a)

    def continuation(src, c, k_b, k_c, k_d, k_s, mask):
        base = c * clen
        a0, a1 = halves(qs[src, base:base + clen])
        d0, d1 = halves(dos[src, base:base + clen])
        e = halves(qs[src, n_cont:n_cont + clen])[c]
        g = halves(dos[src, n_cont:n_cont + clen])[c]
        st = 16 * c
        row = lambda i: sts[src, st + i:st + i + 1]
        p0, s0 = one_head(a0, d0, k_b, k_c, row(0), row(8), mask)
        dv = dot(p0, d0)
        dk = dot(s0, a0)
        dq0 = dot_tn(s0, k_b)
        p1, s1_ = one_head(a1, d1, k_b, k_c, row(1), row(9), mask)
        dv += dot(p1, d1)
        dk += dot(s1_, a1)
        dq1 = dot_tn(s1_, k_b)
        keys, values = (k_d, k_s) if c == 0 else (k_s, k_d)
        p2, s2_ = one_head(e, g, keys, values, row(2), row(10), mask)
        dvd = dot(p2, g)
        dkd = dot(s2_, e)
        dq2 = dot_tn(s2_, keys)
        return dk, dv, dkd, dvd, jnp.where(low, dq0, dq1), dq2

    def source(src, own):
        pair = []
        for c in range(conts):
            pick = msgs[pl.ds(src * 8 + 1 + c, 1)]

            def choose(one, two):
                return jnp.where(pick == 0.0, one.astype(f32), two.astype(f32)).astype(bf16)

            k_b = choose(kv[0:plen, 0:128], kv[plen:2 * plen, 0:128])
            k_c = choose(kv[0:plen, 128:256], kv[plen:2 * plen, 128:256])
            k_d = choose(kv[0:plen, 256:384], kv[plen:2 * plen, 256:384])
            k_s = choose(kd[0:plen], kd[plen:2 * plen])
            dk, dv, dkd, dvd, dqa, dqd = continuation(src, c, k_b, k_c, k_d, k_s, None)
            for g in range(groups):
                keep = (pick == 1.0 * g).astype(f32)
                at = slice(g * plen, (g + 1) * plen)
                acc_k[at] += keep * dk
                acc_v[at] += keep * dv
                acc_kd[at] += keep * dkd
                acc_vd[at] += keep * dvd
            pair.append(dqd)
            if own:
                dq_f[c * clen:(c + 1) * clen] = dqa
            else:
                dqs[n_ctx + src, c * clen:(c + 1) * clen] = dqa.astype(bf16)
        third = jnp.where(low, pair[0], pair[1])
        if own:
            dq_f[n_cont:n_cont + clen] = third
        else:
            dqs[n_ctx + src, n_cont:n_cont + clen] = third.astype(bf16)

    def other_of(d):
        return lax.rem(me + 2 * n_ctx - (d + 1), n_ctx)

    def back_copy(d):
        other = other_of(d)
        return remote(
            dqs.at[n_ctx + other], dqs.at[me], send.at[d, 2], recv.at[d, 2], {"ctx": other}
        )

    def visit(d):
        other = other_of(d)
        for i, ref in enumerate((sts, dos)):
            remote(ref.at[other], ref.at[other], send.at[d, i], recv.at[d, i], {"ctx": other}).wait_recv()
        source(other, False)
        back_copy(d).start()

    source(me, True)
    loop(n_ctx - 1, visit)

    give_xn = Share(xp, home, shares[0:2])

    def normed(i):
        a = first.row(i)
        h = px[rows(a, CH)].astype(f32) + first.take(i)
        h1[rows(a, CH)] = h
        whitened, _ = norm_rows(h)
        xp[rows(home(a), CH)] = (whitened * gains[2:3] + gains[3:4]).astype(bf16)
        give_xn.copy(i, a).start()

    loop(half // CH, normed)
    loop(half // CH, lambda i: give_xn.copy(i, first.row(i)).wait())
    for copy in loads[7:9]:
        copy.wait()

    def hidden(at):
        u = dot(xp[rows(at, BIG)], wu[...])
        return dot((0.5 * u * (1.0 + gelu_tanh(u))).astype(bf16), wd[...])

    second = TpSum(half, 0, place, s2, hidden)
    second.begin()

    for c in range(conts):
        at = slice(n_prompt + c * clen, n_prompt + (c + 1) * clen)
        k_d = kv[at, 256:384]
        k_s = pltpu.roll(k_d.astype(f32), 64, 1).astype(bf16)

        def mask(p):
            key = lax.broadcasted_iota(jnp.int32, p.shape, 0)
            query = lax.broadcasted_iota(jnp.int32, p.shape, 1)
            return jnp.where(
                key <= query, p * valid[c * clen:(c + 1) * clen, 0:1], 0.0
            )

        dk, dv, dkd, dvd, dqa, dqd = continuation(
            me, c, kv[at, 0:128], kv[at, 128:256], k_d, k_s, mask
        )
        dq_f[c * clen:(c + 1) * clen] += dqa
        keep = low if c == 0 else jnp.logical_not(low)
        dq_f[n_cont:n_cont + clen] += jnp.where(keep, dqd, 0.0)
        t = tab[plen:plen + clen]
        dcat[at, 256:384] = turn(dk, t, -1.0, False).astype(bf16)
        dcat[at, 384:512] = dv.astype(bf16)
        if c == 0:
            joined = jnp.where(low, dkd, pltpu.roll(dvd, 64, 1))
        else:
            joined = jnp.where(low, pltpu.roll(dkd, 64, 1), dvd)
        dcat[at, 512:640] = turn(joined, t, -1.0, True).astype(bf16)

    zq = jnp.zeros((plen, 256), bf16)
    wide = lanes_below((plen, 128), 64)
    for g in range(groups):
        at = slice(g * plen, (g + 1) * plen)
        t = tab[0:plen]
        dcat[at, 0:256] = zq
        dcat[at, 256:384] = turn(acc_k[at], t, -1.0, False).astype(bf16)
        dcat[at, 384:512] = acc_v[at].astype(bf16)
        k2 = acc_kd[at] + pltpu.roll(acc_kd[at], 64, 1)
        v2 = acc_vd[at] + pltpu.roll(acc_vd[at], 64, 1)
        dcat[at, 512:640] = turn(jnp.where(wide, k2, v2), t, -1.0, True).astype(bf16)

    if share:
        def stay(at, value):
            gown[at:at + value.shape[0]] = value

        cols = pl.ds(pl.multiple_of(dp * depth, 128), depth)
        weight_grads(hid, dm, xn2, du, o.at[n_prompt:n_prompt + n_cont], da, cols, stay)
        for copy in gives:
            copy.wait()

        def settle(i):
            at = rows(i * 64, 64)
            total = gown[at]
            for d in range(n_dp - 1):
                total += grcv[d, at].astype(f32)
            gsh[at] = total.astype(bf16)

        loop(gsh.shape[0] // 64, settle)

    for d in range(n_ctx - 1):
        back_copy(d).wait_send()
        other = lax.rem(me + d + 1, n_ctx)
        remote(
            dqs.at[n_ctx + other], dqs.at[other], send.at[d, 2], recv.at[d, 2], {"ctx": other}
        ).wait_recv()
        dq_f[...] += dqs[other].astype(f32)
    for c in range(conts):
        at = slice(n_prompt + c * clen, n_prompt + (c + 1) * clen)
        t = tab[plen:plen + clen]
        pair = dq_f[c * clen:(c + 1) * clen] * 0.125
        dcat[at, 0:128] = turn(pair, t, -1.0, False).astype(bf16)
        third = dq_f[n_cont:n_cont + clen] * 0.125
        if c == 1:
            third = pltpu.roll(third, 64, 1)
        third = jnp.where(low, third, 0.0)
        dcat[at, 128:256] = turn(third, t, -1.0, True).astype(bf16)

    loads[9].wait()
    give_out = Share(out, home, shares[2:4])

    def mixed(i):
        a = second.row(i)
        here = rows(a, CH)
        y = h1[here] + second.take(i)
        out[rows(home(a), CH)] = mixed_states(sc, hist, here, y).astype(bf16)
        give_out.copy(i, a).start()

    loop(half // CH, mixed)
    loop(half // CH, lambda i: give_out.copy(i, second.row(i)).wait())
    first.close()
    second.close()
    for copy in sends:
        copy.wait_send()


class LineSum:
    @staticmethod
    def scratch(count, size, width):
        return [
            pltpu.VMEM((count, size, width), bf16), pltpu.VMEM((count, size, width), bf16),
            pltpu.VMEM((count, size, width), bf16), DMA((2, count)), DMA((2, count)),
        ]

    def __init__(self, me, src, dst, scratch, count, size):
        self.src, self.dst, self.count, self.size = src, dst, count, size
        self.got, self.pair, self.far, self.send, self.recv = scratch
        side = me // 2
        self.outer = (me == 0) | (me == 3)
        self.inner = (me == 1) | (me == 2)
        self.near = {"ctx": 1 + side}
        self.back = {"ctx": 3 * side}
        self.twin = {"ctx": 2 - side}

    def at(self, k):
        return rows(k * self.size, self.size)

    def up(self, k):
        return remote(
            self.src.at[self.at(k)], self.got.at[k], self.send.at[0, k], self.recv.at[0, k], self.near
        )

    def cross(self, k):
        return remote(
            self.pair.at[k], self.far.at[k], self.send.at[1, k], self.recv.at[1, k], self.twin
        )

    def down(self, k):
        return remote(
            self.pair.at[k], self.got.at[k], self.send.at[0, k], self.recv.at[0, k], self.back
        )

    def launch(self, k):
        @pl.when(self.outer)
        def _():
            self.up(k).start()

    def meet(self, k):
        @pl.when(self.inner)
        def _():
            self.up(k).wait_recv()
            self.pair[k] = (
                self.src[self.at(k)].astype(f32) + self.got[k].astype(f32)
            ).astype(bf16)
            self.cross(k).start()

    def turn(self, k):
        @pl.when(self.inner)
        def _():
            self.cross(k).wait()
            total = (self.pair[k].astype(f32) + self.far[k].astype(f32)).astype(bf16)
            self.pair[k] = total
            self.down(k).start()
            self.dst[self.at(k)] = total.astype(f32)

    def land(self, k):
        @pl.when(self.outer)
        def _():
            self.up(k).wait_send()
            self.down(k).wait_recv()
            self.dst[self.at(k)] = self.got[k].astype(f32)

        @pl.when(self.inner)
        def _():
            self.down(k).wait_send()


def input_grad_body(
    n_dp, n_ctx, share, split, c_split, depth,
    dcat, w, px, cx, gains, dh1, stat_in, xn_h, *refs,
):
    if share:
        gsh, grad_p, grad_c, fin, r_rest, r_qkv = refs[:6]
        refs = refs[6:]
    else:
        grad_p, grad_c, fin, g_qkv = refs[:4]
        refs = refs[4:]
    xn, lsem, grad, stat, stats_m, stats_c, stats_d, s_s, r_s = refs[:9]
    s1 = refs[9:16]
    shares = refs[16:18]
    refs = refs[18:]
    core, mate, across = tp_place()
    me = lax.axis_index("ctx")
    dp = lax.axis_index("dp")
    ctx_peers = axis_peers("ctx", n_ctx)
    dp_peers = axis_peers("dp", n_dp)
    half = split + c_split
    n_prompt = 2 * split
    load = pltpu.make_async_copy(xn_h, xn, lsem.at[0])
    load.start()
    stat[...] = stat_in[...]
    greet([mate, across] + ctx_peers + dp_peers)
    if share:
        gsnd, gown, grcv, s_g, r_g, qsh = refs[:6]
        rest = LineSum(me, gsh, r_rest, refs[6:11], REST, gsh.shape[0] // REST)
        tail = LineSum(me, qsh, r_qkv, refs[11:16], TAIL, depth // TAIL)
        loop(REST, rest.launch)

    def place(a, c):
        return full_at(a, c, split, c_split)

    def home(a):
        return full_at(a, core, split, c_split)

    def compute(at):
        return dot_nt(dcat[rows(at, BIG)], w[...])

    total = TpSum(half, split, place, s1, compute)
    total.begin()
    load.wait()
    gives = []
    if share:
        for d in range(n_dp - 1):
            other = lax.rem(dp + d + 1, n_dp)
            cols = pl.ds(pl.multiple_of(other * depth, 128), depth)
            for j in range(depth // 128):
                part = pl.ds(pl.multiple_of(other * depth + 128 * j, 128), 128)
                gsnd[d, 128 * j:128 * j + 128] = dot_tn(xn[:, part], dcat[...]).astype(bf16)
            del cols
            copy = remote(gsnd.at[d], grcv.at[d], s_g.at[d], r_g.at[d], {"dp": other})
            copy.start()
            gives.append(copy)
        for j in range(depth // 128):
            part = pl.ds(pl.multiple_of(dp * depth + 128 * j, 128), 128)
            gown[128 * j:128 * j + 128] = dot_tn(xn[:, part], dcat[...])
    else:
        for j in range(xn.shape[1] // 128):
            part = slice(128 * j, 128 * j + 128)
            g_qkv[part] = dot_tn(xn[:, part], dcat[...]).astype(bf16)
    give = Share(grad, home, shares)

    def finish(i):
        a = total.row(i)
        b = a // split
        value = total.take(i)
        p = px[rows((core * split + a) * (1 - b), CH)].astype(f32)
        c = cx[rows((core * c_split + a - split) * b, CH)].astype(f32)
        whitened, inverse = norm_rows(jnp.where(b == 0, p, c))
        back = norm_back(value, whitened, inverse, gains[0:1])
        extra = dh1[rows((a - split) * b, CH)]
        grad[rows(home(a), CH)] = jnp.where(b == 0, back, back + extra).astype(bf16)
        give.copy(i, a).start()
        stat[0:1] += jnp.sum(value * whitened, 0, keepdims=True)
        stat[1:2] += jnp.sum(value, 0, keepdims=True)
        if share:
            rest.meet(i)

            @pl.when(i > 0)
            def _():
                rest.turn(i - 1)

    loop(total.n, finish)

    def small(src, dst, s, r, device):
        return remote(src, dst, s_s.at[s], r_s.at[r], device)

    stats_m[0] = stat[...]
    to_mate = small(stats_m.at[0], stats_m.at[1], 0, 0, mate)
    to_mate.start()
    if share:
        rest.turn(REST - 1)
        for copy in gives:
            copy.wait()

        def settle(i):
            at = rows(i * 64, 64)
            value = gown[at]
            for d in range(n_dp - 1):
                value += grcv[d, at].astype(f32)
            qsh[at] = value.astype(bf16)

        loop(depth // 64, settle)
        loop(TAIL, tail.launch)
    to_mate.wait()
    stats_c[me] = stats_m[0] + stats_m[1]
    to_ctx = [
        small(stats_c.at[me], stats_c.at[me], 1 + d, 1 + d, device)
        for d, device in enumerate(ctx_peers)
    ]
    for copy in to_ctx:
        copy.start()
    if share:
        loop(TAIL, tail.meet)
    for copy in to_ctx:
        copy.wait()
    value = stats_c[0]
    for d in range(1, n_ctx):
        value += stats_c[d]
    stats_d[dp] = value
    to_dp = [
        small(stats_d.at[dp], stats_d.at[dp], n_ctx + d, n_ctx + d, device)
        for d, device in enumerate(dp_peers)
    ]
    for copy in to_dp:
        copy.start()
    if share:
        loop(TAIL, tail.turn)
        loop(REST, rest.land)
    loop(total.n, lambda i: give.copy(i, total.row(i)).wait())
    grad_p[...] = grad[0:n_prompt]
    grad_c[...] = grad[n_prompt:n_prompt + 2 * c_split]
    for copy in to_dp:
        copy.wait()
    value = stats_d[0]
    for d in range(1, n_dp):
        value += stats_d[d]
    fin[...] = value
    total.close()
    if share:
        loop(TAIL, tail.land)


REST = 6
TAIL = 4


def per_device(
    n_dp, n_ctx,
    prompt_x, cont_x, prompt_hist, cont_hist, teacher, valid_mask, cont_group, layer_ids,
    dwa_weights, qkv_weight, out_weight, up_weight, down_weight,
    ln1_gain, ln1_bias, ln2_gain, ln2_bias,
):
    groups, plen, width = prompt_x.shape
    conts, clen, _ = cont_x.shape
    depth = qkv_weight.shape[0]
    n_prompt, n_cont = groups * plen, conts * clen
    n_rows = n_prompt + n_cont
    split, c_split = n_prompt // 2, n_cont // 2
    half = split + c_split
    ff = up_weight.shape[1]
    share = depth % 128 == 0

    w_q, w_k, w_v = qkv_weight[:, 0], qkv_weight[:, 1], qkv_weight[:, 2]
    w_loc = jnp.concatenate(
        [
            w_q, jnp.zeros((depth, 64), bf16), w_k[:, :128], w_v[:, :128],
            w_k[:, 128:], w_v[:, 128:],
        ],
        1,
    )
    px = prompt_x.reshape(n_prompt, width)
    cx = cont_x.reshape(n_cont, width)
    vectors = [v.reshape(1, depth) for v in (ln1_gain, ln1_bias, ln2_gain, ln2_bias)]
    tab_rows = plen + clen
    q, kv, xn1, gains, tab, cnt_dp, w_full = kernel_call(
        functools.partial(project_body, n_dp, n_ctx, plen, clen),
        [
            ((n_rows, 256), bf16), ((n_rows, 384), bf16), ((n_rows, width), bf16),
            ((8, width), f32), ((tab_rows, 384), f32), ((8, 128), f32), ((width, 640), bf16),
        ],
        [
            pltpu.VMEM((8, depth), f32), pltpu.VMEM((n_dp, 8, depth), f32),
            pltpu.VMEM((8, 128), f32), pltpu.VMEM((n_dp, 8, 128), f32),
            DMA((n_dp - 1, 5)), DMA((n_dp - 1, 5)),
        ],
        0, [VMEM_SPEC] * 8, (px, cx, w_loc, *vectors, valid_mask), name="project",
    )

    maskf = valid_mask.astype(f32)
    bias = jnp.where(valid_mask == 1, 0.0, NEG).astype(f32)
    bias = jnp.concatenate([bias, jnp.zeros((8 - conts, clen), f32)], 0)
    mask_rows = jnp.broadcast_to(maskf.reshape(n_cont, 1), (n_cont, 128))
    slot_pick = (layer_ids[:, None] == jnp.arange(4, dtype=jnp.int32)[None, :]).astype(f32)
    slot_w = jnp.sum(slot_pick * dwa_weights[None, :4], 1)
    sc = jnp.concatenate([slot_w, dwa_weights[4:5]])
    states = 3 * (n_prompt // clen + conts)
    outs = [((n_rows, 256), bf16), ((8 * conts, clen), f32), ((8 * n_ctx, 128), f32)]
    args = (cont_group, q, kv, bias, cnt_dp)
    specs = [SMEM_SPEC] + [VMEM_SPEC] * 4
    scratch = [
        pltpu.VMEM((n_ctx, n_prompt, 384), bf16), pltpu.VMEM((n_ctx, 8, 128), f32),
        pltpu.VMEM((states, clen, 128), f32), pltpu.VMEM((states, clen, 128), f32),
        pltpu.VMEM((states, clen, 128), f32),
        DMA((2, n_ctx)), DMA((n_ctx,)), DMA((n_ctx - 1,)), DMA((n_ctx - 1,)),
    ]
    if share:
        args += (out_weight, up_weight, down_weight)
        specs += [VMEM_SPEC] * 3
        outs += [((256, width), bf16), ((width, ff), bf16), ((ff, width), bf16)]
        scratch += [DMA((n_dp - 1, 4)), DMA((n_dp - 1, 4))]
    got = kernel_call(
        functools.partial(attend_body, n_ctx, n_dp, share, plen, clen, groups, conts),
        outs, scratch, 1, specs, args, name="attend",
    )
    o, lse, msgs = got[:3]
    if share:
        wo, wu, wd = got[3:]
    else:
        out_w = lax.all_gather(out_weight, "dp", axis=1, tiled=True)
        wu = lax.all_gather(up_weight, "dp", axis=0, tiled=True)
        wd = lax.all_gather(down_weight, "dp", axis=1, tiled=True)
        wo = jnp.concatenate([out_w[:128], jnp.zeros((64, width), bf16), out_w[128:]], 0)

    packed = n_cont + clen
    cont_out, dm, hid, xn2, du, da, do, dh1, stat, qs = kernel_call(
        functools.partial(middle_body, n_ctx, n_prompt, clen),
        [
            ((n_cont, width), bf16), ((n_cont, width), bf16), ((n_cont, ff), bf16),
            ((n_cont, width), bf16), ((n_cont, ff), bf16), ((n_cont, width), bf16),
            ((n_cont, 256), bf16), ((c_split, width), f32), ((16, width), f32),
            ((n_ctx, packed, 128), bf16),
        ],
        [
            pltpu.VMEM((4, c_split, width), bf16), pltpu.VMEM((c_split, width), bf16),
            pltpu.VMEM((n_cont, ff), f32), pltpu.VMEM((c_split, width), f32),
            pltpu.VMEM((c_split, width), f32), DMA((2,)), DMA((n_ctx - 1,)), DMA((n_ctx - 1,)),
        ]
        + TpSum.scratch(c_split, width) * 3
        + share_scratch(c_split) * 4,
        2,
        [SMEM_SPEC] + [VMEM_SPEC] * 9 + [HBM_SPEC] * 2,
        (
            sc, o, q, msgs, wo, wu, wd, cx, gains, mask_rows,
            cont_hist.reshape(4, n_cont, width), teacher.reshape(n_cont, width),
        ),
        name="middle",
    )

    grad_rows = 2 * ff + 3 * HEAD_DIM
    outs = [((n_rows, 640), bf16), ((n_prompt, width), bf16)]
    extra = []
    if share:
        outs += [((grad_rows, depth), bf16)]
        extra = [
            pltpu.VMEM((n_dp - 1, grad_rows, depth), bf16),
            pltpu.VMEM((n_dp - 1, grad_rows, depth), bf16),
            pltpu.VMEM((grad_rows, depth), f32), DMA((n_dp - 1,)), DMA((n_dp - 1,)),
        ]
    else:
        outs += [((ff, width), bf16), ((width, ff), bf16), ((3 * HEAD_DIM, width), bf16)]
    acc = pltpu.VMEM((n_prompt, 128), f32)
    got = kernel_call(
        functools.partial(
            attend_back_body, n_ctx, n_dp, share, plen, clen, groups, conts, depth
        ),
        outs,
        [
            pltpu.VMEM((n_cont, ff), bf16), pltpu.VMEM((n_cont, width), bf16),
            pltpu.VMEM((n_cont, width), bf16), pltpu.VMEM((n_cont, ff), bf16),
            pltpu.VMEM((n_cont, width), bf16), pltpu.VMEM((256, width), bf16),
            pltpu.VMEM((width, ff), bf16), pltpu.VMEM((ff, width), bf16),
            pltpu.VMEM((split, width), bf16), pltpu.VMEM((4, split, width), bf16), DMA((10,)),
            pltpu.VMEM((n_ctx, packed, 128), bf16), pltpu.VMEM((n_ctx, 16 * conts, clen), f32),
            pltpu.VMEM((2 * n_ctx, packed, 128), bf16), pltpu.VMEM((n_prompt, 128), bf16),
            acc, acc, acc, acc, pltpu.VMEM((packed, 128), f32),
            DMA((n_ctx - 1, 3)), DMA((n_ctx - 1, 3)),
            pltpu.VMEM((n_prompt, width), bf16), pltpu.VMEM((split, width), f32),
        ]
        + TpSum.scratch(split, width) * 2
        + share_scratch(split) * 2
        + extra,
        3,
        [SMEM_SPEC] + [VMEM_SPEC] * 9 + [HBM_SPEC] * 10,
        (
            sc, msgs, qs, do, o, lse, kv, mask_rows, tab, gains, hid, dm, xn2, du, da,
            wo, wu, wd, px, prompt_hist.reshape(4, n_prompt, width),
        ),
        name="attend_back",
    )
    dcat, prompt_out = got[:2]

    stat_rows = pltpu.VMEM((16, width), f32)
    outs = [((n_prompt, width), bf16), ((n_cont, width), bf16), ((16, width), f32)]
    args = (dcat, w_full, px, cx, gains, dh1, stat, xn1)
    specs = [VMEM_SPEC] * 7 + [HBM_SPEC]
    extra = []
    if share:
        args += (got[2],)
        specs += [VMEM_SPEC]
        outs += [((grad_rows, depth), f32), ((depth, 640), f32)]
        extra = [
            pltpu.VMEM((n_dp - 1, depth, 640), bf16), pltpu.VMEM((depth, 640), f32),
            pltpu.VMEM((n_dp - 1, depth, 640), bf16), DMA((n_dp - 1,)), DMA((n_dp - 1,)),
            pltpu.VMEM((depth, 640), bf16),
        ]
        extra += LineSum.scratch(REST, grad_rows // REST, depth)
        extra += LineSum.scratch(TAIL, depth // TAIL, 640)
    else:
        outs += [((width, 640), bf16)]
    last = kernel_call(
        functools.partial(input_grad_body, n_dp, n_ctx, share, split, c_split, depth),
        outs,
        [
            pltpu.VMEM((n_rows, width), bf16), DMA((1,)), pltpu.VMEM((n_rows, width), bf16),
            stat_rows, pltpu.VMEM((2, 16, width), f32), pltpu.VMEM((n_ctx, 16, width), f32),
            pltpu.VMEM((n_dp, 16, width), f32), DMA((n_ctx + n_dp,)), DMA((n_ctx + n_dp,)),
        ]
        + TpSum.scratch(half, width)
        + share_scratch(half)
        + extra,
        4, specs, args, name="input_grad",
    )
    grad_p, grad_c, fin = last[:3]

    def three(g):
        return jnp.stack(
            [
                g[:, 0:192],
                jnp.concatenate([g[:, 256:384], g[:, 512:576]], 1),
                jnp.concatenate([g[:, 384:512], g[:, 576:640]], 1),
            ],
            1,
        )

    if share:
        rest, qkv = last[3:]
        r_down = rest[:ff]
        r_up = jnp.concatenate(
            [rest[ff + j * depth:ff + (j + 1) * depth] for j in range(ff // depth)], 1
        )
        r_out = rest[2 * ff:]
        r_qkv = three(qkv)
    else:
        def scattered(g, dim):
            part = lax.psum_scatter(g, "dp", scatter_dimension=dim, tiled=True)
            return lax.psum(part, "ctx").astype(f32)

        g_down, g_up, g_out = got[2:]
        r_down = scattered(g_down, 1)
        r_up = scattered(g_up, 0)
        r_out = scattered(g_out, 1)
        r_qkv = scattered(three(last[3]), 0)
    norms = lax.dynamic_slice_in_dim(fin[:4], lax.axis_index("dp") * depth, depth, 1)
    sums = jnp.sum(fin[4:10], 1)
    count = msgs[0, 0]
    for j in range(1, n_ctx):
        count = count + msgs[8 * j, 0]
    denom = jnp.maximum(count, 1.0) * width
    raw = jnp.concatenate([jnp.sum(slot_pick * sums[1:5, None], 0), sums[5:6]])
    return (
        prompt_out.reshape(groups, plen, width),
        cont_out.reshape(conts, clen, width),
        sums[0] / denom,
        grad_p.reshape(groups, plen, width),
        grad_c.reshape(conts, clen, width),
        r_qkv, r_out, r_up, r_down,
        norms[0], norms[1], norms[2], norms[3],
        raw * (2.0 / denom),
    )


def solution(mesh):
    n_dp, n_ctx = mesh.shape["dp"], mesh.shape["ctx"]
    in_specs = (
        P("dp", "ctx", None), P(("dp", "ctx"), None, None), P(None, "dp", "ctx", None),
        P(None, ("dp", "ctx"), None, None), P(("dp", "ctx"), None, None), P(("dp", "ctx"), None),
        P(("dp", "ctx")), P(), P(), P("dp", None, "tp"), P("tp", "dp"), P("dp", "tp"),
        P("tp", "dp"), P("dp"), P("dp"), P("dp"), P("dp"),
    )
    out_specs = (
        P("dp", "ctx", None), P(("dp", "ctx"), None, None), P(), P("dp", "ctx", None),
        P(("dp", "ctx"), None, None), P("dp", None, "tp"), P("tp", "dp"), P("dp", "tp"),
        P("tp", "dp"), P("dp"), P("dp"), P("dp"), P("dp"), P(),
    )
    return jax.shard_map(
        functools.partial(per_device, n_dp, n_ctx),
        mesh=mesh, in_specs=in_specs, out_specs=out_specs, check_vma=False,
    )
```

time: 1070 us -> 313 us (0.29); the launches traced: 1060 us -> 312 us
  local copies, waits for them, and re-layouts: 421 us -> 26.7 us
  waiting for transfers between devices: 302 us -> 0 us
  Pallas kernels: 0 us -> 274 us
  matrix products: 115 us -> 0 us
  blocking collectives: 103 us -> 0 us
  other arithmetic: 94.8 us -> 5.56 us
  between operations: 20.9 us -> 5.29 us
    unnamed x202 -> x29, local copies, waits for them, and re-layouts: 403 us -> 7.65 us
    pallas_call x0 -> x5, Pallas kernels: none -> 274 us  [kernel_call(): pl.pallas_call(body, out_shape=[jax.ShapeDtypeStruct(s, d) for s, d in ou...]
    psum x6 -> x0, waiting for transfers between devices: 219 us -> none  [the longest x1 48.5 us: per_device(): attn_p, attn_c = lax.psum((part_p, part_c), 'tp')]
    dot_general x33 -> x0, matrix products: 115 us -> none  [the longest x1 11.8 us: per_device(): jnp.einsum('ghqd,ghkd->ghqk', q_p, prompt_keys, preferred_element_type=f32)]
    psum x3 -> x0, blocking collectives: 51.3 us -> none  [the longest x2 42.6 us: per_device(): err_all, count_all, dwa_all = lax.psum((err, count, raw_dwa), ('dp', 'ctx'))]
    all_gather x4 -> x0, waiting for transfers between devices: 47.9 us -> none  [the longest x1 24.9 us: per_device(): lax.all_gather(v_p, 'ctx', axis=2, tiled=True)]
    all_gather x6 -> x0, blocking collectives: 46.7 us -> none  [the longest x1 16.1 us: per_device(): lax.all_gather(ln2_bias, 'dp', axis=0, tiled=True)]
    convert_element_type x24 -> x0, other arithmetic: 38.2 us -> none  [the longest x1 9.41 us: per_device(): xn1_p = prompt_normalized.astype(bfloat16_cast)]
  transfers between devices with their start and end apart: 16 -> 0, of which waited for: 10 -> 0; matrix products, arithmetic and copies ran while one was open for 20% -> 0% of each run, Pallas kernels for 0% -> 0%
where the time goes in v1:
time: 313 us; the launch traced here: 312 us
  Pallas kernels  274 us (88%)
  local copies, waits for them, and re-layouts  26.7 us (9%)
  other arithmetic  5.56 us (2%)
  between operations  5.29 us (2%)
    pallas_call x5, Pallas kernels, kernel_call(): pl.pallas_call(body, out_shape=[jax.ShapeDtypeStruct(s, d) for s, d in ou...  274 us
    unnamed x29, local copies, waits for them, and re-layouts  7.65 us

profile of v1, /device:TPU:0, one launch (start us, length us, event | category | flops | bytes accessed | tf_op | source)
XLA Modules:
  0.0 312.1 jit_solution(5213062827228949623)
XLA Ops:
  0.6 1.2 slice.94
  2.7 1.2 pad_maximum_fusion.2.sc
  4.0 1.1 fusion.3
  5.6 1.0 concatenate.22.w
  8.9 22.0 %project.1 = (bf16[1536,256]{1,0:T(8,128)(2,1)}, bf16[1536,384]{1,0:T(8,128)(2,1)}, bf16[1536,768]{1,0:T(8,128)(2,1)}, f32[8,768]{1,0:T(8,128)}, f32[768,384]{1,...) custom-call(bf16[1024,768]{1,0:T(8,128)(2,1)} %bitcast.24, bf16[512,768]{1,0:T(8,128)(2,1)} %bitcast.27, ...), custom_call_target="tpu_custom_call" | custom-call | bytes 31457280 | tf_op jit(solution)/shard_map/project/pallas_call | solution.py:53
  31.5 61.5 %attend.1 = (bf16[1536,256]{1,0:T(8,128)(2,1)}, f32[16,256]{1,0:T(8,128)}, f32[32,128]{1,0:T(8,128)}, bf16[256,768]{1,0:T(8,128)(2,1)}, bf16[768,768]{1,0:T(8,128)(2,1)}, /*index=5*/bf16[768,768]{1,0:T(8,128)(2,1)}) custom-call(s32[2]{0:T(128)} %sel.1, bf16[1536,256]{1,0:T(8,128)(2,1)} %get-tuple-element.45.q, bf16[1536,384]{1,0:T(8,128)(2,1)} %get-tuple-element.46.kv, ...), custom_call_target="tpu_custom_call" | custom-call | bytes 31457280 | tf_op jit(solution)/shard_map/attend/pallas_call | solution.py:53
  93.8 54.4 %middle.1 = (bf16[512,768]{1,0:T(8,128)(2,1)}, bf16[512,768]{1,0:T(8,128)(2,1)}, bf16[512,768]{1,0:T(8,128)(2,1)}, bf16[512,768]{1,0:T(8,128)(2,1)}, bf16[512,76...) custom-call(f32[5]{0:T(128)} %pad_maximum_fusion.2.sc, ...), custom_call_target="tpu_custom_call" | custom-call | bytes 31457280 | tf_op jit(solution)/shard_map/middle/pallas_call | solution.py:53
  148.3 55.9 %attend_back.1 = (bf16[1536,640]{1,0:T(8,128)(2,1)}, bf16[1024,768]{1,0:T(8,128)(2,1)}, bf16[1728,384]{1,0:T(8,128)(2,1)}) custom-call(f32[5]{0:T(128)} %pad_maximum_fusion.2.sc, f32[32,128]{1,0:T(8,128)} %get-tuple-element.48.msgs, bf16[4,768,128]{2,1,0:T(8,128)(2,1)} %get-tuple-element.54.qs, bf16[512,256]{1,0:T(8,128)(2,1)} %get-tuple-element.55.do, ...), custom_call_target="tpu_custom_call" | custom-call | bytes 31457280 | tf_op jit(solution)/shard_map/attend_back/pallas_call | solution.py:53
  204.2 80.8 %input_grad.1 = (bf16[1024,768]{1,0:T(8,128)(2,1)}, bf16[512,768]{1,0:T(8,128)(2,1)}, f32[16,768]{1,0:T(8,128)}, f32[1728,384]{1,0:T(8,128)}, f32[384,640]{1,0:T(8,128)}) custom-call(bf16[1536,640]{1,0:T(8,128)(2,1)} %get-tuple-element.65.dcat, bf16[768,640]{1,0:T(8,128)(2,1)} %get-tuple-element.66.w, bf16[1024,768]{1,0:T(8,128)(2,1)} %bitcast.26, ...), custom_call_target="tpu_custom_call" | custom-call | bytes 31457280 | tf_op jit(solution)/shard_map/input_grad/pallas_call | solution.py:53
  284.9 0.9 slice_reduce_fusion
  286.4 1.2 fusion.4
  290.9 1.1 fusion.2
  292.0 1.1 fusion.1
  293.2 1.0 slice_bitcast_fusion
  294.3 1.3 copy.38
  295.5 1.7 slice.113
  297.2 1.3 fusion
  298.6 1.1 pad_maximum_fusion.1
  299.7 2.5 slice.116
  303.8 1.2 maximum_multiply_fusion
  305.0 1.1 copy.47
  306.7 0.9 copy.48
  308.4 1.1 copy.49
  310.1 0.9 copy.50
  (45 shorter events, 9.3 us)
Async XLA Ops:
  5.4 1.3 copy-start.5
  5.4 1.9 copy-start.6
  5.4 2.4 copy-start.7
  5.4 3.0 copy-start.8
  8.9 22.0 %copy-start.4 = (s32[2,256]{1,0:T(2,128)S(1)}, s32[2,256]{1,0:T(2,128)}, u32[]{:S(2)}) copy-start(s32[2,256]{1,0:T(2,128)} %valid.1) | copy-start | bytes 6148
  299.7 4.0 %copy-start.9 = (s32[4]{0:T(128)S(1)}, s32[4]{0:T(128)}, u32[]{:S(2)}) copy-start(s32[4]{0:T(128)} %param.24) | copy-start | bytes 52
  299.7 5.3 %copy-start = (bf16[1024,768]{1,0:T(8,128)(2,1)S(1)}, bf16[1024,768]{1,0:T(8,128)(2,1)}, u32[]{:S(2)}) copy-start(bf16[1024,768]{1,0:T(8,128)(2,1)} %get-tuple-element.63) | copy-start | bytes 4718596
  305.0 1.7 copy-start.2
  306.7 1.7 copy-start.1
  308.4 1.7 copy-start.3

commit v2 on v1

v2 whole, which is shorter than its diff:
```python
import functools
import math

import jax
import jax.numpy as jnp
from jax import lax
from jax.experimental import pallas as pl
from jax.experimental.pallas import tpu as pltpu
from jax.sharding import PartitionSpec as P

HEAD_DIM = 64
EPS = 1e-05
NEG = -1e30
MESH = pl.DeviceIdType.MESH
f32 = jnp.float32
bf16 = jnp.bfloat16
VMEM_SPEC = pl.BlockSpec(memory_space=pltpu.VMEM)
SMEM_SPEC = pl.BlockSpec(memory_space=pltpu.SMEM)
HBM_SPEC = pl.BlockSpec(memory_space=pl.ANY)
DMA = pltpu.SemaphoreType.DMA
LIMIT = 56 << 20
NT = (((1,), (1,)), ((), ()))
TN = (((0,), (0,)), ((), ()))
CH = 128
BIG = 256
REST = 7
LINE_STEP = 2


def dot(a, b):
    return jnp.dot(a, b, preferred_element_type=f32)


def dot_nt(a, b):
    return lax.dot_general(a, b, NT, preferred_element_type=f32)


def dot_tn(a, b):
    return lax.dot_general(a, b, TN, preferred_element_type=f32)


def rows(start, size):
    return pl.ds(pl.multiple_of(start, size), size)


def loop(count, body):
    def step(i, carry):
        body(i)
        return carry

    lax.fori_loop(0, count, step, 0)


def kernel_call(body, outs, scratch, cid, specs, args, name, out_specs=None):
    return pl.pallas_call(
        body,
        out_shape=[jax.ShapeDtypeStruct(s, d) for s, d in outs],
        in_specs=specs,
        out_specs=out_specs or [VMEM_SPEC] * len(outs),
        scratch_shapes=scratch,
        compiler_params=pltpu.CompilerParams(
            collective_id=cid, has_side_effects=True, vmem_limit_bytes=LIMIT
        ),
        cost_estimate=pl.CostEstimate(flops=0, bytes_accessed=30 << 20, transcendentals=0),
        name=name,
    )(*args)


def greet(partners):
    barrier = pltpu.get_barrier_semaphore()
    for device in partners:
        pl.semaphore_signal(barrier, inc=1, device_id=device, device_id_type=MESH)
    pl.semaphore_wait(barrier, len(partners))


def remote(src, dst, send, recv, device):
    return pltpu.make_async_remote_copy(
        src_ref=src,
        dst_ref=dst,
        send_sem=send,
        recv_sem=recv,
        device_id=device,
        device_id_type=MESH,
    )


def axis_peers(axis, count):
    me = lax.axis_index(axis)
    return [{axis: lax.rem(me + d, count)} for d in range(1, count)]


def tp_place():
    tp = lax.axis_index("tp")
    core = lax.rem(tp, 2)
    mate = {"tp": tp + 1 - 2 * core}
    across = {"tp": lax.rem(tp + 2, 4)}
    return core, mate, across


def norm_rows(x):
    mean = jnp.mean(x, -1, keepdims=True)
    centered = x - mean
    var = jnp.mean(centered * centered, -1, keepdims=True)
    inverse = lax.rsqrt(var + EPS)
    return centered * inverse, inverse


def norm_back(gradient, whitened, inverse, gain):
    e = gradient * gain
    return inverse * (
        e - jnp.mean(e, -1, keepdims=True) - whitened * jnp.mean(e * whitened, -1, keepdims=True)
    )


def lanes_below(shape, bound):
    return lax.broadcasted_iota(jnp.int32, shape, len(shape) - 1) < bound


def turn(y, tab, sign, half):
    cos, low, high = tab[:, :128], tab[:, 128:256], tab[:, 256:384]
    turned = sign * (pltpu.roll(y, 96, 1) * low + pltpu.roll(y, 32, 1) * high)
    if not half:
        return y * cos + turned
    return jnp.where(lanes_below(y.shape, 64), y * cos + turned, y)


W_PARTS = ((1, 0, 128, 256), (2, 0, 128, 384), (1, 128, 64, 512), (2, 128, 64, 576), (0, 0, 192, 0))


def front_body(
    n_ctx, n_dp, share, plen, clen, groups, conts,
    sel, px, cx, w, g1, b1, g2, b2, valid, wo, wu, wd,
    xn_o, kv_o, tab_o, w_o, wu_o, wd_o, wo_o, o, lse, msgs, gains, qpack,
    xn, q, kvs, kvc, tab, w_full, gb, gbs, cnt, cnts, notes, m_s, l_s, acc_s,
    wgs, s_x, r_x, s_kv, r_kv, s_c, r_c, s_w, r_w, osem,
):
    me = lax.axis_index("ctx")
    mine = lax.axis_index("dp")
    depth = w.shape[2]
    width = px.shape[1]
    last = n_ctx - 1
    n_prompt = groups * plen
    n_cont = conts * clen
    tile = clen
    dp_peers = axis_peers("dp", n_dp)
    peers = axis_peers("ctx", n_ctx)
    for i, vector in enumerate((g1, b1, g2, b2)):
        gb[i:i + 1] = vector[...].astype(f32).reshape(1, depth)
    gb[4:8] = jnp.zeros((4, depth), f32)
    cnt[...] = jnp.zeros(cnt.shape, f32) + jnp.sum(valid[...].astype(f32))
    greet(dp_peers + peers)

    copies = []
    weights = []
    if share:
        cols = pl.ds(pl.multiple_of(mine * depth, 128), depth)
        here = rows(mine * depth, depth)
    for d, device in enumerate(dp_peers):
        pairs = [(gb, gbs.at[mine]), (cnt, cnts.at[mine])]
        if share:
            pairs += [
                (w.at[p, a:a + n], w_full.at[t:t + n, cols]) for p, a, n, t in W_PARTS
            ]
        else:
            pairs += [(w, wgs.at[mine])]
        copies.append(
            [remote(s, t, s_x.at[d, i], r_x.at[d, i], device) for i, (s, t) in enumerate(pairs)]
        )
    for i in range(len(copies[0])):
        for group in copies:
            group[i].start()
    local = []
    if share:
        pairs = [
            (wo.at[0:128], wo_o.at[0:128, cols]), (wo.at[128:192], wo_o.at[192:256, cols]),
            (wu, wu_o.at[here]), (wd, wd_o.at[:, cols]),
        ]
        for d, device in enumerate(dp_peers):
            for i, (s, t) in enumerate(pairs):
                weights.append(remote(s, t, s_w.at[d, i], r_w.at[d, i], device))
        for copy in weights:
            copy.start()
        local += [pltpu.make_async_copy(s, t, osem.at[i]) for i, (s, t) in enumerate(pairs)]
        for copy in local:
            copy.start()
        for p, a, n, t in W_PARTS:
            w_full[t:t + n, cols] = w[p, a:a + n]
    else:
        wgs[mine] = w[...]
    wo_o[128:192] = jnp.zeros((64, width), bf16)
    w_full[192:256] = jnp.zeros((64, width), bf16)
    gbs[mine] = gb[...]
    cnts[mine] = cnt[...]

    def table(count, base, start):
        def body(i):
            shape = (CH, 128)
            lane = lax.broadcasted_iota(jnp.int32, shape, 1)
            row = lax.broadcasted_iota(jnp.int32, shape, 0)
            turns = lax.rem(lane, 32).astype(f32) * (-2.0 * math.log(10000.0) / HEAD_DIM)
            angle = (row + (start + i * CH)).astype(f32) * jnp.exp(turns)
            sin = jnp.sin(angle)
            left = lax.rem(lane, 64) < 32
            at = rows(base + i * CH, CH)
            tab[at, 0:128] = jnp.cos(angle)
            tab[at, 128:256] = jnp.where(left, -sin, 0.0)
            tab[at, 256:384] = jnp.where(left, 0.0, sin)

        loop(count // CH, body)

    table(plen, 0, me * plen)
    table(clen, plen, n_ctx * plen)

    def save(src, dst, i):
        copy = pltpu.make_async_copy(src, dst, osem.at[i])
        copy.start()
        local.append(copy)

    save(tab, tab_o, 4)
    for group in copies:
        group[0].wait_recv()
        group[1].wait_recv()

    def one_hot(d):
        row = lax.broadcasted_iota(jnp.int32, (depth, width), 0) + d * depth
        col = lax.broadcasted_iota(jnp.int32, (depth, width), 1)
        return (row == col).astype(f32).astype(bf16)

    total = jnp.zeros(gains.shape, f32)
    count = jnp.zeros(cnt.shape, f32)
    for d in range(n_dp):
        total += dot(gbs[d].astype(bf16), one_hot(d))
        count += cnts[d]
    gains[...] = total
    note = notes.at[me]
    notes[me] = count
    for i in range(conts):
        notes[me, 1 + i:2 + i] = jnp.zeros((1, 128), f32) + sel[i].astype(f32)
    counts = [remote(note, note, s_c.at[d], r_c.at[d], device) for d, device in enumerate(peers)]
    for copy in counts:
        copy.start()

    def norm_part(x, base):
        def body(i):
            whitened, _ = norm_rows(x[rows(i * CH, CH)].astype(f32))
            xn[rows(base + i * CH, CH)] = (whitened * gains[0:1] + gains[1:2]).astype(bf16)

        loop(x.shape[0] // CH, body)

    norm_part(px, 0)
    norm_part(cx, n_prompt)
    save(xn, xn_o, 5)

    def arrive(i):
        if share:
            for group in copies:
                group[2 + i].wait_recv()
        elif i == 0:
            for group in copies:
                group[2].wait_recv()
            for p, a, n, t in W_PARTS:
                part = jnp.zeros((n, width), f32)
                for d in range(n_dp):
                    part += dot(wgs[d, p, a:a + n], one_hot(d))
                w_full[t:t + n] = part.astype(bf16)

    def hop(slot, step, side):
        there = kvs.at[slot]
        return remote(there, there, s_kv.at[side, slot], r_kv.at[slot], {"ctx": me + step})

    def kv_rows(count, base, tab_base, period, dst):
        def body(i):
            at = rows(i * BIG, BIG)
            t = tab[rows(tab_base + lax.rem(i * BIG, period), BIG)]
            x = xn[rows(base + i * BIG, BIG)]
            y = dot_nt(x, w_full[256:512])
            dst[at, 0:128] = turn(y[:, 0:128], t, 1.0, False).astype(bf16)
            dst[at, 128:256] = y[:, 128:256].astype(bf16)
            dst[at, 256:384] = turn(dot_nt(x, w_full[512:640]), t, 1.0, True).astype(bf16)

        loop(count // BIG, body)

    def q_rows_of(count, base, tab_base, period):
        def body(i):
            at = rows(base + i * BIG, BIG)
            t = tab[rows(tab_base + lax.rem(i * BIG, period), BIG)]
            y = dot_nt(xn[at], w_full[0:256])
            q[at, 0:128] = (turn(y[:, 0:128], t, 1.0, False) * 0.125).astype(bf16)
            q[at, 128:256] = (turn(y[:, 128:256], t, 1.0, True) * 0.125).astype(bf16)

        loop(count // BIG, body)

    for i in range(4):
        arrive(i)
    kv_rows(n_prompt, 0, 0, plen, kvs.at[me])

    @pl.when(me < last)
    def _():
        hop(me, 1, 0).start()

    @pl.when(me > 0)
    def _():
        hop(me, -1, 1).start()

    save(kvs.at[me], kv_o.at[0:n_prompt], 6)
    kv_rows(n_cont, n_prompt, plen, clen, kvc)
    save(kvc, kv_o.at[n_prompt:n_prompt + n_cont], 7)
    arrive(4)
    save(w_full, w_o, 8)
    q_rows_of(n_cont, n_prompt, plen, clen)
    q_rows_of(n_prompt, 0, 0, plen)

    def update(at, q_rows, k, v, mask, first):
        s = dot_nt(q_rows, k)
        if mask is not None:
            s = mask(s)
        top = jnp.max(s, -1, keepdims=True)
        if first:
            m_new = jnp.broadcast_to(top, (s.shape[0], 128))
        else:
            m_old = m_s[at]
            m_new = jnp.maximum(m_old, top)
        total = None
        parts = []
        for j in range(s.shape[1] // 128):
            p = jnp.exp(s[:, 128 * j:128 * j + 128] - m_new)
            total = p if total is None else total + p
            parts.append(p.astype(bf16))
        pv = dot(jnp.concatenate(parts, 1), v)
        m_s[at] = m_new
        if first:
            l_s[at] = total
            acc_s[at] = pv
        else:
            fade = jnp.exp(m_old - m_new)
            l_s[at] = l_s[at] * fade + total
            acc_s[at] = acc_s[at] * fade + pv

    low = lanes_below((tile, 128), 64)

    def heads(q_at, state, k_b, k_c, k_d, mask, first):
        a = q[q_at, 0:128]
        zero = jnp.zeros_like(a)
        update(state, jnp.where(low, a, zero), k_b, k_c, mask, first)
        update(state + 1, jnp.where(low, zero, a), k_b, k_c, mask, first)
        update(state + 2, q[q_at, 128:256], k_d, k_d, mask, first)

    tiles = plen // tile

    def prompt_part(slot, diagonal):
        def body(i):
            group = i // tiles
            t = lax.rem(i, tiles)
            at = rows(group * plen, plen)
            mask = None
            if diagonal:
                def mask(s):
                    row = lax.broadcasted_iota(jnp.int32, s.shape, 0) + t * tile
                    col = lax.broadcasted_iota(jnp.int32, s.shape, 1)
                    return jnp.where(col <= row, s, NEG)
            heads(
                rows(i * tile, tile), 3 * i,
                kvs[slot, at, 0:128], kvs[slot, at, 128:256], kvs[slot, at, 256:384],
                mask, diagonal,
            )

        loop(groups * tiles, body)

    def cont_part(slot, first):
        def body(i):
            k = kvs[slot, 0:plen]
            for g in range(1, groups):
                k = jnp.where(sel[i] == g, kvs[slot, g * plen:(g + 1) * plen], k)
            heads(
                rows(n_prompt + i * tile, tile), 3 * (groups * tiles + i),
                k[:, 0:128], k[:, 128:256], k[:, 256:384], None, first,
            )

        loop(conts, body)

    def self_part():
        def body(i):
            at = rows(i * tile, tile)

            def mask(s):
                row = lax.broadcasted_iota(jnp.int32, s.shape, 0)
                col = lax.broadcasted_iota(jnp.int32, s.shape, 1)
                bias = (valid[pl.ds(i, 1)].astype(f32) - 1.0) * (-NEG)
                return jnp.where(col <= row, s + bias, NEG)

            heads(
                rows(n_prompt + i * tile, tile), 3 * (groups * tiles + i),
                kvc[at, 0:128], kvc[at, 128:256], kvc[at, 256:384], mask, False,
            )

        loop(conts, body)

    cont_part(me, True)
    prompt_part(me, True)
    self_part()
    e0 = q[n_prompt:n_prompt + clen, 128:256].astype(f32)
    e1 = q[n_prompt + clen:n_prompt + n_cont, 128:256].astype(f32)
    qpack[0:n_cont] = q[n_prompt:n_prompt + n_cont, 0:128]
    qpack[n_cont:n_cont + clen] = jnp.where(low, e0, pltpu.roll(e1, 64, 1)).astype(bf16)

    def ring(e):
        d = e + 1

        @pl.when(me - d >= 0)
        def _():
            hop(me - d, 1, 0).wait_recv()

            @pl.when(me < last)
            def _():
                hop(me - d, 1, 0).start()

        @pl.when(me + d <= last)
        def _():
            hop(me + d, -1, 1).wait_recv()

            @pl.when(me > 0)
            def _():
                hop(me + d, -1, 1).start()

        @pl.when(me - d >= 0)
        def _():
            cont_part(me - d, False)
            prompt_part(me - d, False)

        @pl.when(me + d <= last)
        def _():
            cont_part(me + d, False)

    loop(last, ring)

    for copy in counts:
        copy.wait()
    for d in range(n_ctx):
        msgs[8 * d:8 * d + 8] = notes[d]

    def finish(at, state):
        l0 = jnp.sum(l_s[state], -1, keepdims=True)
        l1 = jnp.sum(l_s[state + 1], -1, keepdims=True)
        l2 = jnp.sum(l_s[state + 2], -1, keepdims=True)
        o[at, 0:128] = jnp.where(low, acc_s[state] / l0, acc_s[state + 1] / l1).astype(bf16)
        o[at, 128:256] = jnp.where(low, 0.0, acc_s[state + 2] / l2).astype(bf16)
        return (l0, l1, l2)

    def finish_prompt(i):
        finish(rows(i * tile, tile), 3 * i)

    loop(groups * tiles, finish_prompt)
    for i in range(conts):
        state = 3 * (groups * tiles + i)
        sums = finish(rows(n_prompt + i * tile, tile), state)
        lse[8 * i:8 * i + 8] = jnp.zeros((8, tile), f32)
        for h in range(3):
            value = m_s[state + h] + jnp.log(sums[h])
            lse[8 * i + h:8 * i + h + 1] = jnp.transpose(value)[0:1]

    for slot in range(n_ctx):
        @pl.when((slot <= me) & (me < last))
        def _():
            hop(slot, 1, 0).wait_send()

        @pl.when((slot >= me) & (me > 0))
        def _():
            hop(slot, -1, 1).wait_send()

    for group in copies:
        for copy in group:
            copy.wait_send()
    for copy in weights:
        copy.wait()
    for copy in local:
        copy.wait()


def full_at(a, core, split, c_split):
    b = a // split
    return a + core * split * (1 - b) + b * (split + core * c_split)


class TpSum:
    @staticmethod
    def scratch(half, width):
        n = half // CH
        return [
            pltpu.VMEM((half, width), bf16), pltpu.VMEM((half, width), bf16),
            pltpu.VMEM((half, width), bf16), pltpu.VMEM((half, width), bf16),
            pltpu.VMEM((half, width), f32), DMA((2, n)), DMA((2, n)),
        ]

    def __init__(self, half, start, place, scratch, compute):
        self.half, self.start, self.place, self.compute = half, start, place, compute
        self.snd1, self.rcv1, self.snd2, self.rcv2, self.own, self.send, self.recv = scratch
        self.core, self.mate, self.across = tp_place()
        self.n = half // CH

    def row(self, i):
        return lax.rem(self.start + i * CH, self.half)

    def pair(self, i):
        at = rows(self.row(i), CH)
        return remote(
            self.snd1.at[at], self.rcv1.at[at], self.send.at[0, i], self.recv.at[0, i], self.mate
        )

    def link(self, i):
        at = rows(self.row(i), CH)
        return remote(
            self.snd2.at[at], self.rcv2.at[at], self.send.at[1, i], self.recv.at[1, i], self.across
        )

    def second(self, i):
        at = rows(self.row(i), CH)
        self.pair(i).wait_recv()
        self.snd2[at] = (self.own[at] + self.rcv1[at].astype(f32)).astype(bf16)
        self.link(i).start()

    def launch(self, i):
        a = self.row(i)
        at = rows(a, CH)
        self.snd1[at] = self.compute(self.place(a, 1 - self.core), CH).astype(bf16)
        self.pair(i).start()
        self.own[at] = self.compute(self.place(a, self.core), CH)

    def begin(self):
        def body(i):
            self.launch(i)

            @pl.when(i > 0)
            def _():
                self.second(i - 1)

        loop(self.n, body)
        self.second(self.n - 1)

    def take(self, i):
        at = rows(self.row(i), CH)
        self.link(i).wait_recv()
        return self.snd2[at].astype(f32) + self.rcv2[at].astype(f32)

    def close(self):
        def body(i):
            self.pair(i).wait_send()
            self.link(i).wait_send()

        loop(self.n, body)


class Share:
    def __init__(self, ref, place, sems):
        self.ref, self.place = ref, place
        self.send, self.recv = sems
        _, self.mate, _ = tp_place()

    def copy(self, i, a):
        at = rows(self.place(a), CH)
        return remote(self.ref.at[at], self.ref.at[at], self.send.at[i], self.recv.at[i], self.mate)


def share_scratch(half):
    return [DMA((half // CH,)), DMA((half // CH,))]


GELU = 0.7978845608028654


def gelu_tanh(u):
    return jnp.tanh(GELU * (u + 0.044715 * (u * u * u)))


def mixed_states(ids, dwa, hist, at, y):
    mixed = dwa[4] * y
    for j in range(4):
        mixed += dwa[ids[j]] * hist[j, at].astype(f32)
    return mixed


def column(row):
    return jnp.transpose(jnp.broadcast_to(row, (128, row.shape[1])))


def middle_body(
    n_ctx, n_prompt, clen,
    ids, dwa, o, qpack, msgs, wo, wu, wd, cx, gains, valid, hist, teach,
    out, dm, hid, xn, du, da, do, dh1, stat, qs,
    hc, tc, slope, h1, dy, mask, hsem, s_q, r_q, *scratch,
):
    core, mate, across = tp_place()
    ctx = lax.axis_index("ctx")
    half = clen
    n_cont = 2 * half
    mine = rows(core * half, half)
    loads = [
        pltpu.make_async_copy(hist.at[:, mine], hc, hsem.at[0]),
        pltpu.make_async_copy(teach.at[mine], tc, hsem.at[1]),
    ]
    for copy in loads:
        copy.start()
    qs[ctx] = qpack[...]
    mask[...] = column(valid[pl.ds(core, 1)].astype(f32))
    stat[...] = jnp.zeros(stat.shape, f32)
    others = axis_peers("ctx", n_ctx)
    greet([mate, across] + others)
    s1, s2, s3 = scratch[0:7], scratch[7:14], scratch[14:21]
    shares = scratch[21:]

    def place(a, c):
        return a + c * half

    def home(a):
        return a + core * half

    def each(body):
        loop(half // CH, body)

    def attn(at, size):
        return dot(o[rows(n_prompt + at, size)], wo[...])

    first = TpSum(half, 0, place, s1, attn)
    each(first.launch)
    each(first.second)
    moves = [
        remote(qs.at[ctx], qs.at[ctx], s_q.at[d], r_q.at[d], device)
        for d, device in enumerate(others)
    ]
    for copy in moves:
        copy.start()
    give_xn = Share(xn, home, shares[0:2])

    def normed(i):
        a = first.row(i)
        h = cx[rows(home(a), CH)].astype(f32) + first.take(i)
        h1[rows(a, CH)] = h
        whitened, _ = norm_rows(h)
        xn[rows(home(a), CH)] = (whitened * gains[2:3] + gains[3:4]).astype(bf16)
        give_xn.copy(i, a).start()

    def hidden(at, size):
        here = rows(at, size)
        u = dot(xn[here], wu[...])
        t = gelu_tanh(u)
        g = (0.5 * u * (1.0 + t)).astype(bf16)
        hid[here] = g
        slope[here] = 0.5 * (1.0 + t) + (0.5 * GELU) * u * (1.0 - t * t) * (
            1.0 + (3.0 * 0.044715) * (u * u)
        )
        return dot(g, wd[...])

    second = TpSum(half, 0, place, s2, hidden)

    def onward(before, share, after):
        def body(i):
            before(i)

            @pl.when(i > 0)
            def _():
                after.second(i - 1)

            share.copy(i, after.row(i)).wait()
            after.launch(i)

        each(body)
        after.second(after.n - 1)

    onward(normed, give_xn, second)
    for copy in loads:
        copy.wait()
    give_dm = Share(dm, home, shares[2:4])
    give_out = Share(out, home, shares[4:6])
    count = msgs[0:1]
    for j in range(1, n_ctx):
        count += msgs[8 * j:8 * j + 1]
    coef = (2.0 * dwa[4]) / (jnp.maximum(count, 1.0) * (1.0 * cx.shape[1]))

    def add(row, value):
        stat[row:row + 1] += jnp.sum(value, 0, keepdims=True)

    def lossy(i):
        a = second.row(i)
        here, there = rows(a, CH), rows(home(a), CH)
        y = h1[here] + second.take(i)
        mixed = mixed_states(ids, dwa, hc, here, y)
        diff = mixed - tc[here].astype(f32)
        weighted = diff * mask[here][:, 0:1]
        grad = weighted * coef[:, 0:1]
        dy[here] = grad
        dm[there] = grad.astype(bf16)
        give_dm.copy(i, a).start()
        out[there] = mixed.astype(bf16)
        give_out.copy(i, a).start()
        add(4, weighted * diff)
        for j in range(4):
            add(5 + j, weighted * hc[j, here].astype(f32))
        add(9, weighted * y)

    def back(at, size):
        here = rows(at, size)
        d = (dot_nt(dm[here], wd[...]) * slope[here]).astype(bf16)
        du[here] = d
        return dot_nt(d, wu[...])

    third = TpSum(half, 0, place, s3, back)
    onward(lossy, give_dm, third)
    give_da = Share(da, home, shares[6:8])

    def grads(i):
        a = third.row(i)
        here = rows(a, CH)
        total = third.take(i)
        whitened, inverse = norm_rows(h1[here])
        grad = dy[here] + norm_back(total, whitened, inverse, gains[2:3])
        dh1[here] = grad
        da[rows(home(a), CH)] = grad.astype(bf16)
        give_da.copy(i, a).start()
        add(2, total * whitened)
        add(3, total)

    each(grads)
    each(lambda i: give_da.copy(i, third.row(i)).wait())

    def last(i):
        at = rows(i * BIG, BIG)
        do[at] = dot_nt(da[at], wo[...]).astype(bf16)

    loop(n_cont // BIG, last)
    each(lambda i: give_out.copy(i, second.row(i)).wait())
    for part in (first, second, third):
        part.close()
    for copy in moves:
        copy.wait()


class LineSum:
    @staticmethod
    def scratch(count, size, width):
        return [
            pltpu.VMEM((count, size, width), bf16), pltpu.VMEM((count, size, width), bf16),
            pltpu.VMEM((count, size, width), bf16), DMA((2, count)), DMA((2, count)),
        ]

    def __init__(self, me, src, dst, scratch, count, size):
        self.src, self.dst, self.count, self.size = src, dst, count, size
        self.got, self.pair, self.far, self.send, self.recv = scratch
        side = me // 2
        self.outer = (me == 0) | (me == 3)
        self.inner = (me == 1) | (me == 2)
        self.near = {"ctx": 1 + side}
        self.back = {"ctx": 3 * side}
        self.twin = {"ctx": 2 - side}

    def at(self, k):
        return rows(k * self.size, self.size)

    def up(self, k):
        return remote(
            self.src.at[self.at(k)], self.got.at[k], self.send.at[0, k], self.recv.at[0, k], self.near
        )

    def cross(self, k):
        return remote(
            self.pair.at[k], self.far.at[k], self.send.at[1, k], self.recv.at[1, k], self.twin
        )

    def down(self, k):
        return remote(
            self.pair.at[k], self.got.at[k], self.send.at[0, k], self.recv.at[0, k], self.back
        )

    def launch(self, k):
        @pl.when(self.outer)
        def _():
            self.up(k).start()

    def meet(self, k):
        @pl.when(self.inner)
        def _():
            self.up(k).wait_recv()
            self.pair[k] = (
                self.src[self.at(k)].astype(f32) + self.got[k].astype(f32)
            ).astype(bf16)
            self.cross(k).start()

    def turn(self, k):
        @pl.when(self.inner)
        def _():
            self.cross(k).wait()
            total = (self.pair[k].astype(f32) + self.far[k].astype(f32)).astype(bf16)
            self.pair[k] = total
            self.down(k).start()
            self.dst[self.at(k)] = total

    def land(self, k):
        @pl.when(self.outer)
        def _():
            self.up(k).wait_send()
            self.down(k).wait_recv()
            self.dst[self.at(k)] = self.got[k]

        @pl.when(self.inner)
        def _():
            self.down(k).wait_send()


def down_grads(hid, dm, cols, store):
    for j in range(hid.shape[1] // 256):
        store(j * 256, dot_tn(hid[:, 256 * j:256 * j + 256], dm[:, cols]))


def other_grads(ff, xn, du, o, da, cols, store):
    size = cols.size
    for j in range(ff // size):
        store(ff + j * size, dot_tn(xn[:, cols], du[:, size * j:size * j + size]))
    g = dot_tn(o[...], da[:, cols])
    store(ff + ff, g[0:128])
    store(ff + ff + 128, g[192:256])


def attend_back_body(
    n_ctx, n_dp, share, plen, clen, groups, conts, depth,
    ids, dwa, msgs, qs, do, o, lse, kv, valid, tab, gains, hid_h, dm_h, xn2_h, du_h, da_h,
    wo_h, wu_h, wd_h, px_h, hist_h, xn1_h, *refs,
):
    if share:
        dcat, out, g_sum, g_part = refs[:4]
        refs = refs[4:]
    else:
        dcat, out, g_down, g_up, g_out, g_kv = refs[:6]
        refs = refs[6:]
    (
        hid, dm, xn2, du, da, wo, wu, wd, px, hist, lsem,
        dos, sts, dqs, kd, acc_k, acc_v, acc_kd, acc_vd, dq_f, send, recv,
        xp, h1, xn1, flags,
    ) = refs[:26]
    s1, s2 = refs[26:33], refs[33:40]
    shares = refs[40:44]
    refs = refs[44:]
    core, mate, across = tp_place()
    me = lax.axis_index("ctx")
    dp = lax.axis_index("dp")
    peers = axis_peers("ctx", n_ctx)
    dp_peers = axis_peers("dp", n_dp) if share else []
    n_prompt = groups * plen
    n_cont = conts * clen
    half = plen
    own_rows = rows(core * half, half)
    pairs = [
        (wo_h, wo), (px_h.at[own_rows], px), (hid_h, hid), (dm_h, dm), (xn2_h, xn2), (du_h, du),
        (da_h, da), (wu_h, wu), (wd_h, wd), (hist_h.at[:, own_rows], hist), (xn1_h, xn1),
    ]
    loads = [
        pltpu.make_async_copy(s, t, lsem.at[i]) for i, (s, t) in enumerate(pairs)
    ]
    for copy in loads:
        copy.start()
    low = lanes_below((clen, 128), 64)
    zero = jnp.zeros((clen, 128), bf16)
    for c in range(conts):
        flags[c * clen:(c + 1) * clen] = column(valid[c:c + 1].astype(f32))

    g0 = do[0:clen, 128:256].astype(f32)
    g1 = do[clen:2 * clen, 128:256].astype(f32)
    dos[me, 0:n_cont] = do[:, 0:128]
    dos[me, n_cont:n_cont + clen] = jnp.where(low, pltpu.roll(g0, 64, 1), g1).astype(bf16)
    for c in range(conts):
        at = slice(c * clen, (c + 1) * clen)
        full = slice(n_prompt + c * clen, n_prompt + (c + 1) * clen)
        pa = do[at, 0:128].astype(f32) * o[full, 0:128].astype(f32)
        pe = do[at, 128:256].astype(f32) * o[full, 128:256].astype(f32)
        ta = jnp.transpose(pa)
        te = jnp.transpose(pe)
        st = 8 * c
        sts[me, st:st + 8] = lse[8 * c:8 * c + 8]
        sts[me, st + 3:st + 4] = jnp.sum(ta[0:64], 0, keepdims=True)
        sts[me, st + 4:st + 5] = jnp.sum(ta[64:128], 0, keepdims=True)
        sts[me, st + 5:st + 6] = jnp.sum(te[64:128], 0, keepdims=True)
    greet(peers + [mate, across] + dp_peers)
    sends = []
    for d, device in enumerate(peers):
        for i, ref in enumerate((sts, dos)):
            sends.append(remote(ref.at[me], ref.at[me], send.at[d, i], recv.at[d, i], device))
    for copy in sends:
        copy.start()

    def place(a, c):
        return a + c * half

    def home(a):
        return a + core * half

    loads[0].wait()
    loads[1].wait()

    def attn(at, size):
        return dot(o[rows(at, size)], wo[...])

    first = TpSum(half, 0, place, s1, attn)
    first.begin()

    for copy in loads[2:7]:
        copy.wait()
    ff = hid.shape[1]
    o_c = o.at[n_prompt:n_prompt + n_cont]
    bounds = (0, ff, 2 * ff + 192, 2 * ff + 576)
    if share:
        gsnd, grcv, gown, gdn, s_g, r_g = refs[:6]
        line = LineSum(me, gdn, g_sum, refs[6:11], 4, ff // 4)

    def cols_of(d):
        return pl.ds(pl.multiple_of(lax.rem(dp + d, n_dp) * depth, 128), depth)

    def give(d, i):
        span = slice(bounds[i], bounds[i + 1])
        return remote(
            gsnd.at[d - 1, span], grcv.at[d - 1, span], s_g.at[d - 1, i], r_g.at[d - 1, i],
            {"dp": lax.rem(dp + d, n_dp)},
        )

    def keeper(d):
        if d == 0:
            def store(at, value):
                gown[at:at + value.shape[0]] = value
        else:
            def store(at, value):
                gsnd[d - 1, at:at + value.shape[0]] = value.astype(bf16)
        return store

    def kv_grads(cols, store):
        for lo, hi in ((256, 384), (384, 512), (512, 640)):
            store(2 * ff + 192 + lo - 256, dot_tn(dcat[:, lo:hi], xn1[:, cols]))

    def settle(dst, i):
        for d in range(1, n_dp):
            give(d, i).wait()

        def body(j):
            at = rows(bounds[i] + j * 64, 64)
            total = gown[at]
            for d in range(n_dp - 1):
                total += grcv[d, at].astype(f32)
            dst(at, j, total.astype(bf16))

        loop((bounds[i + 1] - bounds[i]) // 64, body)

    if share:
        for d in range(1, n_dp):
            down_grads(hid, dm, cols_of(d), keeper(d))
            give(d, 0).start()
        for d in range(1, n_dp):
            other_grads(ff, xn2, du, o_c, da, cols_of(d), keeper(d))
            give(d, 1).start()
    else:
        width = dm.shape[1]
        for j in range(width // 256):
            cols = pl.ds(256 * j, 256)
            span = slice(256 * j, 256 * j + 256)

            def lay(at, value, span=span):
                if at < ff:
                    g_down[at:at + 256, span] = value.astype(bf16)
                elif at < 2 * ff:
                    g_up[span, at - ff:at - ff + 256] = value.astype(bf16)
                else:
                    g_out[at - 2 * ff:at - 2 * ff + value.shape[0], span] = value.astype(bf16)

            down_grads(hid, dm, cols, lay)
            other_grads(ff, xn2, du, o_c, da, cols, lay)

    kd[...] = pltpu.roll(kv[0:n_prompt, 256:384].astype(f32), 64, 1).astype(bf16)
    for acc in (acc_k, acc_v, acc_kd, acc_vd):
        acc[...] = jnp.zeros(acc.shape, f32)

    def one_head(q_rows, do_rows, k, v, lse_row, delta_row, mask):
        s = dot_nt(k, q_rows)
        p = jnp.exp(s - lse_row)
        if mask is not None:
            p = mask(p)
        dp_ = dot_nt(v, do_rows)
        ds = (p * (dp_ - delta_row)).astype(bf16)
        return p.astype(bf16), ds

    def halves(a):
        return jnp.where(low, a, zero), jnp.where(low, zero, a)

    def continuation(src, c, k_b, k_c, k_d, k_s, mask):
        base = c * clen
        a0, a1 = halves(qs[src, base:base + clen])
        d0, d1 = halves(dos[src, base:base + clen])
        e = halves(qs[src, n_cont:n_cont + clen])[c]
        g = halves(dos[src, n_cont:n_cont + clen])[c]
        st = 8 * c
        row = lambda i: sts[src, st + i:st + i + 1]
        p0, s0 = one_head(a0, d0, k_b, k_c, row(0), row(3), mask)
        dv = dot(p0, d0)
        dk = dot(s0, a0)
        dq0 = dot_tn(s0, k_b)
        p1, s1_ = one_head(a1, d1, k_b, k_c, row(1), row(4), mask)
        dv += dot(p1, d1)
        dk += dot(s1_, a1)
        dq1 = dot_tn(s1_, k_b)
        keys, values = (k_d, k_s) if c == 0 else (k_s, k_d)
        p2, s2_ = one_head(e, g, keys, values, row(2), row(5), mask)
        dvd = dot(p2, g)
        dkd = dot(s2_, e)
        dq2 = dot_tn(s2_, keys)
        return dk, dv, dkd, dvd, jnp.where(low, dq0, dq1), dq2

    def source(src, own):
        pair = []
        for c in range(conts):
            pick = msgs[pl.ds(src * 8 + 1 + c, 1)]

            def choose(one, two):
                return jnp.where(pick == 0.0, one.astype(f32), two.astype(f32)).astype(bf16)

            k_b = choose(kv[0:plen, 0:128], kv[plen:2 * plen, 0:128])
            k_c = choose(kv[0:plen, 128:256], kv[plen:2 * plen, 128:256])
            k_d = choose(kv[0:plen, 256:384], kv[plen:2 * plen, 256:384])
            k_s = choose(kd[0:plen], kd[plen:2 * plen])
            dk, dv, dkd, dvd, dqa, dqd = continuation(src, c, k_b, k_c, k_d, k_s, None)
            for g in range(groups):
                keep = (pick == 1.0 * g).astype(f32)
                at = slice(g * plen, (g + 1) * plen)
                acc_k[at] += keep * dk
                acc_v[at] += keep * dv
                acc_kd[at] += keep * dkd
                acc_vd[at] += keep * dvd
            pair.append(dqd)
            if own:
                dq_f[c * clen:(c + 1) * clen] = dqa
            else:
                dqs[n_ctx + src, c * clen:(c + 1) * clen] = dqa.astype(bf16)
        third = jnp.where(low, pair[0], pair[1])
        if own:
            dq_f[n_cont:n_cont + clen] = third
        else:
            dqs[n_ctx + src, n_cont:n_cont + clen] = third.astype(bf16)

    def other_of(d):
        return lax.rem(me + 2 * n_ctx - (d + 1), n_ctx)

    def back_copy(d):
        other = other_of(d)
        return remote(
            dqs.at[n_ctx + other], dqs.at[me], send.at[d, 2], recv.at[d, 2], {"ctx": other}
        )

    def visit(d):
        other = other_of(d)
        for i, ref in enumerate((sts, dos)):
            remote(ref.at[other], ref.at[other], send.at[d, i], recv.at[d, i], {"ctx": other}).wait_recv()
        source(other, False)
        back_copy(d).start()

    give_xn = Share(xp, home, shares[0:2])

    def normed(i):
        a = first.row(i)
        h = px[rows(a, CH)].astype(f32) + first.take(i)
        h1[rows(a, CH)] = h
        whitened, _ = norm_rows(h)
        xp[rows(home(a), CH)] = (whitened * gains[2:3] + gains[3:4]).astype(bf16)
        give_xn.copy(i, a).start()

    def hidden(at, size):
        u = dot(xp[rows(at, size)], wu[...])
        return dot((0.5 * u * (1.0 + gelu_tanh(u))).astype(bf16), wd[...])

    second = TpSum(half, 0, place, s2, hidden)
    def to_line(at, j, value):
        gdn[rows(j * 64, 64)] = value

    def to_part(at, j, value):
        g_part[rows(at.start - ff, 64)] = value

    source(me, True)
    for copy in loads[7:9]:
        copy.wait()

    def step(i):
        @pl.when(i < first.n)
        def _():
            normed(i)
            give_xn.copy(i, first.row(i)).wait()
            second.launch(i)

        @pl.when((i > 0) & (i < n_ctx))
        def _():
            visit(i - 1)

        @pl.when(i < first.n)
        def _():
            second.second(i)

        if share:
            @pl.when(i == LINE_STEP)
            def _():
                down_grads(hid, dm, cols_of(0), keeper(0))
                settle(to_line, 0)
                loop(4, line.launch)

    loop(max(half // CH, n_ctx), step)

    for c in range(conts):
        at = slice(n_prompt + c * clen, n_prompt + (c + 1) * clen)
        k_d = kv[at, 256:384]
        k_s = pltpu.roll(k_d.astype(f32), 64, 1).astype(bf16)

        def mask(p):
            key = lax.broadcasted_iota(jnp.int32, p.shape, 0)
            query = lax.broadcasted_iota(jnp.int32, p.shape, 1)
            return jnp.where(
                key <= query, p * flags[c * clen:(c + 1) * clen, 0:1], 0.0
            )

        dk, dv, dkd, dvd, dqa, dqd = continuation(
            me, c, kv[at, 0:128], kv[at, 128:256], k_d, k_s, mask
        )
        dq_f[c * clen:(c + 1) * clen] += dqa
        keep = low if c == 0 else jnp.logical_not(low)
        dq_f[n_cont:n_cont + clen] += jnp.where(keep, dqd, 0.0)
        t = tab[plen:plen + clen]
        dcat[at, 256:384] = turn(dk, t, -1.0, False).astype(bf16)
        dcat[at, 384:512] = dv.astype(bf16)
        if c == 0:
            joined = jnp.where(low, dkd, pltpu.roll(dvd, 64, 1))
        else:
            joined = jnp.where(low, pltpu.roll(dkd, 64, 1), dvd)
        dcat[at, 512:640] = turn(joined, t, -1.0, True).astype(bf16)

    zq = jnp.zeros((plen, 256), bf16)
    wide = lanes_below((plen, 128), 64)
    for g in range(groups):
        at = slice(g * plen, (g + 1) * plen)
        t = tab[0:plen]
        dcat[at, 0:256] = zq
        dcat[at, 256:384] = turn(acc_k[at], t, -1.0, False).astype(bf16)
        dcat[at, 384:512] = acc_v[at].astype(bf16)
        k2 = acc_kd[at] + pltpu.roll(acc_kd[at], 64, 1)
        v2 = acc_vd[at] + pltpu.roll(acc_vd[at], 64, 1)
        dcat[at, 512:640] = turn(jnp.where(wide, k2, v2), t, -1.0, True).astype(bf16)

    loads[10].wait()
    if share:
        for d in range(1, n_dp):
            kv_grads(cols_of(d), keeper(d))
            give(d, 2).start()
        other_grads(ff, xn2, du, o_c, da, cols_of(0), keeper(0))
        kv_grads(cols_of(0), keeper(0))
        loop(4, line.meet)
        settle(to_part, 1)
    else:
        for j in range(xn1.shape[1] // 256):
            span = slice(256 * j, 256 * j + 256)

            def lay_kv(at, value, span=span):
                at = at - 2 * ff - 192
                g_kv[at:at + 128, span] = value.astype(bf16)

            kv_grads(pl.ds(256 * j, 256), lay_kv)

    for d in range(n_ctx - 1):
        back_copy(d).wait_send()
        other = lax.rem(me + d + 1, n_ctx)
        remote(
            dqs.at[n_ctx + other], dqs.at[other], send.at[d, 2], recv.at[d, 2], {"ctx": other}
        ).wait_recv()
        dq_f[...] += dqs[other].astype(f32)
    for c in range(conts):
        at = slice(n_prompt + c * clen, n_prompt + (c + 1) * clen)
        t = tab[plen:plen + clen]
        pair = dq_f[c * clen:(c + 1) * clen] * 0.125
        dcat[at, 0:128] = turn(pair, t, -1.0, False).astype(bf16)
        third = dq_f[n_cont:n_cont + clen] * 0.125
        if c == 1:
            third = pltpu.roll(third, 64, 1)
        third = jnp.where(low, third, 0.0)
        dcat[at, 128:256] = turn(third, t, -1.0, True).astype(bf16)

    if share:
        loop(4, line.turn)

    loads[9].wait()
    give_out = Share(out, home, shares[2:4])

    def mixed(i):
        a = second.row(i)
        here = rows(a, CH)
        y = h1[here] + second.take(i)
        out[rows(home(a), CH)] = mixed_states(ids, dwa, hist, here, y).astype(bf16)
        give_out.copy(i, a).start()

    loop(half // CH, mixed)
    loop(half // CH, lambda i: give_out.copy(i, second.row(i)).wait())
    if share:
        settle(to_part, 2)
        loop(4, line.land)
    first.close()
    second.close()
    for copy in sends:
        copy.wait_send()


def input_grad_body(
    n_dp, n_ctx, share, split, c_split, depth,
    dcat, w, px, cx, gains, dh1, stat_in, xn_h, *refs,
):
    if share:
        g_part, grad_p, grad_c, fin, g_rest = refs[:5]
        refs = refs[5:]
    else:
        grad_p, grad_c, fin, g_q = refs[:4]
        refs = refs[4:]
    xn, lsem, grad, stat, stats_m, stats_y, stats_c, stats_d, s_s, r_s = refs[:10]
    s1 = refs[10:17]
    shares = refs[17:19]
    refs = refs[19:]
    core, mate, across = tp_place()
    me = lax.axis_index("ctx")
    dp = lax.axis_index("dp")
    ctx_peers = axis_peers("ctx", n_ctx)
    dp_peers = axis_peers("dp", n_dp)
    half = split + c_split
    n_prompt = 2 * split
    n_cont = 2 * c_split
    load = pltpu.make_async_copy(xn_h.at[n_prompt:n_prompt + n_cont], xn, lsem.at[0])
    load.start()
    stat[...] = 0.5 * stat_in[...]
    greet([mate, across] + ctx_peers + dp_peers)
    if share:
        gsnd, gown, grcv, s_g, r_g, qsh, qsum = refs[:7]
        n_rest = g_part.shape[0]
        rest = LineSum(me, g_part, g_rest.at[0:n_rest], refs[7:12], REST, n_rest // REST)
        tail = LineSum(me, qsh, qsum, refs[12:17], 1, 3 * HEAD_DIM)
        loop(REST, rest.launch)

    def place(a, c):
        return full_at(a, c, split, c_split)

    def home(a):
        return full_at(a, core, split, c_split)

    def compute(at, size):
        part = dot(dcat[rows(at, size)], w[...])
        b = at // n_prompt
        p = px[rows(at * (1 - b), size)].astype(f32)
        c = cx[rows((at - n_prompt) * b, size)].astype(f32)
        whitened, _ = norm_rows(jnp.where(b == 0, p, c))
        stat[0:1] += jnp.sum(part * whitened, 0, keepdims=True)
        stat[1:2] += jnp.sum(part, 0, keepdims=True)
        return part

    total = TpSum(half, split, place, s1, compute)
    total.begin()

    def small(src, dst, i, device):
        return remote(src, dst, s_s.at[i], r_s.at[i], device)

    stats_m[0] = stat[...]
    to_mate = small(stats_m.at[0], stats_m.at[1], 0, mate)
    to_mate.start()
    load.wait()

    def q_grads(cols):
        return dot_tn(dcat[n_prompt:n_prompt + n_cont, 0:256], xn[:, cols])[0:3 * HEAD_DIM]

    gives = []
    if share:
        for d in range(1, n_dp):
            other = lax.rem(dp + d, n_dp)
            cols = pl.ds(pl.multiple_of(other * depth, 128), depth)
            gsnd[d - 1] = q_grads(cols).astype(bf16)
            copy = remote(
                gsnd.at[d - 1], grcv.at[d - 1], s_g.at[d - 1], r_g.at[d - 1], {"dp": other}
            )
            copy.start()
            gives.append(copy)
        gown[...] = q_grads(pl.ds(pl.multiple_of(dp * depth, 128), depth))
    else:
        g_q[...] = q_grads(slice(None)).astype(bf16)
    to_mate.wait()
    stats_y[0] = stats_m[0] + stats_m[1]
    to_far = small(stats_y.at[0], stats_y.at[1], 1, across)
    to_far.start()
    give = Share(grad, home, shares)

    def finish(i):
        a = total.row(i)
        b = a // split
        value = total.take(i)
        p = px[rows((core * split + a) * (1 - b), CH)].astype(f32)
        c = cx[rows((core * c_split + a - split) * b, CH)].astype(f32)
        whitened, inverse = norm_rows(jnp.where(b == 0, p, c))
        back = norm_back(value, whitened, inverse, gains[0:1])
        extra = dh1[rows((a - split) * b, CH)]
        grad[rows(home(a), CH)] = jnp.where(b == 0, back, back + extra).astype(bf16)
        give.copy(i, a).start()
        if share:
            rest.meet(i + 1)

            @pl.when(i > 0)
            def _():
                rest.turn(i - 1)

    def part(lo, hi):
        loop(hi - lo, lambda i: finish(i + lo))

    if share:
        rest.meet(0)
    third = total.n // 3
    part(0, third)
    to_far.wait()
    stats_c[me] = stats_y[0] + stats_y[1]
    to_ctx = [
        small(stats_c.at[me], stats_c.at[me], 2 + d, device) for d, device in enumerate(ctx_peers)
    ]
    for copy in to_ctx:
        copy.start()
    if share:
        for copy in gives:
            copy.wait()
        value = gown[...]
        for d in range(n_dp - 1):
            value += grcv[d].astype(f32)
        qsh[...] = value.astype(bf16)
        tail.launch(0)
    part(third, 2 * third)
    for copy in to_ctx:
        copy.wait()
    value = stats_c[0]
    for d in range(1, n_ctx):
        value += stats_c[d]
    stats_d[dp] = value
    to_dp = [
        small(stats_d.at[dp], stats_d.at[dp], 1 + n_ctx + d, device)
        for d, device in enumerate(dp_peers)
    ]
    for copy in to_dp:
        copy.start()
    part(2 * third, total.n)
    if share:
        tail.meet(0)
        rest.turn(REST - 2)
        rest.turn(REST - 1)
        tail.turn(0)
    loop(total.n, lambda i: give.copy(i, total.row(i)).wait())
    grad_p[...] = grad[0:n_prompt]
    grad_c[...] = grad[n_prompt:n_prompt + n_cont]
    for copy in to_dp:
        copy.wait()
    value = stats_d[0]
    for d in range(1, n_dp):
        value += stats_d[d]
    fin[...] = value
    total.close()
    if share:
        loop(REST, rest.land)
        tail.land(0)
        g_rest[n_rest:n_rest + 3 * HEAD_DIM] = qsum[...]


def output_body(
    n_ctx, n_dp, share, ff,
    ids, msgs, fin, p_out, c_out, p_grad, c_grad, *refs,
):
    n = 2 if share else 0
    parts = refs[:n]
    p_out_o, c_out_o, p_grad_o, c_grad_o, loss, dwa_g, g1, b1, g2, b2 = refs[n:n + 10]
    refs = refs[n + 10:]
    if share:
        r_qkv, r_out, r_up, r_down = refs[:4]
        refs = refs[4:]
    held, sem = refs[:4], refs[4]
    moves = (
        (p_out, p_out_o), (c_out, c_out_o), (p_grad, p_grad_o), (c_grad, c_grad_o)
    )
    reads = [
        pltpu.make_async_copy(s, h, sem.at[0, i]) for i, ((s, _), h) in enumerate(zip(moves, held))
    ]
    copies = [
        pltpu.make_async_copy(h, t, sem.at[1, i]) for i, ((_, t), h) in enumerate(zip(moves, held))
    ]
    for copy in reads:
        copy.start()
    depth = g1.shape[0]
    width = fin.shape[1]
    count = msgs[0:1, 0:1]
    for j in range(1, n_ctx):
        count += msgs[8 * j:8 * j + 1, 0:1]
    factor = 1.0 / (jnp.maximum(count, 1.0) * (1.0 * width))
    sums = jnp.sum(fin[...], -1, keepdims=True) * factor
    row = lax.broadcasted_iota(jnp.int32, sums.shape, 0)

    def entry(i):
        return jnp.sum(jnp.where(row == i, sums, 0.0))

    loss[0] = entry(4)
    for k in range(4):
        value = 0.0
        for j in range(4):
            value += jnp.where(ids[j] == k, 2.0 * entry(5 + j), 0.0)
        dwa_g[k] = value
    dwa_g[4] = 2.0 * entry(9)
    for i, ref in enumerate((g1, b1, g2, b2)):
        if share:
            ref[...] = fin[i, pl.ds(pl.multiple_of(lax.axis_index("dp") * depth, 128), depth)]
        else:
            piece = jnp.zeros((1, depth), f32)
            for d in range(n_dp):
                here = fin[i:i + 1, d * depth:(d + 1) * depth]
                piece += jnp.where(lax.axis_index("dp") == d, here, 0.0)
            ref[...] = piece.reshape(depth)
    for read, copy in zip(reads, copies):
        read.wait()
        copy.start()
    if share:
        down, rest = parts
        r_down[...] = down[...].astype(f32)
        for j in range(ff // depth):
            r_up[:, j * depth:(j + 1) * depth] = rest[j * depth:(j + 1) * depth].astype(f32)
        r_out[...] = rest[ff:ff + 192].astype(f32)
        base = ff + 192
        r_qkv[1, 0:128] = rest[base:base + 128].astype(f32)
        r_qkv[2, 0:128] = rest[base + 128:base + 256].astype(f32)
        r_qkv[1, 128:192] = rest[base + 256:base + 320].astype(f32)
        r_qkv[2, 128:192] = rest[base + 320:base + 384].astype(f32)
        r_qkv[0] = rest[base + 384:base + 576].astype(f32)
    for copy in copies:
        copy.wait()


def per_device(
    n_dp, n_ctx,
    prompt_x, cont_x, prompt_hist, cont_hist, teacher, valid_mask, cont_group, layer_ids,
    dwa_weights, qkv_weight, out_weight, up_weight, down_weight,
    ln1_gain, ln1_bias, ln2_gain, ln2_bias,
):
    groups, plen, width = prompt_x.shape
    conts, clen, _ = cont_x.shape
    depth = qkv_weight.shape[0]
    n_prompt, n_cont = groups * plen, conts * clen
    n_rows = n_prompt + n_cont
    split, c_split = n_prompt // 2, n_cont // 2
    half = split + c_split
    ff = up_weight.shape[1]
    share = depth % 128 == 0
    packed = n_cont + clen
    tab_rows = plen + clen
    vmem = pltpu.VMEM

    w_t = qkv_weight.transpose(1, 2, 0)
    px = prompt_x.reshape(n_prompt, width)
    cx = cont_x.reshape(n_cont, width)
    vectors = (ln1_gain, ln1_bias, ln2_gain, ln2_bias)
    states = vmem((3 * (n_prompt // clen + conts), clen, 128), f32)
    xn1, kv, tab, w_full, wu, wd, wo, o, lse, msgs, gains, qpack = kernel_call(
        functools.partial(front_body, n_ctx, n_dp, share, plen, clen, groups, conts),
        [
            ((n_rows, width), bf16), ((n_rows, 384), bf16), ((tab_rows, 384), f32),
            ((640, width), bf16), ((width, ff), bf16), ((ff, width), bf16), ((256, width), bf16),
            ((n_rows, 256), bf16), ((8 * conts, clen), f32), ((8 * n_ctx, 128), f32),
            ((8, width), f32), ((packed, 128), bf16),
        ],
        [
            vmem((n_rows, width), bf16), vmem((n_rows, 256), bf16),
            vmem((n_ctx, n_prompt, 384), bf16), vmem((n_cont, 384), bf16),
            vmem((tab_rows, 384), f32), vmem((640, width), bf16),
            vmem((8, depth), f32), vmem((n_dp, 8, depth), f32),
            vmem((8, 128), f32), vmem((n_dp, 8, 128), f32), vmem((n_ctx, 8, 128), f32),
            states, states, states,
            vmem((1, 3, 192, depth) if share else (n_dp, 3, 192, depth), bf16),
            DMA((n_dp - 1, 7)), DMA((n_dp - 1, 7)),
            DMA((2, n_ctx)), DMA((n_ctx,)), DMA((n_ctx - 1,)), DMA((n_ctx - 1,)),
            DMA((n_dp - 1, 4)), DMA((n_dp - 1, 4)), DMA((9,)),
        ],
        0,
        [SMEM_SPEC] + [VMEM_SPEC] * 11,
        (cont_group, px, cx, w_t, *vectors, valid_mask, out_weight, up_weight, down_weight),
        "front",
        [HBM_SPEC] * 6 + [VMEM_SPEC] * 6,
    )
    if not share:
        out_w = lax.all_gather(out_weight, "dp", axis=1, tiled=True)
        wu = lax.all_gather(up_weight, "dp", axis=0, tiled=True)
        wd = lax.all_gather(down_weight, "dp", axis=1, tiled=True)
        wo = jnp.concatenate([out_w[:128], jnp.zeros((64, width), bf16), out_w[128:]], 0)

    cont_out, dm, hid, xn2, du, da, do, dh1, stat, qs = kernel_call(
        functools.partial(middle_body, n_ctx, n_prompt, clen),
        [
            ((n_cont, width), bf16), ((n_cont, width), bf16), ((n_cont, ff), bf16),
            ((n_cont, width), bf16), ((n_cont, ff), bf16), ((n_cont, width), bf16),
            ((n_cont, 256), bf16), ((c_split, width), f32), ((16, width), f32),
            ((n_ctx, packed, 128), bf16),
        ],
        [
            vmem((4, c_split, width), bf16), vmem((c_split, width), bf16),
            vmem((n_cont, ff), f32), vmem((c_split, width), f32),
            vmem((c_split, width), f32), vmem((clen, 128), f32),
            DMA((2,)), DMA((n_ctx - 1,)), DMA((n_ctx - 1,)),
        ]
        + TpSum.scratch(c_split, width) * 3
        + share_scratch(c_split) * 4,
        1,
        [SMEM_SPEC] * 2 + [VMEM_SPEC] * 9 + [HBM_SPEC] * 2,
        (
            layer_ids, dwa_weights, o, qpack, msgs, wo, wu, wd, cx, gains, valid_mask,
            cont_hist.reshape(4, n_cont, width), teacher.reshape(n_cont, width),
        ),
        "middle",
    )

    grad_rows = 2 * ff + 9 * HEAD_DIM
    outs = [((n_rows, 640), bf16), ((n_prompt, width), bf16)]
    if share:
        outs += [((ff, depth), bf16), ((grad_rows - ff, depth), bf16)]
        extra = [
            vmem((n_dp - 1, grad_rows, depth), bf16), vmem((n_dp - 1, grad_rows, depth), bf16),
            vmem((grad_rows, depth), f32), vmem((ff, depth), bf16),
            DMA((n_dp - 1, 3)), DMA((n_dp - 1, 3)),
        ] + LineSum.scratch(4, ff // 4, depth)
    else:
        outs += [
            ((ff, width), bf16), ((width, ff), bf16), ((3 * HEAD_DIM, width), bf16),
            ((384, width), bf16),
        ]
        extra = []
    acc = vmem((n_prompt, 128), f32)
    got = kernel_call(
        functools.partial(
            attend_back_body, n_ctx, n_dp, share, plen, clen, groups, conts, depth
        ),
        outs,
        [
            vmem((n_cont, ff), bf16), vmem((n_cont, width), bf16),
            vmem((n_cont, width), bf16), vmem((n_cont, ff), bf16),
            vmem((n_cont, width), bf16), vmem((256, width), bf16),
            vmem((width, ff), bf16), vmem((ff, width), bf16),
            vmem((split, width), bf16), vmem((4, split, width), bf16), DMA((11,)),
            vmem((n_ctx, packed, 128), bf16), vmem((n_ctx, 8 * conts, clen), f32),
            vmem((2 * n_ctx, packed, 128), bf16), vmem((n_prompt, 128), bf16),
            acc, acc, acc, acc, vmem((packed, 128), f32),
            DMA((n_ctx - 1, 3)), DMA((n_ctx - 1, 3)),
            vmem((n_prompt, width), bf16), vmem((split, width), f32),
            vmem((n_rows, width), bf16), vmem((n_cont, 128), f32),
        ]
        + TpSum.scratch(split, width) * 2
        + share_scratch(split) * 2
        + extra,
        2,
        [SMEM_SPEC] * 2 + [VMEM_SPEC] * 9 + [HBM_SPEC] * 11,
        (
            layer_ids, dwa_weights, msgs, qs, do, o, lse, kv, valid_mask, tab, gains,
            hid, dm, xn2, du, da, wo, wu, wd, px, prompt_hist.reshape(4, n_prompt, width), xn1,
        ),
        "attend_back",
    )
    dcat, prompt_out = got[:2]

    stat_rows = vmem((16, width), f32)
    outs = [((n_prompt, width), bf16), ((n_cont, width), bf16), ((16, width), f32)]
    args = (dcat, w_full, px, cx, gains, dh1, stat, xn1)
    specs = [VMEM_SPEC] * 7 + [HBM_SPEC]
    if share:
        args += (got[3],)
        specs += [VMEM_SPEC]
        outs += [((grad_rows - ff + 3 * HEAD_DIM, depth), bf16)]
        third = vmem((3 * HEAD_DIM, depth), bf16)
        extra = [
            vmem((n_dp - 1, 3 * HEAD_DIM, depth), bf16), vmem((3 * HEAD_DIM, depth), f32),
            vmem((n_dp - 1, 3 * HEAD_DIM, depth), bf16), DMA((n_dp - 1,)), DMA((n_dp - 1,)),
            third, third,
        ]
        extra += LineSum.scratch(REST, (grad_rows - ff) // REST, depth)
        extra += LineSum.scratch(1, 3 * HEAD_DIM, depth)
    else:
        outs += [((3 * HEAD_DIM, width), bf16)]
        extra = []
    last = kernel_call(
        functools.partial(input_grad_body, n_dp, n_ctx, share, split, c_split, depth),
        outs,
        [
            vmem((n_cont, width), bf16), DMA((1,)), vmem((n_rows, width), bf16),
            stat_rows, vmem((2, 16, width), f32), vmem((2, 16, width), f32),
            vmem((n_ctx, 16, width), f32), vmem((n_dp, 16, width), f32),
            DMA((1 + n_ctx + n_dp,)), DMA((1 + n_ctx + n_dp,)),
        ]
        + TpSum.scratch(half, width)
        + share_scratch(half)
        + extra,
        3, specs, args, "input_grad",
    )
    grad_p, grad_c, fin = last[:3]

    outs = [
        ((n_prompt, width), bf16), ((n_cont, width), bf16), ((n_prompt, width), bf16),
        ((n_cont, width), bf16), ((1,), f32), ((5,), f32),
    ] + [((depth,), f32)] * 4
    out_specs = [HBM_SPEC] * 4 + [SMEM_SPEC] * 2 + [VMEM_SPEC] * 4
    specs = [SMEM_SPEC] + [VMEM_SPEC] * 2 + [HBM_SPEC] * 4
    args = (layer_ids, msgs, fin, prompt_out, cont_out, grad_p, grad_c)
    if share:
        outs += [((3, 192, depth), f32), ((192, depth), f32), ((depth, ff), f32), ((ff, depth), f32)]
        out_specs += [VMEM_SPEC] * 4
        args += (got[2], last[3])
        specs += [VMEM_SPEC] * 2
    done = pl.pallas_call(
        functools.partial(output_body, n_ctx, n_dp, share, ff),
        out_shape=[jax.ShapeDtypeStruct(s, d) for s, d in outs],
        in_specs=specs,
        out_specs=out_specs,
        scratch_shapes=[
            vmem((n_prompt, width), bf16), vmem((n_cont, width), bf16),
            vmem((n_prompt, width), bf16), vmem((n_cont, width), bf16), DMA((2, 4)),
        ],
        compiler_params=pltpu.CompilerParams(vmem_limit_bytes=LIMIT),
        name="outputs",
    )(*args)
    if share:
        r_qkv, r_out, r_up, r_down = done[10:]
        r_qkv = r_qkv.transpose(2, 0, 1)
    else:
        def scattered(g, dim):
            part = lax.psum_scatter(g, "dp", scatter_dimension=dim, tiled=True)
            return lax.psum(part, "ctx").astype(f32)

        g_down, g_up, g_out, g_kv = got[2:]
        r_down = scattered(g_down, 1)
        r_up = scattered(g_up, 0)
        r_out = scattered(g_out, 1)
        g_k = jnp.concatenate([g_kv[0:128], g_kv[256:320]], 0)
        g_v = jnp.concatenate([g_kv[128:256], g_kv[320:384]], 0)
        r_qkv = scattered(jnp.stack([last[3], g_k, g_v]).transpose(2, 0, 1), 0)
    return (
        done[0].reshape(groups, plen, width),
        done[1].reshape(conts, clen, width),
        done[4].reshape(()),
        done[2].reshape(groups, plen, width),
        done[3].reshape(conts, clen, width),
        r_qkv, r_out, r_up, r_down,
        done[6], done[7], done[8], done[9],
        done[5],
    )


def solution(mesh):
    n_dp, n_ctx = mesh.shape["dp"], mesh.shape["ctx"]
    in_specs = (
        P("dp", "ctx", None), P(("dp", "ctx"), None, None), P(None, "dp", "ctx", None),
        P(None, ("dp", "ctx"), None, None), P(("dp", "ctx"), None, None), P(("dp", "ctx"), None),
        P(("dp", "ctx")), P(), P(), P("dp", None, "tp"), P("tp", "dp"), P("dp", "tp"),
        P("tp", "dp"), P("dp"), P("dp"), P("dp"), P("dp"),
    )
    out_specs = (
        P("dp", "ctx", None), P(("dp", "ctx"), None, None), P(), P("dp", "ctx", None),
        P(("dp", "ctx"), None, None), P("dp", None, "tp"), P("tp", "dp"), P("dp", "tp"),
        P("tp", "dp"), P("dp"), P("dp"), P("dp"), P("dp"), P(),
    )
    return jax.shard_map(
        functools.partial(per_device, n_dp, n_ctx),
        mesh=mesh, in_specs=in_specs, out_specs=out_specs, check_vma=False,
    )
```

time: 313 us -> 262 us (0.84)
  local copies, waits for them, and re-layouts: 26.7 us -> 0 us
  Pallas kernels: 274 us -> 261 us
  other arithmetic: 5.56 us -> 0 us
  between operations: 5.29 us -> 0.86 us
    pallas_call x5 -> x4, Pallas kernels: 274 us -> 254 us  [kernel_call(): pl.pallas_call(body, out_shape=[jax.ShapeDtypeStruct(s, d) for s, d in ou...]
    slice x16 -> x0, local copies, waits for them, and re-layouts: 13.3 us -> none  [the longest x1 2.48 us: per_device(): r_down = rest[:ff]]
    unnamed x29 -> x0, local copies, waits for them, and re-layouts: 7.65 us -> none
    pallas_call x0 -> x1, Pallas kernels: none -> 7 us  [per_device(): pl.pallas_call(functools.partial(output_body, n_ctx, n_dp, share, ff), ou...]
where the time goes in v2:
time: 262 us; the launch traced here: 261 us
  Pallas kernels  261 us (100%)
    pallas_call x4, Pallas kernels, kernel_call(): pl.pallas_call(body, out_shape=[jax.ShapeDtypeStruct(s, d) for s, d in ou...  254 us
    pallas_call x1, Pallas kernels, per_device(): pl.pallas_call(functools.partial(output_body, n_ctx, n_dp, share, ff), ou...  7 us

profile of v2, /device:TPU:0, one launch (start us, length us, event | category | flops | bytes accessed | tf_op | source)
XLA Modules:
  0.0 261.5 jit_solution(693690393675342752)
XLA Ops:
  0.6 73.9 %front.1 = (bf16[1536,768]{1,0:T(8,128)(2,1)}, bf16[1536,384]{1,0:T(8,128)(2,1)}, f32[768,384]{1,0:T(8,128)}, bf16[640,768]{1,0:T(8,128)(2,1)}, bf16[768,768]{1,...) custom-call(s32[2]{0:T(128)} %sel.1, ...), custom_call_target="tpu_custom_call" | custom-call | bytes 31457280 | tf_op jit(solution)/shard_map/front/pallas_call | solution.py:55
  74.6 48.0 %middle.1 = (bf16[512,768]{1,0:T(8,128)(2,1)}, bf16[512,768]{1,0:T(8,128)(2,1)}, bf16[512,768]{1,0:T(8,128)(2,1)}, bf16[512,768]{1,0:T(8,128)(2,1)}, bf16[512,76...) custom-call(s32[4]{0:T(128)} %ids.5, f32[5]{0:T(128)} %dwa.3, ...), custom_call_target="tpu_custom_call" | custom-call | bytes 31457280 | tf_op jit(solution)/shard_map/middle/pallas_call | solution.py:55
  122.6 67.6 %attend_back.1 = (bf16[1536,640]{1,0:T(8,128)(2,1)}, bf16[1024,768]{1,0:T(8,128)(2,1)}, bf16[768,384]{1,0:T(8,128)(2,1)}, bf16[1344,384]{1,0:T(8,128)(2,1)}) custom-call(s32[4]{0:T(128)} %ids.5, f32[5]{0:T(128)} %dwa.3, f32[32,128]{1,0:T(8,128)} %get-tuple-element.58.msgs, bf16[4,768,128]{2,1,0:T(8,128)(2,1)} %get-tuple-element.65.qs, ...), custom_call_target="tpu_custom_call" | custom-call | bytes 31457280 | tf_op jit(solution)/shard_map/attend_back/pallas_call | solution.py:55
  190.2 64.0 %input_grad.1 = (bf16[1024,768]{1,0:T(8,128)(2,1)}, bf16[512,768]{1,0:T(8,128)(2,1)}, f32[16,768]{1,0:T(8,128)}, bf16[1536,384]{1,0:T(8,128)(2,1)}) custom-call(bf16[1536,640]{1,0:T(8,128)(2,1)} %get-tuple-element.76.dcat, bf16[640,768]{1,0:T(8,128)(2,1)} %get-tuple-element.77.w, bf16[1024,768]{1,0:T(8,128)(2,1)} %bitcast.14, bf16[512,768]{1,0:T(8,128)(2,1)} %bitcast.17, ...), custom_call_target="tpu_custom_call" | custom-call | bytes 31457280 | tf_op jit(solution)/shard_map/input_grad/pallas_call | solution.py:55
  254.3 7.0 %outputs.1 = (bf16[1024,768]{1,0:T(8,128)(2,1)}, bf16[512,768]{1,0:T(8,128)(2,1)}, bf16[1024,768]{1,0:T(8,128)(2,1)}, bf16[512,768]{1,0:T(8,128)(2,1)}, f32[1]{0...) custom-call(s32[4]{0:T(128)} %ids.5, ...), custom_call_target="tpu_custom_call" | custom-call | tf_op jit(solution)/shard_map/outputs/pallas_call | solution.py:1609

commit v3 on v2

--- a/solution.py
+++ b/solution.py
@@ -23,8 +23,7 @@
 TN = (((0,), (0,)), ((), ()))
 CH = 128
 BIG = 256
-REST = 7
-LINE_STEP = 2
+LINE = 192
 
 
 def dot(a, b):
@@ -525,16 +524,21 @@
         self.pair(i).start()
         self.own[at] = self.compute(self.place(a, self.core), CH)
 
-    def begin(self):
+    def begin(self, held=0):
         def body(i):
             self.launch(i)
 
-            @pl.when(i > 0)
+            @pl.when((i > 0) & (i <= self.n - held))
             def _():
                 self.second(i - 1)
 
         loop(self.n, body)
-        self.second(self.n - 1)
+        if not held:
+            self.second(self.n - 1)
+
+    def resume(self, held):
+        for i in range(self.n - held, self.n):
+            self.second(i)
 
     def take(self, i):
         at = rows(self.row(i), CH)
@@ -735,14 +739,12 @@
 
 class LineSum:
     @staticmethod
-    def scratch(count, size, width):
-        return [
-            pltpu.VMEM((count, size, width), bf16), pltpu.VMEM((count, size, width), bf16),
-            pltpu.VMEM((count, size, width), bf16), DMA((2, count)), DMA((2, count)),
-        ]
-
-    def __init__(self, me, src, dst, scratch, count, size):
-        self.src, self.dst, self.count, self.size = src, dst, count, size
+    def scratch(count, width):
+        buffer = pltpu.VMEM((count, LINE, width), bf16)
+        return [buffer, buffer, buffer, DMA((2, count)), DMA((2, count))]
+
+    def __init__(self, me, src, dst, scratch, ready):
+        self.src, self.dst, self.ready = src, dst, ready
         self.got, self.pair, self.far, self.send, self.recv = scratch
         side = me // 2
         self.outer = (me == 0) | (me == 3)
@@ -752,7 +754,7 @@
         self.twin = {"ctx": 2 - side}
 
     def at(self, k):
-        return rows(k * self.size, self.size)
+        return rows(k * LINE, LINE)
 
     def up(self, k):
         return remote(
@@ -773,6 +775,12 @@
         @pl.when(self.outer)
         def _():
             self.up(k).start()
+
+    def skip(self, k):
+        @pl.when(self.inner)
+        def _():
+            self.pair[k] = self.src[self.at(k)]
+            self.cross(k).start()
 
     def meet(self, k):
         @pl.when(self.inner)
@@ -793,9 +801,12 @@
             self.dst[self.at(k)] = total
 
     def land(self, k):
+        @pl.when(self.outer & (k >= self.ready))
+        def _():
+            self.up(k).wait_send()
+
         @pl.when(self.outer)
         def _():
-            self.up(k).wait_send()
             self.down(k).wait_recv()
             self.dst[self.at(k)] = self.got[k]
 
@@ -824,8 +835,8 @@
     wo_h, wu_h, wd_h, px_h, hist_h, xn1_h, *refs,
 ):
     if share:
-        dcat, out, g_sum, g_part = refs[:4]
-        refs = refs[4:]
+        dcat, out, g_all = refs[:3]
+        refs = refs[3:]
     else:
         dcat, out, g_down, g_up, g_out, g_kv = refs[:6]
         refs = refs[6:]
@@ -906,7 +917,13 @@
     bounds = (0, ff, 2 * ff + 192, 2 * ff + 576)
     if share:
         gsnd, grcv, gown, gdn, s_g, r_g = refs[:6]
-        line = LineSum(me, gdn, g_sum, refs[6:11], 4, ff // 4)
+        got, s_l, r_l = refs[6:9]
+        outer = (me == 0) | (me == 3)
+        inner = (me == 1) | (me == 2)
+
+        def up(k):
+            at = rows(k * LINE, LINE)
+            return remote(gdn.at[at], got.at[at], s_l.at[k], r_l.at[k], {"ctx": 1 + me // 2})
 
     def cols_of(d):
         return pl.ds(pl.multiple_of(lax.rem(dp + d, n_dp) * depth, 128), depth)
@@ -1073,7 +1090,7 @@
         gdn[rows(j * 64, 64)] = value
 
     def to_part(at, j, value):
-        g_part[rows(at.start - ff, 64)] = value
+        g_all[at] = value
 
     source(me, True)
     for copy in loads[7:9]:
@@ -1094,14 +1111,14 @@
         def _():
             second.second(i)
 
-        if share:
-            @pl.when(i == LINE_STEP)
-            def _():
-                down_grads(hid, dm, cols_of(0), keeper(0))
-                settle(to_line, 0)
-                loop(4, line.launch)
-
     loop(max(half // CH, n_ctx), step)
+    if share:
+        down_grads(hid, dm, cols_of(0), keeper(0))
+        settle(to_line, 0)
+
+        @pl.when(outer)
+        def _():
+            loop(ff // LINE, lambda k: up(k).start())
 
     for c in range(conts):
         at = slice(n_prompt + c * clen, n_prompt + (c + 1) * clen)
@@ -1149,7 +1166,6 @@
             give(d, 2).start()
         other_grads(ff, xn2, du, o_c, da, cols_of(0), keeper(0))
         kv_grads(cols_of(0), keeper(0))
-        loop(4, line.meet)
         settle(to_part, 1)
     else:
         for j in range(xn1.shape[1] // 256):
@@ -1179,9 +1195,6 @@
         third = jnp.where(low, third, 0.0)
         dcat[at, 128:256] = turn(third, t, -1.0, True).astype(bf16)
 
-    if share:
-        loop(4, line.turn)
-
     loads[9].wait()
     give_out = Share(out, home, shares[2:4])
 
@@ -1196,7 +1209,20 @@
     loop(half // CH, lambda i: give_out.copy(i, second.row(i)).wait())
     if share:
         settle(to_part, 2)
-        loop(4, line.land)
+
+        @pl.when(outer)
+        def _():
+            g_all[0:ff] = gdn[...]
+            loop(ff // LINE, lambda k: up(k).wait_send())
+
+        @pl.when(inner)
+        def _():
+            def meet(k):
+                at = rows(k * LINE, LINE)
+                up(k).wait_recv()
+                g_all[at] = (gdn[at].astype(f32) + got[at].astype(f32)).astype(bf16)
+
+            loop(ff // LINE, meet)
     first.close()
     second.close()
     for copy in sends:
@@ -1204,11 +1230,11 @@
 
 
 def input_grad_body(
-    n_dp, n_ctx, share, split, c_split, depth,
+    n_dp, n_ctx, share, split, c_split, depth, ready,
     dcat, w, px, cx, gains, dh1, stat_in, xn_h, *refs,
 ):
     if share:
-        g_part, grad_p, grad_c, fin, g_rest = refs[:5]
+        g_part, grad_p, grad_c, fin, g_sum = refs[:5]
         refs = refs[5:]
     else:
         grad_p, grad_c, fin, g_q = refs[:4]
@@ -1230,11 +1256,15 @@
     stat[...] = 0.5 * stat_in[...]
     greet([mate, across] + ctx_peers + dp_peers)
     if share:
-        gsnd, gown, grcv, s_g, r_g, qsh, qsum = refs[:7]
-        n_rest = g_part.shape[0]
-        rest = LineSum(me, g_part, g_rest.at[0:n_rest], refs[7:12], REST, n_rest // REST)
-        tail = LineSum(me, qsh, qsum, refs[12:17], 1, 3 * HEAD_DIM)
-        loop(REST, rest.launch)
+        gsnd, gown, grcv, s_g, r_g, gall = refs[:6]
+        n_part = g_part.shape[0]
+        n_line = n_part // LINE
+        take_part = pltpu.make_async_copy(g_part, gall.at[0:n_part], lsem.at[1])
+        take_part.start()
+        line = LineSum(me, gall, g_sum, refs[6:11], ready)
+        take_part.wait()
+        loop(n_line - ready, lambda k: line.launch(k + ready))
+        loop(ready, line.skip)
 
     def place(a, c):
         return full_at(a, c, split, c_split)
@@ -1253,7 +1283,7 @@
         return part
 
     total = TpSum(half, split, place, s1, compute)
-    total.begin()
+    total.begin(2)
 
     def small(src, dst, i, device):
         return remote(src, dst, s_s.at[i], r_s.at[i], device)
@@ -1284,6 +1314,7 @@
     stats_y[0] = stats_m[0] + stats_m[1]
     to_far = small(stats_y.at[0], stats_y.at[1], 1, across)
     to_far.start()
+    total.resume(2)
     give = Share(grad, home, shares)
 
     def finish(i):
@@ -1298,19 +1329,25 @@
         grad[rows(home(a), CH)] = jnp.where(b == 0, back, back + extra).astype(bf16)
         give.copy(i, a).start()
         if share:
-            rest.meet(i + 1)
-
-            @pl.when(i > 0)
-            def _():
-                rest.turn(i - 1)
+            line.meet(ready + i + 1)
+            line.turn(2 * i)
+            line.turn(2 * i + 1)
 
     def part(lo, hi):
         loop(hi - lo, lambda i: finish(i + lo))
 
     if share:
-        rest.meet(0)
-    third = total.n // 3
-    part(0, third)
+        line.meet(ready)
+    part(0, 2)
+    if share:
+        for copy in gives:
+            copy.wait()
+        value = gown[...]
+        for d in range(n_dp - 1):
+            value += grcv[d].astype(f32)
+        gall[n_part:n_part + 3 * HEAD_DIM] = value.astype(bf16)
+        line.launch(n_line)
+    part(2, 4)
     to_far.wait()
     stats_c[me] = stats_y[0] + stats_y[1]
     to_ctx = [
@@ -1318,15 +1355,10 @@
     ]
     for copy in to_ctx:
         copy.start()
-    if share:
-        for copy in gives:
-            copy.wait()
-        value = gown[...]
-        for d in range(n_dp - 1):
-            value += grcv[d].astype(f32)
-        qsh[...] = value.astype(bf16)
-        tail.launch(0)
-    part(third, 2 * third)
+    part(4, 5)
+    if share:
+        line.meet(n_line)
+    part(5, 6)
     for copy in to_ctx:
         copy.wait()
     value = stats_c[0]
@@ -1339,12 +1371,6 @@
     ]
     for copy in to_dp:
         copy.start()
-    part(2 * third, total.n)
-    if share:
-        tail.meet(0)
-        rest.turn(REST - 2)
-        rest.turn(REST - 1)
-        tail.turn(0)
     loop(total.n, lambda i: give.copy(i, total.row(i)).wait())
     grad_p[...] = grad[0:n_prompt]
     grad_c[...] = grad[n_prompt:n_prompt + n_cont]
@@ -1356,16 +1382,14 @@
     fin[...] = value
     total.close()
     if share:
-        loop(REST, rest.land)
-        tail.land(0)
-        g_rest[n_rest:n_rest + 3 * HEAD_DIM] = qsum[...]
+        loop(n_line + 1, line.land)
 
 
 def output_body(
     n_ctx, n_dp, share, ff,
     ids, msgs, fin, p_out, c_out, p_grad, c_grad, *refs,
 ):
-    n = 2 if share else 0
+    n = 1 if share else 0
     parts = refs[:n]
     p_out_o, c_out_o, p_grad_o, c_grad_o, loss, dwa_g, g1, b1, g2, b2 = refs[n:n + 10]
     refs = refs[n + 10:]
@@ -1416,8 +1440,8 @@
         read.wait()
         copy.start()
     if share:
-        down, rest = parts
-        r_down[...] = down[...].astype(f32)
+        rest = parts[0].at[ff:]
+        r_down[...] = parts[0][0:ff].astype(f32)
         for j in range(ff // depth):
             r_up[:, j * depth:(j + 1) * depth] = rest[j * depth:(j + 1) * depth].astype(f32)
         r_out[...] = rest[ff:ff + 192].astype(f32)
@@ -1515,12 +1539,13 @@
     grad_rows = 2 * ff + 9 * HEAD_DIM
     outs = [((n_rows, 640), bf16), ((n_prompt, width), bf16)]
     if share:
-        outs += [((ff, depth), bf16), ((grad_rows - ff, depth), bf16)]
+        outs += [((grad_rows, depth), bf16)]
         extra = [
             vmem((n_dp - 1, grad_rows, depth), bf16), vmem((n_dp - 1, grad_rows, depth), bf16),
             vmem((grad_rows, depth), f32), vmem((ff, depth), bf16),
             DMA((n_dp - 1, 3)), DMA((n_dp - 1, 3)),
-        ] + LineSum.scratch(4, ff // 4, depth)
+            vmem((ff, depth), bf16), DMA((ff // LINE,)), DMA((ff // LINE,)),
+        ]
     else:
         outs += [
             ((ff, width), bf16), ((width, ff), bf16), ((3 * HEAD_DIM, width), bf16),
@@ -1564,25 +1589,24 @@
     args = (dcat, w_full, px, cx, gains, dh1, stat, xn1)
     specs = [VMEM_SPEC] * 7 + [HBM_SPEC]
     if share:
-        args += (got[3],)
-        specs += [VMEM_SPEC]
-        outs += [((grad_rows - ff + 3 * HEAD_DIM, depth), bf16)]
-        third = vmem((3 * HEAD_DIM, depth), bf16)
+        args += (got[2],)
+        specs += [HBM_SPEC]
+        outs += [((grad_rows + LINE, depth), bf16)]
         extra = [
             vmem((n_dp - 1, 3 * HEAD_DIM, depth), bf16), vmem((3 * HEAD_DIM, depth), f32),
             vmem((n_dp - 1, 3 * HEAD_DIM, depth), bf16), DMA((n_dp - 1,)), DMA((n_dp - 1,)),
-            third, third,
-        ]
-        extra += LineSum.scratch(REST, (grad_rows - ff) // REST, depth)
-        extra += LineSum.scratch(1, 3 * HEAD_DIM, depth)
+            vmem((grad_rows + LINE, depth), bf16),
+        ] + LineSum.scratch(grad_rows // LINE + 1, depth)
     else:
         outs += [((3 * HEAD_DIM, width), bf16)]
         extra = []
     last = kernel_call(
-        functools.partial(input_grad_body, n_dp, n_ctx, share, split, c_split, depth),
+        functools.partial(
+            input_grad_body, n_dp, n_ctx, share, split, c_split, depth, ff // LINE
+        ),
         outs,
         [
-            vmem((n_cont, width), bf16), DMA((1,)), vmem((n_rows, width), bf16),
+            vmem((n_cont, width), bf16), DMA((2,)), vmem((n_rows, width), bf16),
             stat_rows, vmem((2, 16, width), f32), vmem((2, 16, width), f32),
             vmem((n_ctx, 16, width), f32), vmem((n_dp, 16, width), f32),
             DMA((1 + n_ctx + n_dp,)), DMA((1 + n_ctx + n_dp,)),
@@ -1604,8 +1628,8 @@
     if share:
         outs += [((3, 192, depth), f32), ((192, depth), f32), ((depth, ff), f32), ((ff, depth), f32)]
         out_specs += [VMEM_SPEC] * 4
-        args += (got[2], last[3])
-        specs += [VMEM_SPEC] * 2
+        args += (last[3],)
+        specs += [VMEM_SPEC]
     done = pl.pallas_call(
         functools.partial(output_body, n_ctx, n_dp, share, ff),
         out_shape=[jax.ShapeDtypeStruct(s, d) for s, d in outs],

time: 262 us -> 245 us (0.935)
  Pallas kernels: 261 us -> 243 us
    pallas_call x4, Pallas kernels: 254 us -> 236 us  [kernel_call(): pl.pallas_call(body, out_shape=[jax.ShapeDtypeStruct(s, d) for s, d in ou...]
where the time goes in v3:
time: 245 us; the launch traced here: 244 us
  Pallas kernels  243 us (99%)
    pallas_call x4, Pallas kernels, kernel_call(): pl.pallas_call(body, out_shape=[jax.ShapeDtypeStruct(s, d) for s, d in ou...  236 us
    pallas_call x1, Pallas kernels, per_device(): pl.pallas_call(functools.partial(output_body, n_ctx, n_dp, share, ff), ou...  7.01 us

profile of v3, /device:TPU:0, one launch (start us, length us, event | category | flops | bytes accessed | tf_op | source)
XLA Modules:
  0.0 244.3 jit_solution(1226806718154133522)
XLA Ops:
  0.6 74.0 %front.1 = (bf16[1536,768]{1,0:T(8,128)(2,1)}, bf16[1536,384]{1,0:T(8,128)(2,1)}, f32[768,384]{1,0:T(8,128)}, bf16[640,768]{1,0:T(8,128)(2,1)}, bf16[768,768]{1,...) custom-call(s32[2]{0:T(128)} %sel.1, ...), custom_call_target="tpu_custom_call" | custom-call | bytes 31457280 | tf_op jit(solution)/shard_map/front/pallas_call | solution.py:54
  74.6 48.0 %middle.1 = (bf16[512,768]{1,0:T(8,128)(2,1)}, bf16[512,768]{1,0:T(8,128)(2,1)}, bf16[512,768]{1,0:T(8,128)(2,1)}, bf16[512,768]{1,0:T(8,128)(2,1)}, bf16[512,76...) custom-call(s32[4]{0:T(128)} %ids.5, f32[5]{0:T(128)} %dwa.3, ...), custom_call_target="tpu_custom_call" | custom-call | bytes 31457280 | tf_op jit(solution)/shard_map/middle/pallas_call | solution.py:54
  122.6 52.7 %attend_back.1 = (bf16[1536,640]{1,0:T(8,128)(2,1)}, bf16[1024,768]{1,0:T(8,128)(2,1)}, bf16[2112,384]{1,0:T(8,128)(2,1)}) custom-call(s32[4]{0:T(128)} %ids.5, f32[5]{0:T(128)} %dwa.3, f32[32,128]{1,0:T(8,128)} %get-tuple-element.57.msgs, bf16[4,768,128]{2,1,0:T(8,128)(2,1)} %get-tuple-element.64.qs, bf16[512,256]{1,0:T(8,128)(2,1)} %get-tuple-element.65.do, ...), custom_call_target="tpu_custom_call" | custom-call | bytes 31457280 | tf_op jit(solution)/shard_map/attend_back/pallas_call | solution.py:54
  175.3 61.8 %input_grad.1 = (bf16[1024,768]{1,0:T(8,128)(2,1)}, bf16[512,768]{1,0:T(8,128)(2,1)}, f32[16,768]{1,0:T(8,128)}, bf16[2304,384]{1,0:T(8,128)(2,1)}) custom-call(bf16[1536,640]{1,0:T(8,128)(2,1)} %get-tuple-element.75.dcat, bf16[640,768]{1,0:T(8,128)(2,1)} %get-tuple-element.76.w, bf16[1024,768]{1,0:T(8,128)(2,1)} %bitcast.14, bf16[512,768]{1,0:T(8,128)(2,1)} %bitcast.17, ...), custom_call_target="tpu_custom_call" | custom-call | bytes 31457280 | tf_op jit(solution)/shard_map/input_grad/pallas_call | solution.py:54
  237.1 7.0 %outputs.1 = (bf16[1024,768]{1,0:T(8,128)(2,1)}, bf16[512,768]{1,0:T(8,128)(2,1)}, bf16[1024,768]{1,0:T(8,128)(2,1)}, bf16[512,768]{1,0:T(8,128)(2,1)}, f32[1]{0...) custom-call(s32[4]{0:T(128)} %ids.5, ...), custom_call_target="tpu_custom_call" | custom-call | tf_op jit(solution)/shard_map/outputs/pallas_call | solution.py:1633

commit v4 on v3

--- a/solution.py
+++ b/solution.py
@@ -18,12 +18,13 @@
 SMEM_SPEC = pl.BlockSpec(memory_space=pltpu.SMEM)
 HBM_SPEC = pl.BlockSpec(memory_space=pl.ANY)
 DMA = pltpu.SemaphoreType.DMA
-LIMIT = 56 << 20
+LIMIT = 62 << 20
 NT = (((1,), (1,)), ((), ()))
 TN = (((0,), (0,)), ((), ()))
 CH = 128
 BIG = 256
 LINE = 192
+EARLY = 2 * LINE
 
 
 def dot(a, b):
@@ -83,9 +84,24 @@
     )
 
 
+def fetch(pairs, sems):
+    copies = [pltpu.make_async_copy(s, d, sems.at[i]) for i, (s, d) in enumerate(pairs)]
+    for copy in copies:
+        copy.start()
+    return copies
+
+
+def like(*arrays):
+    return [pltpu.VMEM(a.shape, a.dtype) for a in arrays]
+
+
 def axis_peers(axis, count):
     me = lax.axis_index(axis)
     return [{axis: lax.rem(me + d, count)} for d in range(1, count)]
+
+
+def me_of(axis):
+    return lax.axis_index(axis)
 
 
 def tp_place():
@@ -128,11 +144,15 @@
 
 def front_body(
     n_ctx, n_dp, share, plen, clen, groups, conts,
-    sel, px, cx, w, g1, b1, g2, b2, valid, wo, wu, wd,
+    sel, px_h, cx_h, w_h, g1, b1, g2, b2, valid, wo_h, wu_h, wd_h,
     xn_o, kv_o, tab_o, w_o, wu_o, wd_o, wo_o, o, lse, msgs, gains, qpack,
     xn, q, kvs, kvc, tab, w_full, gb, gbs, cnt, cnts, notes, m_s, l_s, acc_s,
     wgs, s_x, r_x, s_kv, r_kv, s_c, r_c, s_w, r_w, osem,
+    w, px, cx, wo, wu, wd, lsem,
 ):
+    loads = fetch(
+        ((w_h, w), (px_h, px), (cx_h, cx), (wo_h, wo), (wu_h, wu), (wd_h, wd)), lsem
+    )
     me = lax.axis_index("ctx")
     mine = lax.axis_index("dp")
     depth = w.shape[2]
@@ -148,6 +168,7 @@
     gb[4:8] = jnp.zeros((4, depth), f32)
     cnt[...] = jnp.zeros(cnt.shape, f32) + jnp.sum(valid[...].astype(f32))
     greet(dp_peers + peers)
+    loads[0].wait()
 
     copies = []
     weights = []
@@ -170,6 +191,13 @@
             group[i].start()
     local = []
     if share:
+        for p, a, n, t in W_PARTS:
+            w_full[t:t + n, cols] = w[p, a:a + n]
+    else:
+        wgs[mine] = w[...]
+    for copy in loads[1:]:
+        copy.wait()
+    if share:
         pairs = [
             (wo.at[0:128], wo_o.at[0:128, cols]), (wo.at[128:192], wo_o.at[192:256, cols]),
             (wu, wu_o.at[here]), (wd, wd_o.at[:, cols]),
@@ -179,13 +207,7 @@
                 weights.append(remote(s, t, s_w.at[d, i], r_w.at[d, i], device))
         for copy in weights:
             copy.start()
-        local += [pltpu.make_async_copy(s, t, osem.at[i]) for i, (s, t) in enumerate(pairs)]
-        for copy in local:
-            copy.start()
-        for p, a, n, t in W_PARTS:
-            w_full[t:t + n, cols] = w[p, a:a + n]
-    else:
-        wgs[mine] = w[...]
+        local += fetch(pairs, osem)
     wo_o[128:192] = jnp.zeros((64, width), bf16)
     w_full[192:256] = jnp.zeros((64, width), bf16)
     gbs[mine] = gb[...]
@@ -263,13 +285,13 @@
                     part += dot(wgs[d, p, a:a + n], one_hot(d))
                 w_full[t:t + n] = part.astype(bf16)
 
-    def hop(slot, step, side):
-        there = kvs.at[slot]
-        return remote(there, there, s_kv.at[side, slot], r_kv.at[slot], {"ctx": me + step})
-
-    def kv_rows(count, base, tab_base, period, dst):
+    def hop(slot, g, step, side):
+        there = kvs.at[slot, rows(g * plen, plen)]
+        return remote(there, there, s_kv.at[side, slot, g], r_kv.at[slot, g], {"ctx": me + step})
+
+    def kv_rows(count, base, tab_base, period, dst, first):
         def body(i):
-            at = rows(i * BIG, BIG)
+            at = rows(first + i * BIG, BIG)
             t = tab[rows(tab_base + lax.rem(i * BIG, period), BIG)]
             x = xn[rows(base + i * BIG, BIG)]
             y = dot_nt(x, w_full[256:512])
@@ -291,18 +313,21 @@
 
     for i in range(4):
         arrive(i)
-    kv_rows(n_prompt, 0, 0, plen, kvs.at[me])
-
-    @pl.when(me < last)
-    def _():
-        hop(me, 1, 0).start()
-
-    @pl.when(me > 0)
-    def _():
-        hop(me, -1, 1).start()
-
+
+    def send_own(g):
+        kv_rows(plen, g * plen, 0, plen, kvs.at[me], g * plen)
+
+        @pl.when(me < last)
+        def _():
+            hop(me, g, 1, 0).start()
+
+        @pl.when(me > 0)
+        def _():
+            hop(me, g, -1, 1).start()
+
+    loop(groups, send_own)
     save(kvs.at[me], kv_o.at[0:n_prompt], 6)
-    kv_rows(n_cont, n_prompt, plen, clen, kvc)
+    kv_rows(n_cont, n_prompt, plen, clen, kvc, 0)
     save(kvc, kv_o.at[n_prompt:n_prompt + n_cont], 7)
     arrive(4)
     save(w_full, w_o, 8)
@@ -346,10 +371,9 @@
 
     tiles = plen // tile
 
-    def prompt_part(slot, diagonal):
-        def body(i):
-            group = i // tiles
-            t = lax.rem(i, tiles)
+    def prompt_part(slot, group, diagonal):
+        def body(t):
+            i = group * tiles + t
             at = rows(group * plen, plen)
             mask = None
             if diagonal:
@@ -363,7 +387,7 @@
                 mask, diagonal,
             )
 
-        loop(groups * tiles, body)
+        loop(tiles, body)
 
     def cont_part(slot, first):
         def body(i):
@@ -395,7 +419,7 @@
         loop(conts, body)
 
     cont_part(me, True)
-    prompt_part(me, True)
+    loop(groups, lambda g: prompt_part(me, g, True))
     self_part()
     e0 = q[n_prompt:n_prompt + clen, 128:256].astype(f32)
     e1 = q[n_prompt + clen:n_prompt + n_cont, 128:256].astype(f32)
@@ -405,26 +429,32 @@
     def ring(e):
         d = e + 1
 
-        @pl.when(me - d >= 0)
-        def _():
-            hop(me - d, 1, 0).wait_recv()
-
-            @pl.when(me < last)
+        def group(g):
+            @pl.when(me - d >= 0)
             def _():
-                hop(me - d, 1, 0).start()
-
-        @pl.when(me + d <= last)
-        def _():
-            hop(me + d, -1, 1).wait_recv()
-
-            @pl.when(me > 0)
+                hop(me - d, g, 1, 0).wait_recv()
+
+                @pl.when(me < last)
+                def _():
+                    hop(me - d, g, 1, 0).start()
+
+            @pl.when(me + d <= last)
             def _():
-                hop(me + d, -1, 1).start()
+                hop(me + d, g, -1, 1).wait_recv()
+
+                @pl.when(me > 0)
+                def _():
+                    hop(me + d, g, -1, 1).start()
+
+            @pl.when(me - d >= 0)
+            def _():
+                prompt_part(me - d, g, False)
+
+        loop(groups, group)
 
         @pl.when(me - d >= 0)
         def _():
             cont_part(me - d, False)
-            prompt_part(me - d, False)
 
         @pl.when(me + d <= last)
         def _():
@@ -458,13 +488,14 @@
             lse[8 * i + h:8 * i + h + 1] = jnp.transpose(value)[0:1]
 
     for slot in range(n_ctx):
-        @pl.when((slot <= me) & (me < last))
-        def _():
-            hop(slot, 1, 0).wait_send()
-
-        @pl.when((slot >= me) & (me > 0))
-        def _():
-            hop(slot, -1, 1).wait_send()
+        for g in range(groups):
+            @pl.when((slot <= me) & (me < last))
+            def _():
+                hop(slot, g, 1, 0).wait_send()
+
+            @pl.when((slot >= me) & (me > 0))
+            def _():
+                hop(slot, g, -1, 1).wait_send()
 
     for group in copies:
         for copy in group:
@@ -513,7 +544,7 @@
 
     def second(self, i):
         at = rows(self.row(i), CH)
-        self.pair(i).wait_recv()
+        self.pair(i).wait()
         self.snd2[at] = (self.own[at] + self.rcv1[at].astype(f32)).astype(bf16)
         self.link(i).start()
 
@@ -542,16 +573,8 @@
 
     def take(self, i):
         at = rows(self.row(i), CH)
-        self.link(i).wait_recv()
+        self.link(i).wait()
         return self.snd2[at].astype(f32) + self.rcv2[at].astype(f32)
-
-    def close(self):
-        def body(i):
-            self.pair(i).wait_send()
-            self.link(i).wait_send()
-
-        loop(self.n, body)
-
 
 class Share:
     def __init__(self, ref, place, sems):
@@ -586,30 +609,52 @@
     return jnp.transpose(jnp.broadcast_to(row, (128, row.shape[1])))
 
 
+def down_grads(hid, dm, cols, lo, hi, store):
+    for j in range(lo, hi, 128):
+        store(j, dot_tn(hid[:, j:j + 128], dm[:, cols]))
+
+
+def other_grads(ff, xn, du, o, da, cols, store):
+    size = cols.size
+    for j in range(ff // size):
+        store(j * size, dot_tn(xn[:, cols], du[:, size * j:size * j + size]))
+    g = dot_tn(o[...], da[:, cols])
+    store(ff, g[0:128])
+    store(ff + 128, g[192:256])
+
+
 def middle_body(
-    n_ctx, n_prompt, clen,
-    ids, dwa, o, qpack, msgs, wo, wu, wd, cx, gains, valid, hist, teach,
-    out, dm, hid, xn, du, da, do, dh1, stat, qs,
-    hc, tc, slope, h1, dy, mask, hsem, s_q, r_q, *scratch,
+    n_ctx, n_dp, share, n_prompt, clen, depth,
+    ids, dwa, o_h, qpack, msgs, wo_h, wu_h, wd_h, cx_h, gains, valid, hist, teach, *refs,
 ):
+    if share:
+        gdn = refs[0]
+        refs = refs[1:]
+    out, dm, hid, xn, du, da, do, dh1, stat, qs = refs[:10]
+    hc, tc, slope, h1, dy, mask, hsem, s_q, r_q, o, wo, cx, wu, wd = refs[10:24]
+    scratch = refs[24:]
     core, mate, across = tp_place()
     ctx = lax.axis_index("ctx")
+    dp = lax.axis_index("dp")
     half = clen
     n_cont = 2 * half
     mine = rows(core * half, half)
-    loads = [
-        pltpu.make_async_copy(hist.at[:, mine], hc, hsem.at[0]),
-        pltpu.make_async_copy(teach.at[mine], tc, hsem.at[1]),
-    ]
-    for copy in loads:
-        copy.start()
+    loads = fetch(
+        (
+            (o_h.at[n_prompt:n_prompt + n_cont], o), (wo_h, wo), (cx_h.at[mine], cx),
+            (wu_h, wu), (wd_h, wd), (hist.at[:, mine], hc), (teach.at[mine], tc),
+        ),
+        hsem,
+    )
     qs[ctx] = qpack[...]
     mask[...] = column(valid[pl.ds(core, 1)].astype(f32))
     stat[...] = jnp.zeros(stat.shape, f32)
     others = axis_peers("ctx", n_ctx)
-    greet([mate, across] + others)
+    greet([mate, across] + others + (axis_peers("dp", n_dp) if share else []))
+    for copy in loads[:3]:
+        copy.wait()
     s1, s2, s3 = scratch[0:7], scratch[7:14], scratch[14:21]
-    shares = scratch[21:]
+    shares = scratch[21:29]
 
     def place(a, c):
         return a + c * half
@@ -621,7 +666,7 @@
         loop(half // CH, body)
 
     def attn(at, size):
-        return dot(o[rows(n_prompt + at, size)], wo[...])
+        return dot(o[rows(at, size)], wo[...])
 
     first = TpSum(half, 0, place, s1, attn)
     each(first.launch)
@@ -636,7 +681,7 @@
 
     def normed(i):
         a = first.row(i)
-        h = cx[rows(home(a), CH)].astype(f32) + first.take(i)
+        h = cx[rows(a, CH)].astype(f32) + first.take(i)
         h1[rows(a, CH)] = h
         whitened, _ = norm_rows(h)
         xn[rows(home(a), CH)] = (whitened * gains[2:3] + gains[3:4]).astype(bf16)
@@ -669,15 +714,15 @@
         each(body)
         after.second(after.n - 1)
 
+    for copy in loads[3:]:
+        copy.wait()
     onward(normed, give_xn, second)
-    for copy in loads:
-        copy.wait()
     give_dm = Share(dm, home, shares[2:4])
     give_out = Share(out, home, shares[4:6])
     count = msgs[0:1]
     for j in range(1, n_ctx):
         count += msgs[8 * j:8 * j + 1]
-    coef = (2.0 * dwa[4]) / (jnp.maximum(count, 1.0) * (1.0 * cx.shape[1]))
+    coef = (2.0 * dwa[4]) / (jnp.maximum(count, 1.0) * (1.0 * xn.shape[1]))
 
     def add(row, value):
         stat[row:row + 1] += jnp.sum(value, 0, keepdims=True)
@@ -708,6 +753,25 @@
 
     third = TpSum(half, 0, place, s3, back)
     onward(lossy, give_dm, third)
+    if share:
+        gsnd, grcv, gown, s_g, r_g = scratch[29:34]
+        gives = []
+        for d in range(1, n_dp):
+            def lay(at, value, d=d):
+                gsnd[d - 1, at:at + value.shape[0]] = value.astype(bf16)
+
+            other = lax.rem(dp + d, n_dp)
+            down_grads(hid, dm, pl.ds(pl.multiple_of(other * depth, 128), depth), 0, EARLY, lay)
+            copy = remote(
+                gsnd.at[d - 1], grcv.at[d - 1], s_g.at[d - 1], r_g.at[d - 1], {"dp": other}
+            )
+            copy.start()
+            gives.append(copy)
+
+        def stay(at, value):
+            gown[at:at + value.shape[0]] = value
+
+        down_grads(hid, dm, pl.ds(pl.multiple_of(dp * depth, 128), depth), 0, EARLY, stay)
     give_da = Share(da, home, shares[6:8])
 
     def grads(i):
@@ -731,10 +795,20 @@
 
     loop(n_cont // BIG, last)
     each(lambda i: give_out.copy(i, second.row(i)).wait())
-    for part in (first, second, third):
-        part.close()
     for copy in moves:
         copy.wait()
+    if share:
+        for copy in gives:
+            copy.wait()
+
+        def settle(i):
+            at = rows(i * 64, 64)
+            total = gown[at]
+            for d in range(n_dp - 1):
+                total += grcv[d, at].astype(f32)
+            gdn[at] = total.astype(bf16)
+
+        loop(gdn.shape[0] // 64, settle)
 
 
 class LineSum:
@@ -743,8 +817,8 @@
         buffer = pltpu.VMEM((count, LINE, width), bf16)
         return [buffer, buffer, buffer, DMA((2, count)), DMA((2, count))]
 
-    def __init__(self, me, src, dst, scratch, ready):
-        self.src, self.dst, self.ready = src, dst, ready
+    def __init__(self, me, src, dst, scratch):
+        self.src, self.dst = src, dst
         self.got, self.pair, self.far, self.send, self.recv = scratch
         side = me // 2
         self.outer = (me == 0) | (me == 3)
@@ -775,12 +849,6 @@
         @pl.when(self.outer)
         def _():
             self.up(k).start()
-
-    def skip(self, k):
-        @pl.when(self.inner)
-        def _():
-            self.pair[k] = self.src[self.at(k)]
-            self.cross(k).start()
 
     def meet(self, k):
         @pl.when(self.inner)
@@ -801,12 +869,9 @@
             self.dst[self.at(k)] = total
 
     def land(self, k):
-        @pl.when(self.outer & (k >= self.ready))
+        @pl.when(self.outer)
         def _():
             self.up(k).wait_send()
-
-        @pl.when(self.outer)
-        def _():
             self.down(k).wait_recv()
             self.dst[self.at(k)] = self.got[k]
 
@@ -815,39 +880,184 @@
             self.down(k).wait_send()
 
 
-def down_grads(hid, dm, cols, store):
-    for j in range(hid.shape[1] // 256):
-        store(j * 256, dot_tn(hid[:, 256 * j:256 * j + 256], dm[:, cols]))
-
-
-def other_grads(ff, xn, du, o, da, cols, store):
-    size = cols.size
-    for j in range(ff // size):
-        store(ff + j * size, dot_tn(xn[:, cols], du[:, size * j:size * j + size]))
-    g = dot_tn(o[...], da[:, cols])
-    store(ff + ff, g[0:128])
-    store(ff + ff + 128, g[192:256])
+def input_grad_tail(
+    n_dp, n_ctx, share, split, c_split, depth,
+    dcat, w, px, cx, gains, dh1, stat_in, xn1, grad_p, grad_c, fin,
+    smalls, sums, shares, prompts_out, *q_state,
+):
+    grad, stat, stats_m, stats_y, stats_c, stats_d, s_s, r_s, osem = smalls
+    core, mate, across = tp_place()
+    me = lax.axis_index("ctx")
+    dp = lax.axis_index("dp")
+    ctx_peers = axis_peers("ctx", n_ctx)
+    dp_peers = axis_peers("dp", n_dp)
+    half = split + c_split
+    n_prompt = 2 * split
+    n_cont = 2 * c_split
+    if share:
+        qsnd, qrcv, s_q, r_q, gall, line, settle_kv, n_late = q_state
+        n_line = gall.shape[0] // LINE - 1
+    else:
+        (g_q,) = q_state
+
+    def q_grads(cols):
+        part = dot_tn(dcat[n_prompt:n_prompt + n_cont, 0:256], xn1[n_prompt:n_prompt + n_cont, cols])
+        return part[0:3 * HEAD_DIM]
+
+    gives = []
+    if share:
+        for d in range(1, n_dp):
+            other = lax.rem(dp + d, n_dp)
+            cols = pl.ds(pl.multiple_of(other * depth, 128), depth)
+            qsnd[d - 1] = q_grads(cols).astype(bf16)
+            copy = remote(
+                qsnd.at[d - 1], qrcv.at[d - 1], s_q.at[d - 1], r_q.at[d - 1], {"dp": other}
+            )
+            copy.start()
+            gives.append(copy)
+
+    stat[...] = 0.5 * stat_in[...]
+
+    def place(a, c):
+        return full_at(a, c, split, c_split)
+
+    def home(a):
+        return full_at(a, core, split, c_split)
+
+    def compute(at, size):
+        part = dot(dcat[rows(at, size)], w[...])
+        b = at // n_prompt
+        p = px[rows(at * (1 - b), size)].astype(f32)
+        c = cx[rows((at - n_prompt) * b, size)].astype(f32)
+        whitened, _ = norm_rows(jnp.where(b == 0, p, c))
+        stat[0:1] += jnp.sum(part * whitened, 0, keepdims=True)
+        stat[1:2] += jnp.sum(part, 0, keepdims=True)
+        return part
+
+    total = TpSum(half, split, place, sums, compute)
+    total.begin(2)
+
+    def small(src, dst, i, device):
+        return remote(src, dst, s_s.at[i], r_s.at[i], device)
+
+    stats_m[0] = stat[...]
+    to_mate = small(stats_m.at[0], stats_m.at[1], 0, mate)
+    to_mate.start()
+    if share:
+        settle_kv()
+        loop(n_line - n_late, lambda k: line.launch(k + n_late))
+    else:
+        g_q[...] = q_grads(slice(None)).astype(bf16)
+    to_mate.wait()
+    stats_y[0] = stats_m[0] + stats_m[1]
+    to_far = small(stats_y.at[0], stats_y.at[1], 1, across)
+    to_far.start()
+    total.resume(2)
+    if share:
+        for k in range(2, 5):
+            line.meet(k)
+        for copy in gives:
+            copy.wait()
+        value = q_grads(pl.ds(pl.multiple_of(dp * depth, 128), depth))
+        for d in range(n_dp - 1):
+            value += qrcv[d].astype(f32)
+        gall[n_line * LINE:n_line * LINE + 3 * HEAD_DIM] = value.astype(bf16)
+        line.launch(n_line)
+    prompts_out()
+    give = Share(grad, home, shares)
+
+    def finish(i):
+        a = total.row(i)
+        b = a // split
+        value = total.take(i)
+        p = px[rows((core * split + a) * (1 - b), CH)].astype(f32)
+        c = cx[rows((core * c_split + a - split) * b, CH)].astype(f32)
+        whitened, inverse = norm_rows(jnp.where(b == 0, p, c))
+        back = norm_back(value, whitened, inverse, gains[0:1])
+        extra = dh1[rows((a - split) * b, CH)]
+        grad[rows(home(a), CH)] = jnp.where(b == 0, back, back + extra).astype(bf16)
+        give.copy(i, a).start()
+        if share:
+            k = i + i // 3
+            line.turn(k)
+            line.meet(5 + i)
+
+            @pl.when(lax.rem(i, 3) == 2)
+            def _():
+                line.turn(k + 1)
+
+    def part(lo, hi):
+        loop(hi - lo, lambda i: finish(i + lo))
+
+    part(0, 4)
+    to_far.wait()
+    stats_c[me] = stats_y[0] + stats_y[1]
+    to_ctx = [
+        small(stats_c.at[me], stats_c.at[me], 2 + d, device) for d, device in enumerate(ctx_peers)
+    ]
+    for copy in to_ctx:
+        copy.start()
+    part(4, 6)
+    if share:
+        line.meet(n_line)
+        line.turn(8)
+    for copy in to_ctx:
+        copy.wait()
+    value = stats_c[0]
+    for d in range(1, n_ctx):
+        value += stats_c[d]
+    stats_d[dp] = value
+    to_dp = [
+        small(stats_d.at[dp], stats_d.at[dp], 1 + n_ctx + d, device)
+        for d, device in enumerate(dp_peers)
+    ]
+    for copy in to_dp:
+        copy.start()
+    if share:
+        for k in range(9, n_line + 1):
+            line.turn(k)
+    loop(total.n, lambda i: give.copy(i, total.row(i)).wait())
+    saves = fetch(
+        ((grad.at[0:n_prompt], grad_p), (grad.at[n_prompt:n_prompt + n_cont], grad_c)), osem
+    )
+    for copy in to_dp:
+        copy.wait()
+    value = stats_d[0]
+    for d in range(1, n_dp):
+        value += stats_d[d]
+    fin[...] = value
+    if share:
+        loop(n_line + 1, line.land)
+    for copy in saves:
+        copy.wait()
 
 
 def attend_back_body(
     n_ctx, n_dp, share, plen, clen, groups, conts, depth,
-    ids, dwa, msgs, qs, do, o, lse, kv, valid, tab, gains, hid_h, dm_h, xn2_h, du_h, da_h,
-    wo_h, wu_h, wd_h, px_h, hist_h, xn1_h, *refs,
+    ids, dwa, msgs, do_h, o_h, lse, valid, gains, kv_h, tab_h, qs_h, hid_h, dm_h, xn2_h, du_h, da_h,
+    wo_h, wu_h, wd_h, px_h, hist_h, xn1_h, w_h, cx_h, dh1_h, stat_in, *refs,
 ):
     if share:
-        dcat, out, g_all = refs[:3]
-        refs = refs[3:]
+        g_first, out, grad_p, grad_c, fin, g_sum = refs[:6]
+        refs = refs[6:]
     else:
-        dcat, out, g_down, g_up, g_out, g_kv = refs[:6]
-        refs = refs[6:]
+        out, grad_p, grad_c, fin, g_down, g_up, g_out, g_kv, g_q = refs[:9]
+        refs = refs[9:]
     (
         hid, dm, xn2, du, da, wo, wu, wd, px, hist, lsem,
         dos, sts, dqs, kd, acc_k, acc_v, acc_kd, acc_vd, dq_f, send, recv,
-        xp, h1, xn1, flags,
-    ) = refs[:26]
-    s1, s2 = refs[26:33], refs[33:40]
-    shares = refs[40:44]
-    refs = refs[44:]
+        xp, h1, xn1, flags, do, o, kv, tab, qs, w, cx, dh1, dcat,
+    ) = refs[:35]
+    snd1, own = refs[35:37]
+    s1 = (snd1, refs[37], refs[39], refs[38], own, *refs[40:42])
+    s2 = (snd1, refs[42], refs[39], refs[43], own, *refs[44:46])
+    s3 = (snd1, refs[46], refs[47], refs[48], own, *refs[49:51])
+    shares = refs[51:57]
+    smalls = refs[57:66]
+    refs = refs[66:]
+    if share:
+        gsnd, grcv, s_g, r_g, qsnd, qrcv, s_q, r_q, gall = refs[:9]
+        line = LineSum(me_of("ctx"), gall, g_sum, refs[9:14])
     core, mate, across = tp_place()
     me = lax.axis_index("ctx")
     dp = lax.axis_index("dp")
@@ -857,20 +1067,23 @@
     n_cont = conts * clen
     half = plen
     own_rows = rows(core * half, half)
-    pairs = [
-        (wo_h, wo), (px_h.at[own_rows], px), (hid_h, hid), (dm_h, dm), (xn2_h, xn2), (du_h, du),
-        (da_h, da), (wu_h, wu), (wd_h, wd), (hist_h.at[:, own_rows], hist), (xn1_h, xn1),
-    ]
-    loads = [
-        pltpu.make_async_copy(s, t, lsem.at[i]) for i, (s, t) in enumerate(pairs)
-    ]
-    for copy in loads:
-        copy.start()
+    loads = fetch(
+        (
+            (do_h, do), (o_h, o), (wo_h, wo), (px_h, px), (kv_h, kv), (qs_h, qs),
+            (hid_h, hid), (dm_h, dm), (xn2_h, xn2), (du_h, du), (da_h, da), (wu_h, wu), (wd_h, wd),
+            (tab_h, tab), (xn1_h, xn1), (hist_h.at[:, own_rows], hist),
+            (w_h, w), (cx_h, cx), (dh1_h, dh1),
+        )
+        + (((g_first, gall.at[0:EARLY]),) if share else ()),
+        lsem,
+    )
     low = lanes_below((clen, 128), 64)
     zero = jnp.zeros((clen, 128), bf16)
     for c in range(conts):
         flags[c * clen:(c + 1) * clen] = column(valid[c:c + 1].astype(f32))
 
+    loads[0].wait()
+    loads[1].wait()
     g0 = do[0:clen, 128:256].astype(f32)
     g1 = do[clen:2 * clen, 128:256].astype(f32)
     dos[me, 0:n_cont] = do[:, 0:128]
@@ -894,6 +1107,9 @@
             sends.append(remote(ref.at[me], ref.at[me], send.at[d, i], recv.at[d, i], device))
     for copy in sends:
         copy.start()
+    if share:
+        loads[19].wait()
+        loop(EARLY // LINE, line.launch)
 
     def place(a, c):
         return a + c * half
@@ -901,8 +1117,8 @@
     def home(a):
         return a + core * half
 
-    loads[0].wait()
-    loads[1].wait()
+    loads[2].wait()
+    loads[3].wait()
 
     def attn(at, size):
         return dot(o[rows(at, size)], wo[...])
@@ -910,21 +1126,12 @@
     first = TpSum(half, 0, place, s1, attn)
     first.begin()
 
-    for copy in loads[2:7]:
+    for copy in loads[4:11]:
         copy.wait()
     ff = hid.shape[1]
     o_c = o.at[n_prompt:n_prompt + n_cont]
-    bounds = (0, ff, 2 * ff + 192, 2 * ff + 576)
-    if share:
-        gsnd, grcv, gown, gdn, s_g, r_g = refs[:6]
-        got, s_l, r_l = refs[6:9]
-        outer = (me == 0) | (me == 3)
-        inner = (me == 1) | (me == 2)
-
-        def up(k):
-            at = rows(k * LINE, LINE)
-            return remote(gdn.at[at], got.at[at], s_l.at[k], r_l.at[k], {"ctx": 1 + me // 2})
-
+    late = ff - EARLY
+    bounds = (0, late + ff + 192, late + ff + 576)
     def cols_of(d):
         return pl.ds(pl.multiple_of(lax.rem(dp + d, n_dp) * depth, 128), depth)
 
@@ -936,53 +1143,50 @@
         )
 
     def keeper(d):
-        if d == 0:
-            def store(at, value):
-                gown[at:at + value.shape[0]] = value
-        else:
-            def store(at, value):
-                gsnd[d - 1, at:at + value.shape[0]] = value.astype(bf16)
+        def store(at, value):
+            here = slice(at, at + value.shape[0])
+            if d > 0:
+                gsnd[d - 1, here] = value.astype(bf16)
+            else:
+                for k in range(n_dp - 1):
+                    value = value + grcv[k, here].astype(f32)
+                gall[EARLY + at:EARLY + at + value.shape[0]] = value.astype(bf16)
+
         return store
+
+    def late_grads(cols, store):
+        down_grads(hid, dm, cols, EARLY, ff, lambda at, value: store(at - EARLY, value))
+        other_grads(ff, xn2, du, o_c, da, cols, lambda at, value: store(at + late, value))
 
     def kv_grads(cols, store):
         for lo, hi in ((256, 384), (384, 512), (512, 640)):
-            store(2 * ff + 192 + lo - 256, dot_tn(dcat[:, lo:hi], xn1[:, cols]))
-
-    def settle(dst, i):
+            store(late + ff + 192 + lo - 256, dot_tn(dcat[:, lo:hi], xn1[:, cols]))
+
+    def settle(i):
         for d in range(1, n_dp):
             give(d, i).wait()
-
-        def body(j):
-            at = rows(bounds[i] + j * 64, 64)
-            total = gown[at]
-            for d in range(n_dp - 1):
-                total += grcv[d, at].astype(f32)
-            dst(at, j, total.astype(bf16))
-
-        loop((bounds[i + 1] - bounds[i]) // 64, body)
+        (late_grads, kv_grads)[i](cols_of(0), keeper(0))
 
     if share:
         for d in range(1, n_dp):
-            down_grads(hid, dm, cols_of(d), keeper(d))
+            late_grads(cols_of(d), keeper(d))
             give(d, 0).start()
-        for d in range(1, n_dp):
-            other_grads(ff, xn2, du, o_c, da, cols_of(d), keeper(d))
-            give(d, 1).start()
     else:
         width = dm.shape[1]
         for j in range(width // 256):
             cols = pl.ds(256 * j, 256)
             span = slice(256 * j, 256 * j + 256)
 
+            def lay_down(at, value, span=span):
+                g_down[at:at + 128, span] = value.astype(bf16)
+
             def lay(at, value, span=span):
                 if at < ff:
-                    g_down[at:at + 256, span] = value.astype(bf16)
-                elif at < 2 * ff:
-                    g_up[span, at - ff:at - ff + 256] = value.astype(bf16)
+                    g_up[span, at:at + 256] = value.astype(bf16)
                 else:
-                    g_out[at - 2 * ff:at - 2 * ff + value.shape[0], span] = value.astype(bf16)
-
-            down_grads(hid, dm, cols, lay)
+                    g_out[at - ff:at - ff + value.shape[0], span] = value.astype(bf16)
+
+            down_grads(hid, dm, cols, 0, ff, lay_down)
             other_grads(ff, xn2, du, o_c, da, cols, lay)
 
     kd[...] = pltpu.roll(kv[0:n_prompt, 256:384].astype(f32), 64, 1).astype(bf16)
@@ -1075,7 +1279,7 @@
 
     def normed(i):
         a = first.row(i)
-        h = px[rows(a, CH)].astype(f32) + first.take(i)
+        h = px[rows(home(a), CH)].astype(f32) + first.take(i)
         h1[rows(a, CH)] = h
         whitened, _ = norm_rows(h)
         xp[rows(home(a), CH)] = (whitened * gains[2:3] + gains[3:4]).astype(bf16)
@@ -1086,14 +1290,8 @@
         return dot((0.5 * u * (1.0 + gelu_tanh(u))).astype(bf16), wd[...])
 
     second = TpSum(half, 0, place, s2, hidden)
-    def to_line(at, j, value):
-        gdn[rows(j * 64, 64)] = value
-
-    def to_part(at, j, value):
-        g_all[at] = value
-
     source(me, True)
-    for copy in loads[7:9]:
+    for copy in loads[11:13]:
         copy.wait()
 
     def step(i):
@@ -1113,12 +1311,8 @@
 
     loop(max(half // CH, n_ctx), step)
     if share:
-        down_grads(hid, dm, cols_of(0), keeper(0))
-        settle(to_line, 0)
-
-        @pl.when(outer)
-        def _():
-            loop(ff // LINE, lambda k: up(k).start())
+        loop(EARLY // LINE, line.meet)
+    loads[13].wait()
 
     for c in range(conts):
         at = slice(n_prompt + c * clen, n_prompt + (c + 1) * clen)
@@ -1159,20 +1353,20 @@
         v2 = acc_vd[at] + pltpu.roll(acc_vd[at], 64, 1)
         dcat[at, 512:640] = turn(jnp.where(wide, k2, v2), t, -1.0, True).astype(bf16)
 
-    loads[10].wait()
+    loads[14].wait()
     if share:
         for d in range(1, n_dp):
             kv_grads(cols_of(d), keeper(d))
-            give(d, 2).start()
-        other_grads(ff, xn2, du, o_c, da, cols_of(0), keeper(0))
-        kv_grads(cols_of(0), keeper(0))
-        settle(to_part, 1)
+            give(d, 1).start()
+        settle(0)
+        n_late = (EARLY + bounds[1]) // LINE
+        loop(n_late - EARLY // LINE, lambda k: line.launch(k + EARLY // LINE))
     else:
         for j in range(xn1.shape[1] // 256):
             span = slice(256 * j, 256 * j + 256)
 
             def lay_kv(at, value, span=span):
-                at = at - 2 * ff - 192
+                at = at - late - ff - 192
                 g_kv[at:at + 128, span] = value.astype(bf16)
 
             kv_grads(pl.ds(256 * j, 256), lay_kv)
@@ -1195,7 +1389,6 @@
         third = jnp.where(low, third, 0.0)
         dcat[at, 128:256] = turn(third, t, -1.0, True).astype(bf16)
 
-    loads[9].wait()
     give_out = Share(out, home, shares[2:4])
 
     def mixed(i):
@@ -1205,184 +1398,24 @@
         out[rows(home(a), CH)] = mixed_states(ids, dwa, hist, here, y).astype(bf16)
         give_out.copy(i, a).start()
 
-    loop(half // CH, mixed)
+    def prompts_out():
+        loads[15].wait()
+        loop(half // CH, mixed)
+
+    for copy in loads[16:19]:
+        copy.wait()
+    if share:
+        q_state = (qsnd, qrcv, s_q, r_q, gall, line, lambda: settle(1), n_late)
+    else:
+        q_state = (g_q,)
+    input_grad_tail(
+        n_dp, n_ctx, share, plen, clen, depth,
+        dcat, w, px, cx, gains, dh1, stat_in, xn1, grad_p, grad_c, fin,
+        smalls, s3, shares[4:6], prompts_out, *q_state,
+    )
     loop(half // CH, lambda i: give_out.copy(i, second.row(i)).wait())
-    if share:
-        settle(to_part, 2)
-
-        @pl.when(outer)
-        def _():
-            g_all[0:ff] = gdn[...]
-            loop(ff // LINE, lambda k: up(k).wait_send())
-
-        @pl.when(inner)
-        def _():
-            def meet(k):
-                at = rows(k * LINE, LINE)
-                up(k).wait_recv()
-                g_all[at] = (gdn[at].astype(f32) + got[at].astype(f32)).astype(bf16)
-
-            loop(ff // LINE, meet)
-    first.close()
-    second.close()
     for copy in sends:
         copy.wait_send()
-
-
-def input_grad_body(
-    n_dp, n_ctx, share, split, c_split, depth, ready,
-    dcat, w, px, cx, gains, dh1, stat_in, xn_h, *refs,
-):
-    if share:
-        g_part, grad_p, grad_c, fin, g_sum = refs[:5]
-        refs = refs[5:]
-    else:
-        grad_p, grad_c, fin, g_q = refs[:4]
-        refs = refs[4:]
-    xn, lsem, grad, stat, stats_m, stats_y, stats_c, stats_d, s_s, r_s = refs[:10]
-    s1 = refs[10:17]
-    shares = refs[17:19]
-    refs = refs[19:]
-    core, mate, across = tp_place()
-    me = lax.axis_index("ctx")
-    dp = lax.axis_index("dp")
-    ctx_peers = axis_peers("ctx", n_ctx)
-    dp_peers = axis_peers("dp", n_dp)
-    half = split + c_split
-    n_prompt = 2 * split
-    n_cont = 2 * c_split
-    load = pltpu.make_async_copy(xn_h.at[n_prompt:n_prompt + n_cont], xn, lsem.at[0])
-    load.start()
-    stat[...] = 0.5 * stat_in[...]
-    greet([mate, across] + ctx_peers + dp_peers)
-    if share:
-        gsnd, gown, grcv, s_g, r_g, gall = refs[:6]
-        n_part = g_part.shape[0]
-        n_line = n_part // LINE
-        take_part = pltpu.make_async_copy(g_part, gall.at[0:n_part], lsem.at[1])
-        take_part.start()
-        line = LineSum(me, gall, g_sum, refs[6:11], ready)
-        take_part.wait()
-        loop(n_line - ready, lambda k: line.launch(k + ready))
-        loop(ready, line.skip)
-
-    def place(a, c):
-        return full_at(a, c, split, c_split)
-
-    def home(a):
-        return full_at(a, core, split, c_split)
-
-    def compute(at, size):
-        part = dot(dcat[rows(at, size)], w[...])
-        b = at // n_prompt
-        p = px[rows(at * (1 - b), size)].astype(f32)
-        c = cx[rows((at - n_prompt) * b, size)].astype(f32)
-        whitened, _ = norm_rows(jnp.where(b == 0, p, c))
-        stat[0:1] += jnp.sum(part * whitened, 0, keepdims=True)
-        stat[1:2] += jnp.sum(part, 0, keepdims=True)
-        return part
-
-    total = TpSum(half, split, place, s1, compute)
-    total.begin(2)
-
-    def small(src, dst, i, device):
-        return remote(src, dst, s_s.at[i], r_s.at[i], device)
-
-    stats_m[0] = stat[...]
-    to_mate = small(stats_m.at[0], stats_m.at[1], 0, mate)
-    to_mate.start()
-    load.wait()
-
-    def q_grads(cols):
-        return dot_tn(dcat[n_prompt:n_prompt + n_cont, 0:256], xn[:, cols])[0:3 * HEAD_DIM]
-
-    gives = []
-    if share:
-        for d in range(1, n_dp):
-            other = lax.rem(dp + d, n_dp)
-            cols = pl.ds(pl.multiple_of(other * depth, 128), depth)
-            gsnd[d - 1] = q_grads(cols).astype(bf16)
-            copy = remote(
-                gsnd.at[d - 1], grcv.at[d - 1], s_g.at[d - 1], r_g.at[d - 1], {"dp": other}
-            )
-            copy.start()
-            gives.append(copy)
-        gown[...] = q_grads(pl.ds(pl.multiple_of(dp * depth, 128), depth))
-    else:
-        g_q[...] = q_grads(slice(None)).astype(bf16)
-    to_mate.wait()
-    stats_y[0] = stats_m[0] + stats_m[1]
-    to_far = small(stats_y.at[0], stats_y.at[1], 1, across)
-    to_far.start()
-    total.resume(2)
-    give = Share(grad, home, shares)
-
-    def finish(i):
-        a = total.row(i)
-        b = a // split
-        value = total.take(i)
-        p = px[rows((core * split + a) * (1 - b), CH)].astype(f32)
-        c = cx[rows((core * c_split + a - split) * b, CH)].astype(f32)
-        whitened, inverse = norm_rows(jnp.where(b == 0, p, c))
-        back = norm_back(value, whitened, inverse, gains[0:1])
-        extra = dh1[rows((a - split) * b, CH)]
-        grad[rows(home(a), CH)] = jnp.where(b == 0, back, back + extra).astype(bf16)
-        give.copy(i, a).start()
-        if share:
-            line.meet(ready + i + 1)
-            line.turn(2 * i)
-            line.turn(2 * i + 1)
-
-    def part(lo, hi):
-        loop(hi - lo, lambda i: finish(i + lo))
-
-    if share:
-        line.meet(ready)
-    part(0, 2)
-    if share:
-        for copy in gives:
-            copy.wait()
-        value = gown[...]
-        for d in range(n_dp - 1):
-            value += grcv[d].astype(f32)
-        gall[n_part:n_part + 3 * HEAD_DIM] = value.astype(bf16)
-        line.launch(n_line)
-    part(2, 4)
-    to_far.wait()
-    stats_c[me] = stats_y[0] + stats_y[1]
-    to_ctx = [
-        small(stats_c.at[me], stats_c.at[me], 2 + d, device) for d, device in enumerate(ctx_peers)
-    ]
-    for copy in to_ctx:
-        copy.start()
-    part(4, 5)
-    if share:
-        line.meet(n_line)
-    part(5, 6)
-    for copy in to_ctx:
-        copy.wait()
-    value = stats_c[0]
-    for d in range(1, n_ctx):
-        value += stats_c[d]
-    stats_d[dp] = value
-    to_dp = [
-        small(stats_d.at[dp], stats_d.at[dp], 1 + n_ctx + d, device)
-        for d, device in enumerate(dp_peers)
-    ]
-    for copy in to_dp:
-        copy.start()
-    loop(total.n, lambda i: give.copy(i, total.row(i)).wait())
-    grad_p[...] = grad[0:n_prompt]
-    grad_c[...] = grad[n_prompt:n_prompt + n_cont]
-    for copy in to_dp:
-        copy.wait()
-    value = stats_d[0]
-    for d in range(1, n_dp):
-        value += stats_d[d]
-    fin[...] = value
-    total.close()
-    if share:
-        loop(n_line + 1, line.land)
 
 
 def output_body(
@@ -1496,11 +1529,13 @@
             states, states, states,
             vmem((1, 3, 192, depth) if share else (n_dp, 3, 192, depth), bf16),
             DMA((n_dp - 1, 7)), DMA((n_dp - 1, 7)),
-            DMA((2, n_ctx)), DMA((n_ctx,)), DMA((n_ctx - 1,)), DMA((n_ctx - 1,)),
+            DMA((2, n_ctx, groups)), DMA((n_ctx, groups)), DMA((n_ctx - 1,)), DMA((n_ctx - 1,)),
             DMA((n_dp - 1, 4)), DMA((n_dp - 1, 4)), DMA((9,)),
-        ],
+        ]
+        + like(w_t, px, cx, out_weight, up_weight, down_weight)
+        + [DMA((6,))],
         0,
-        [SMEM_SPEC] + [VMEM_SPEC] * 11,
+        [SMEM_SPEC] + [HBM_SPEC] * 3 + [VMEM_SPEC] * 5 + [HBM_SPEC] * 3,
         (cont_group, px, cx, w_t, *vectors, valid_mask, out_weight, up_weight, down_weight),
         "front",
         [HBM_SPEC] * 6 + [VMEM_SPEC] * 6,
@@ -1511,9 +1546,17 @@
         wd = lax.all_gather(down_weight, "dp", axis=1, tiled=True)
         wo = jnp.concatenate([out_w[:128], jnp.zeros((64, width), bf16), out_w[128:]], 0)
 
-    cont_out, dm, hid, xn2, du, da, do, dh1, stat, qs = kernel_call(
-        functools.partial(middle_body, n_ctx, n_prompt, clen),
-        [
+    outs = [((EARLY, depth), bf16)] if share else []
+    extra = []
+    if share:
+        extra = [
+            vmem((n_dp - 1, EARLY, depth), bf16), vmem((n_dp - 1, EARLY, depth), bf16),
+            vmem((EARLY, depth), f32), DMA((n_dp - 1,)), DMA((n_dp - 1,)),
+        ]
+    got = kernel_call(
+        functools.partial(middle_body, n_ctx, n_dp, share, n_prompt, clen, depth),
+        outs
+        + [
             ((n_cont, width), bf16), ((n_cont, width), bf16), ((n_cont, ff), bf16),
             ((n_cont, width), bf16), ((n_cont, ff), bf16), ((n_cont, width), bf16),
             ((n_cont, 256), bf16), ((c_split, width), f32), ((16, width), f32),
@@ -1523,37 +1566,54 @@
             vmem((4, c_split, width), bf16), vmem((c_split, width), bf16),
             vmem((n_cont, ff), f32), vmem((c_split, width), f32),
             vmem((c_split, width), f32), vmem((clen, 128), f32),
-            DMA((2,)), DMA((n_ctx - 1,)), DMA((n_ctx - 1,)),
+            DMA((7,)), DMA((n_ctx - 1,)), DMA((n_ctx - 1,)),
+            vmem((n_cont, 256), bf16), vmem((256, width), bf16), vmem((c_split, width), bf16),
+            vmem((width, ff), bf16), vmem((ff, width), bf16),
         ]
         + TpSum.scratch(c_split, width) * 3
-        + share_scratch(c_split) * 4,
+        + share_scratch(c_split) * 4
+        + extra,
         1,
-        [SMEM_SPEC] * 2 + [VMEM_SPEC] * 9 + [HBM_SPEC] * 2,
+        [SMEM_SPEC] * 2
+        + [HBM_SPEC] + [VMEM_SPEC] * 2 + [HBM_SPEC] * 4 + [VMEM_SPEC] * 2 + [HBM_SPEC] * 2,
         (
             layer_ids, dwa_weights, o, qpack, msgs, wo, wu, wd, cx, gains, valid_mask,
             cont_hist.reshape(4, n_cont, width), teacher.reshape(n_cont, width),
         ),
         "middle",
     )
-
-    grad_rows = 2 * ff + 9 * HEAD_DIM
-    outs = [((n_rows, 640), bf16), ((n_prompt, width), bf16)]
+    cont_out, dm, hid, xn2, du, da, do, dh1, stat, qs = got[-10:]
+    g_first = list(got[:-10])
+
+    grad_rows = 2 * ff + 12 * HEAD_DIM
+    outs = [
+        ((n_prompt, width), bf16), ((n_prompt, width), bf16), ((n_cont, width), bf16),
+        ((16, width), f32),
+    ]
+    out_specs = [VMEM_SPEC] + [HBM_SPEC] * 2 + [VMEM_SPEC]
     if share:
         outs += [((grad_rows, depth), bf16)]
+        out_specs += [VMEM_SPEC]
+        late = grad_rows - EARLY - 3 * HEAD_DIM
+        third = (n_dp - 1, 3 * HEAD_DIM, depth)
         extra = [
-            vmem((n_dp - 1, grad_rows, depth), bf16), vmem((n_dp - 1, grad_rows, depth), bf16),
-            vmem((grad_rows, depth), f32), vmem((ff, depth), bf16),
-            DMA((n_dp - 1, 3)), DMA((n_dp - 1, 3)),
-            vmem((ff, depth), bf16), DMA((ff // LINE,)), DMA((ff // LINE,)),
-        ]
+            vmem((n_dp - 1, late, depth), bf16), vmem((n_dp - 1, late, depth), bf16),
+            DMA((n_dp - 1, 2)), DMA((n_dp - 1, 2)),
+            vmem(third, bf16), vmem(third, bf16),
+            DMA((n_dp - 1,)), DMA((n_dp - 1,)), vmem((grad_rows, depth), bf16),
+        ] + LineSum.scratch(grad_rows // LINE, depth)
     else:
         outs += [
             ((ff, width), bf16), ((width, ff), bf16), ((3 * HEAD_DIM, width), bf16),
-            ((384, width), bf16),
+            ((384, width), bf16), ((3 * HEAD_DIM, width), bf16),
         ]
+        out_specs += [VMEM_SPEC] * 5
         extra = []
     acc = vmem((n_prompt, 128), f32)
-    got = kernel_call(
+    wide = vmem((split, width), bf16)
+    tall = vmem((half, width), bf16)
+    n_p, n_h = split // CH, half // CH
+    back = kernel_call(
         functools.partial(
             attend_back_body, n_ctx, n_dp, share, plen, clen, groups, conts, depth
         ),
@@ -1563,7 +1623,7 @@
             vmem((n_cont, width), bf16), vmem((n_cont, ff), bf16),
             vmem((n_cont, width), bf16), vmem((256, width), bf16),
             vmem((width, ff), bf16), vmem((ff, width), bf16),
-            vmem((split, width), bf16), vmem((4, split, width), bf16), DMA((11,)),
+            vmem((n_prompt, width), bf16), vmem((4, split, width), bf16), DMA((20,)),
             vmem((n_ctx, packed, 128), bf16), vmem((n_ctx, 8 * conts, clen), f32),
             vmem((2 * n_ctx, packed, 128), bf16), vmem((n_prompt, 128), bf16),
             acc, acc, acc, acc, vmem((packed, 128), f32),
@@ -1571,52 +1631,35 @@
             vmem((n_prompt, width), bf16), vmem((split, width), f32),
             vmem((n_rows, width), bf16), vmem((n_cont, 128), f32),
         ]
-        + TpSum.scratch(split, width) * 2
+        + like(do, o, kv, tab, qs, w_full, cx, dh1)
+        + [
+            vmem((n_rows, 640), bf16), tall, vmem((half, width), f32),
+            wide, wide, wide, DMA((2, n_p)), DMA((2, n_p)),
+            wide, wide, DMA((2, n_p)), DMA((2, n_p)),
+            tall, tall, tall, DMA((2, n_h)), DMA((2, n_h)),
+        ]
         + share_scratch(split) * 2
+        + share_scratch(half)
+        + [
+            vmem((n_rows, width), bf16), vmem((16, width), f32), vmem((2, 16, width), f32),
+            vmem((2, 16, width), f32), vmem((n_ctx, 16, width), f32),
+            vmem((n_dp, 16, width), f32),
+            DMA((1 + n_ctx + n_dp,)), DMA((1 + n_ctx + n_dp,)), DMA((2,)),
+        ]
         + extra,
         2,
-        [SMEM_SPEC] * 2 + [VMEM_SPEC] * 9 + [HBM_SPEC] * 11,
+        [SMEM_SPEC] * 2
+        + [VMEM_SPEC] + [HBM_SPEC] * 2 + [VMEM_SPEC] * 3 + [HBM_SPEC] * 17 + [VMEM_SPEC]
+        + [HBM_SPEC] * len(g_first),
         (
-            layer_ids, dwa_weights, msgs, qs, do, o, lse, kv, valid_mask, tab, gains,
+            layer_ids, dwa_weights, msgs, do, o, lse, valid_mask, gains, kv, tab, qs,
             hid, dm, xn2, du, da, wo, wu, wd, px, prompt_hist.reshape(4, n_prompt, width), xn1,
+            w_full, cx, dh1, stat, *g_first,
         ),
-        "attend_back",
+        "back",
+        out_specs,
     )
-    dcat, prompt_out = got[:2]
-
-    stat_rows = vmem((16, width), f32)
-    outs = [((n_prompt, width), bf16), ((n_cont, width), bf16), ((16, width), f32)]
-    args = (dcat, w_full, px, cx, gains, dh1, stat, xn1)
-    specs = [VMEM_SPEC] * 7 + [HBM_SPEC]
-    if share:
-        args += (got[2],)
-        specs += [HBM_SPEC]
-        outs += [((grad_rows + LINE, depth), bf16)]
-        extra = [
-            vmem((n_dp - 1, 3 * HEAD_DIM, depth), bf16), vmem((3 * HEAD_DIM, depth), f32),
-            vmem((n_dp - 1, 3 * HEAD_DIM, depth), bf16), DMA((n_dp - 1,)), DMA((n_dp - 1,)),
-            vmem((grad_rows + LINE, depth), bf16),
-        ] + LineSum.scratch(grad_rows // LINE + 1, depth)
-    else:
-        outs += [((3 * HEAD_DIM, width), bf16)]
-        extra = []
-    last = kernel_call(
-        functools.partial(
-            input_grad_body, n_dp, n_ctx, share, split, c_split, depth, ff // LINE
-        ),
-        outs,
-        [
-            vmem((n_cont, width), bf16), DMA((2,)), vmem((n_rows, width), bf16),
-            stat_rows, vmem((2, 16, width), f32), vmem((2, 16, width), f32),
-            vmem((n_ctx, 16, width), f32), vmem((n_dp, 16, width), f32),
-            DMA((1 + n_ctx + n_dp,)), DMA((1 + n_ctx + n_dp,)),
-        ]
-        + TpSum.scratch(half, width)
-        + share_scratch(half)
-        + extra,
-        3, specs, args, "input_grad",
-    )
-    grad_p, grad_c, fin = last[:3]
+    prompt_out, grad_p, grad_c, fin = back[:4]
 
     outs = [
         ((n_prompt, width), bf16), ((n_cont, width), bf16), ((n_prompt, width), bf16),
@@ -1628,7 +1671,7 @@
     if share:
         outs += [((3, 192, depth), f32), ((192, depth), f32), ((depth, ff), f32), ((ff, depth), f32)]
         out_specs += [VMEM_SPEC] * 4
-        args += (last[3],)
+        args += (back[4],)
         specs += [VMEM_SPEC]
     done = pl.pallas_call(
         functools.partial(output_body, n_ctx, n_dp, share, ff),
@@ -1650,13 +1693,13 @@
             part = lax.psum_scatter(g, "dp", scatter_dimension=dim, tiled=True)
             return lax.psum(part, "ctx").astype(f32)
 
-        g_down, g_up, g_out, g_kv = got[2:]
+        g_down, g_up, g_out, g_kv, g_q = back[4:]
         r_down = scattered(g_down, 1)
         r_up = scattered(g_up, 0)
         r_out = scattered(g_out, 1)
         g_k = jnp.concatenate([g_kv[0:128], g_kv[256:320]], 0)
         g_v = jnp.concatenate([g_kv[128:256], g_kv[320:384]], 0)
-        r_qkv = scattered(jnp.stack([last[3], g_k, g_v]).transpose(2, 0, 1), 0)
+        r_qkv = scattered(jnp.stack([g_q, g_k, g_v]).transpose(2, 0, 1), 0)
     return (
         done[0].reshape(groups, plen, width),
         done[1].reshape(conts, clen, width),

time: 245 us -> 226 us (0.922)
  Pallas kernels: 243 us -> 225 us
    pallas_call x4 -> x3, Pallas kernels: 236 us -> 218 us  [kernel_call(): pl.pallas_call(body, out_shape=[jax.ShapeDtypeStruct(s, d) for s, d in ou...]
where the time goes in v4:
time: 226 us
  Pallas kernels  225 us (100%)
    pallas_call x3, Pallas kernels, kernel_call(): pl.pallas_call(body, out_shape=[jax.ShapeDtypeStruct(s, d) for s, d in ou...  218 us
    pallas_call x1, Pallas kernels, per_device(): pl.pallas_call(functools.partial(output_body, n_ctx, n_dp, share, ff), ou...  7.01 us

profile of v4, /device:TPU:0, one launch (start us, length us, event | category | flops | bytes accessed | tf_op | source)
XLA Modules:
  0.0 226.1 jit_solution(3233696771493362593)
XLA Ops:
  0.6 71.7 %front.1 = (bf16[1536,768]{1,0:T(8,128)(2,1)}, bf16[1536,384]{1,0:T(8,128)(2,1)}, f32[768,384]{1,0:T(8,128)}, bf16[640,768]{1,0:T(8,128)(2,1)}, bf16[768,768]{1,...) custom-call(s32[2]{0:T(128)} %sel.1, ...), custom_call_target="tpu_custom_call" | custom-call | bytes 31457280 | tf_op jit(solution)/shard_map/front/pallas_call | solution.py:55
  72.4 44.7 %middle.1 = (bf16[384,384]{1,0:T(8,128)(2,1)}, bf16[512,768]{1,0:T(8,128)(2,1)}, bf16[512,768]{1,0:T(8,128)(2,1)}, bf16[512,768]{1,0:T(8,128)(2,1)}, bf16[512,76...) custom-call(s32[4]{0:T(128)} %ids.5, f32[5]{0:T(128)} %dwa.3, ...), custom_call_target="tpu_custom_call" | custom-call | bytes 31457280 | tf_op jit(solution)/shard_map/middle/pallas_call | solution.py:55
  117.0 101.9 %back.1 = (bf16[1024,768]{1,0:T(8,128)(2,1)}, bf16[1024,768]{1,0:T(8,128)(2,1)}, bf16[512,768]{1,0:T(8,128)(2,1)}, f32[16,768]{1,0:T(8,128)}, bf16[2304,384]{1,0:T(8,128)(2,1)}) custom-call(s32[4]{0:T(128)} %ids.5, f32[5]{0:T(128)} %dwa.3, f32[32,128]{1,0:T(8,128)} %get-tuple-element.56.msgs, bf16[512,256]{1,0:T(8,128)(2,1)} %get-tuple-element.63.do_h, ...), custom_call_target="tpu_custom_call" | custom-call | bytes 31457280 | tf_op jit(solution)/shard_map/back/pallas_call | solution.py:55
  219.0 7.0 %outputs.1 = (bf16[1024,768]{1,0:T(8,128)(2,1)}, bf16[512,768]{1,0:T(8,128)(2,1)}, bf16[1024,768]{1,0:T(8,128)(2,1)}, bf16[512,768]{1,0:T(8,128)(2,1)}, f32[1]{0...) custom-call(s32[4]{0:T(128)} %ids.5, ...), custom_call_target="tpu_custom_call" | custom-call | tf_op jit(solution)/shard_map/outputs/pallas_call | solution.py:1676

commit v5 on v4

--- a/solution.py
+++ b/solution.py
@@ -144,15 +144,30 @@
 
 def front_body(
     n_ctx, n_dp, share, plen, clen, groups, conts,
-    sel, px_h, cx_h, w_h, g1, b1, g2, b2, valid, wo_h, wu_h, wd_h,
-    xn_o, kv_o, tab_o, w_o, wu_o, wd_o, wo_o, o, lse, msgs, gains, qpack,
-    xn, q, kvs, kvc, tab, w_full, gb, gbs, cnt, cnts, notes, m_s, l_s, acc_s,
-    wgs, s_x, r_x, s_kv, r_kv, s_c, r_c, s_w, r_w, osem,
-    w, px, cx, wo, wu, wd, lsem,
+    sel, ids, dwa, px_h, cx_h, w_h, g1, b1, g2, b2, valid, wo_h, wu_h, wd_h, hist, teach, *refs,
 ):
-    loads = fetch(
-        ((w_h, w), (px_h, px), (cx_h, cx), (wo_h, wo), (wu_h, wu), (wd_h, wd)), lsem
-    )
+    xn_o, kv_o, tab_o, w_o, o, lse, msgs, gains = refs[:8]
+    middle_outs = refs[8:18]
+    refs = refs[18:]
+    if share:
+        gdn, wu_o, wd_o, wo_o = refs[:4]
+        refs = refs[4:]
+    (
+        qpack, xn, q, kvs, kvc, tab, w_full, gb, gbs, cnt, cnts, notes, m_s, l_s, acc_s,
+        wgs, s_x, r_x, s_kv, r_kv, s_c, r_c, s_w, r_w, osem, w, px, cx, lsem, wu_f, wd_f,
+    ) = refs[:31]
+    refs = refs[31:]
+    if share:
+        wo, wu, wd = refs[:3]
+        refs = refs[3:]
+        weight_pairs = ((wo_h, wo), (wu_h, wu), (wd_h, wd))
+    else:
+        wo_o = refs[0]
+        gdn = None
+        refs = refs[1:]
+        weight_pairs = ((wo_h, wo_o), (wu_h, wu_f), (wd_h, wd_f))
+    core, mate, across = tp_place()
+    loads = fetch(((w_h, w), (px_h, px), (cx_h, cx)) + weight_pairs, lsem)
     me = lax.axis_index("ctx")
     mine = lax.axis_index("dp")
     depth = w.shape[2]
@@ -167,7 +182,7 @@
         gb[i:i + 1] = vector[...].astype(f32).reshape(1, depth)
     gb[4:8] = jnp.zeros((4, depth), f32)
     cnt[...] = jnp.zeros(cnt.shape, f32) + jnp.sum(valid[...].astype(f32))
-    greet(dp_peers + peers)
+    greet(dp_peers + peers + [mate, across])
     loads[0].wait()
 
     copies = []
@@ -200,7 +215,7 @@
     if share:
         pairs = [
             (wo.at[0:128], wo_o.at[0:128, cols]), (wo.at[128:192], wo_o.at[192:256, cols]),
-            (wu, wu_o.at[here]), (wd, wd_o.at[:, cols]),
+            (wu, wu_f.at[here]), (wd, wd_f.at[:, cols]),
         ]
         for d, device in enumerate(dp_peers):
             for i, (s, t) in enumerate(pairs):
@@ -208,7 +223,8 @@
         for copy in weights:
             copy.start()
         local += fetch(pairs, osem)
-    wo_o[128:192] = jnp.zeros((64, width), bf16)
+    if share:
+        wo_o[128:192] = jnp.zeros((64, width), bf16)
     w_full[192:256] = jnp.zeros((64, width), bf16)
     gbs[mine] = gb[...]
     cnts[mine] = cnt[...]
@@ -446,7 +462,7 @@
                 def _():
                     hop(me + d, g, -1, 1).start()
 
-            @pl.when(me - d >= 0)
+            @pl.when((me - d > 0) | ((me == d) & (g < groups - 1)))
             def _():
                 prompt_part(me - d, g, False)
 
@@ -475,10 +491,13 @@
         o[at, 128:256] = jnp.where(low, 0.0, acc_s[state + 2] / l2).astype(bf16)
         return (l0, l1, l2)
 
-    def finish_prompt(i):
-        finish(rows(i * tile, tile), 3 * i)
-
-    loop(groups * tiles, finish_prompt)
+    def rest_of_prompts():
+        @pl.when(me > 0)
+        def _():
+            prompt_part(0, groups - 1, False)
+
+        loop(groups * tiles, lambda i: finish(rows(i * tile, tile), 3 * i))
+
     for i in range(conts):
         state = 3 * (groups * tiles + i)
         sums = finish(rows(n_prompt + i * tile, tile), state)
@@ -487,6 +506,19 @@
             value = m_s[state + h] + jnp.log(sums[h])
             lse[8 * i + h:8 * i + h + 1] = jnp.transpose(value)[0:1]
 
+    for copy in weights:
+        copy.wait()
+    for copy in local:
+        copy.wait()
+    if share:
+        local = fetch(((wu_f, wu_o), (wd_f, wd_o)), osem)
+    else:
+        local = []
+    middle_part(
+        n_ctx, n_dp, share, n_prompt, clen, depth, rest_of_prompts,
+        ids, dwa, o, qpack, msgs, wo_o, wu_f, wd_f, cx, gains, valid, hist, teach,
+        gdn, middle_outs, refs,
+    )
     for slot in range(n_ctx):
         for g in range(groups):
             @pl.when((slot <= me) & (me < last))
@@ -500,8 +532,6 @@
     for group in copies:
         for copy in group:
             copy.wait_send()
-    for copy in weights:
-        copy.wait()
     for copy in local:
         copy.wait()
 
@@ -555,13 +585,16 @@
         self.pair(i).start()
         self.own[at] = self.compute(self.place(a, self.core), CH)
 
-    def begin(self, held=0):
+    def begin(self, held=0, after=None):
         def body(i):
             self.launch(i)
 
             @pl.when((i > 0) & (i <= self.n - held))
             def _():
                 self.second(i - 1)
+
+            if after is not None:
+                after(i)
 
         loop(self.n, body)
         if not held:
@@ -623,36 +656,24 @@
     store(ff + 128, g[192:256])
 
 
-def middle_body(
-    n_ctx, n_dp, share, n_prompt, clen, depth,
-    ids, dwa, o_h, qpack, msgs, wo_h, wu_h, wd_h, cx_h, gains, valid, hist, teach, *refs,
+def middle_part(
+    n_ctx, n_dp, share, n_prompt, clen, depth, between,
+    ids, dwa, o, qpack, msgs, wo, wu, wd, cx, gains, valid, hist, teach, gdn, outs, refs,
 ):
-    if share:
-        gdn = refs[0]
-        refs = refs[1:]
-    out, dm, hid, xn, du, da, do, dh1, stat, qs = refs[:10]
-    hc, tc, slope, h1, dy, mask, hsem, s_q, r_q, o, wo, cx, wu, wd = refs[10:24]
-    scratch = refs[24:]
+    out, dm, hid, xn, du, da, do, dh1, stat, qs = outs
+    hc, tc, slope, h1, dy, mask, hsem, s_q, r_q = refs[:9]
+    scratch = refs[9:]
     core, mate, across = tp_place()
     ctx = lax.axis_index("ctx")
     dp = lax.axis_index("dp")
     half = clen
     n_cont = 2 * half
     mine = rows(core * half, half)
-    loads = fetch(
-        (
-            (o_h.at[n_prompt:n_prompt + n_cont], o), (wo_h, wo), (cx_h.at[mine], cx),
-            (wu_h, wu), (wd_h, wd), (hist.at[:, mine], hc), (teach.at[mine], tc),
-        ),
-        hsem,
-    )
+    loads = fetch(((hist.at[:, mine], hc), (teach.at[mine], tc)), hsem)
     qs[ctx] = qpack[...]
     mask[...] = column(valid[pl.ds(core, 1)].astype(f32))
     stat[...] = jnp.zeros(stat.shape, f32)
     others = axis_peers("ctx", n_ctx)
-    greet([mate, across] + others + (axis_peers("dp", n_dp) if share else []))
-    for copy in loads[:3]:
-        copy.wait()
     s1, s2, s3 = scratch[0:7], scratch[7:14], scratch[14:21]
     shares = scratch[21:29]
 
@@ -666,7 +687,7 @@
         loop(half // CH, body)
 
     def attn(at, size):
-        return dot(o[rows(at, size)], wo[...])
+        return dot(o[rows(n_prompt + at, size)], wo[...])
 
     first = TpSum(half, 0, place, s1, attn)
     each(first.launch)
@@ -675,13 +696,12 @@
         remote(qs.at[ctx], qs.at[ctx], s_q.at[d], r_q.at[d], device)
         for d, device in enumerate(others)
     ]
-    for copy in moves:
-        copy.start()
+    between()
     give_xn = Share(xn, home, shares[0:2])
 
     def normed(i):
         a = first.row(i)
-        h = cx[rows(a, CH)].astype(f32) + first.take(i)
+        h = cx[rows(home(a), CH)].astype(f32) + first.take(i)
         h1[rows(a, CH)] = h
         whitened, _ = norm_rows(h)
         xn[rows(home(a), CH)] = (whitened * gains[2:3] + gains[3:4]).astype(bf16)
@@ -714,9 +734,11 @@
         each(body)
         after.second(after.n - 1)
 
-    for copy in loads[3:]:
+    for copy in loads:
         copy.wait()
     onward(normed, give_xn, second)
+    for copy in moves:
+        copy.start()
     give_dm = Share(dm, home, shares[2:4])
     give_out = Share(out, home, shares[4:6])
     count = msgs[0:1]
@@ -935,7 +957,14 @@
         return part
 
     total = TpSum(half, split, place, sums, compute)
-    total.begin(2)
+
+    def also(i):
+        if share:
+            @pl.when(lax.rem(i, 2) == 0)
+            def _():
+                line.meet(2 + i // 2)
+
+    total.begin(2, also)
 
     def small(src, dst, i, device):
         return remote(src, dst, s_s.at[i], r_s.at[i], device)
@@ -954,8 +983,7 @@
     to_far.start()
     total.resume(2)
     if share:
-        for k in range(2, 5):
-            line.meet(k)
+        line.meet(5)
         for copy in gives:
             copy.wait()
         value = q_grads(pl.ds(pl.multiple_of(dp * depth, 128), depth))
@@ -964,6 +992,9 @@
         gall[n_line * LINE:n_line * LINE + 3 * HEAD_DIM] = value.astype(bf16)
         line.launch(n_line)
     prompts_out()
+    if share:
+        line.turn(0)
+        line.meet(6)
     give = Share(grad, home, shares)
 
     def finish(i):
@@ -978,9 +1009,12 @@
         grad[rows(home(a), CH)] = jnp.where(b == 0, back, back + extra).astype(bf16)
         give.copy(i, a).start()
         if share:
-            k = i + i // 3
+            k = 1 + i + i // 3
             line.turn(k)
-            line.meet(5 + i)
+
+            @pl.when(i < 5)
+            def _():
+                line.meet(7 + i)
 
             @pl.when(lax.rem(i, 3) == 2)
             def _():
@@ -999,8 +1033,7 @@
         copy.start()
     part(4, 6)
     if share:
-        line.meet(n_line)
-        line.turn(8)
+        line.turn(9)
     for copy in to_ctx:
         copy.wait()
     value = stats_c[0]
@@ -1014,7 +1047,7 @@
     for copy in to_dp:
         copy.start()
     if share:
-        for k in range(9, n_line + 1):
+        for k in range(10, n_line + 1):
             line.turn(k)
     loop(total.n, lambda i: give.copy(i, total.row(i)).wait())
     saves = fetch(
@@ -1205,7 +1238,10 @@
     def halves(a):
         return jnp.where(low, a, zero), jnp.where(low, zero, a)
 
-    def continuation(src, c, k_b, k_c, k_d, k_s, mask):
+    def beside(a, keeps):
+        return a if keeps is None else jnp.concatenate([a * keep for keep in keeps], 1)
+
+    def continuation(src, c, k_b, k_c, k_d, k_s, mask, keeps):
         base = c * clen
         a0, a1 = halves(qs[src, base:base + clen])
         d0, d1 = halves(dos[src, base:base + clen])
@@ -1214,40 +1250,35 @@
         st = 8 * c
         row = lambda i: sts[src, st + i:st + i + 1]
         p0, s0 = one_head(a0, d0, k_b, k_c, row(0), row(3), mask)
-        dv = dot(p0, d0)
-        dk = dot(s0, a0)
-        dq0 = dot_tn(s0, k_b)
         p1, s1_ = one_head(a1, d1, k_b, k_c, row(1), row(4), mask)
-        dv += dot(p1, d1)
-        dk += dot(s1_, a1)
-        dq1 = dot_tn(s1_, k_b)
+        dv = dot(jnp.concatenate([p0, p1], 1), beside(jnp.concatenate([d0, d1], 0), keeps))
+        dk = dot(jnp.concatenate([s0, s1_], 1), beside(jnp.concatenate([a0, a1], 0), keeps))
+        dq = jnp.where(low, dot_tn(s0, k_b), dot_tn(s1_, k_b))
         keys, values = (k_d, k_s) if c == 0 else (k_s, k_d)
         p2, s2_ = one_head(e, g, keys, values, row(2), row(5), mask)
-        dvd = dot(p2, g)
-        dkd = dot(s2_, e)
-        dq2 = dot_tn(s2_, keys)
-        return dk, dv, dkd, dvd, jnp.where(low, dq0, dq1), dq2
+        dvd = dot(p2, beside(g, keeps))
+        dkd = dot(s2_, beside(e, keeps))
+        return dk, dv, dkd, dvd, dq, dot_tn(s2_, keys)
 
     def source(src, own):
         pair = []
         for c in range(conts):
             pick = msgs[pl.ds(src * 8 + 1 + c, 1)]
-
-            def choose(one, two):
-                return jnp.where(pick == 0.0, one.astype(f32), two.astype(f32)).astype(bf16)
-
-            k_b = choose(kv[0:plen, 0:128], kv[plen:2 * plen, 0:128])
-            k_c = choose(kv[0:plen, 128:256], kv[plen:2 * plen, 128:256])
-            k_d = choose(kv[0:plen, 256:384], kv[plen:2 * plen, 256:384])
-            k_s = choose(kd[0:plen], kd[plen:2 * plen])
-            dk, dv, dkd, dvd, dqa, dqd = continuation(src, c, k_b, k_c, k_d, k_s, None)
-            for g in range(groups):
-                keep = (pick == 1.0 * g).astype(f32)
-                at = slice(g * plen, (g + 1) * plen)
-                acc_k[at] += keep * dk
-                acc_v[at] += keep * dv
-                acc_kd[at] += keep * dkd
-                acc_vd[at] += keep * dvd
+            keeps = [(pick == 1.0 * g).astype(f32).astype(bf16) for g in range(groups)]
+
+            def choose(ref, lo, hi):
+                return sum(
+                    ref[g * plen:(g + 1) * plen, lo:hi] * keep for g, keep in enumerate(keeps)
+                )
+
+            dk, dv, dkd, dvd, dqa, dqd = continuation(
+                src, c, choose(kv, 0, 128), choose(kv, 128, 256), choose(kv, 256, 384),
+                choose(kd, 0, 128), None, keeps,
+            )
+            acc_k[...] += dk
+            acc_v[...] += dv
+            acc_kd[...] += dkd
+            acc_vd[...] += dvd
             pair.append(dqd)
             if own:
                 dq_f[c * clen:(c + 1) * clen] = dqa
@@ -1298,8 +1329,10 @@
         @pl.when(i < first.n)
         def _():
             normed(i)
-            give_xn.copy(i, first.row(i)).wait()
-            second.launch(i)
+
+        @pl.when((i > 0) & (i <= first.n))
+        def _():
+            second.second(i - 1)
 
         @pl.when((i > 0) & (i < n_ctx))
         def _():
@@ -1307,10 +1340,14 @@
 
         @pl.when(i < first.n)
         def _():
-            second.second(i)
-
-    loop(max(half // CH, n_ctx), step)
-    if share:
+            give_xn.copy(i, first.row(i)).wait()
+            second.launch(i)
+
+    loop(max(half // CH + 1, n_ctx), step)
+    if share:
+        settle(0)
+        n_late = (EARLY + bounds[1]) // LINE
+        loop(n_late - EARLY // LINE, lambda k: line.launch(k + EARLY // LINE))
         loop(EARLY // LINE, line.meet)
     loads[13].wait()
 
@@ -1327,7 +1364,7 @@
             )
 
         dk, dv, dkd, dvd, dqa, dqd = continuation(
-            me, c, kv[at, 0:128], kv[at, 128:256], k_d, k_s, mask
+            me, c, kv[at, 0:128], kv[at, 128:256], k_d, k_s, mask, None
         )
         dq_f[c * clen:(c + 1) * clen] += dqa
         keep = low if c == 0 else jnp.logical_not(low)
@@ -1347,10 +1384,11 @@
         at = slice(g * plen, (g + 1) * plen)
         t = tab[0:plen]
         dcat[at, 0:256] = zq
-        dcat[at, 256:384] = turn(acc_k[at], t, -1.0, False).astype(bf16)
-        dcat[at, 384:512] = acc_v[at].astype(bf16)
-        k2 = acc_kd[at] + pltpu.roll(acc_kd[at], 64, 1)
-        v2 = acc_vd[at] + pltpu.roll(acc_vd[at], 64, 1)
+        part = slice(128 * g, 128 * g + 128)
+        dcat[at, 256:384] = turn(acc_k[:, part], t, -1.0, False).astype(bf16)
+        dcat[at, 384:512] = acc_v[:, part].astype(bf16)
+        k2 = acc_kd[:, part] + pltpu.roll(acc_kd[:, part], 64, 1)
+        v2 = acc_vd[:, part] + pltpu.roll(acc_vd[:, part], 64, 1)
         dcat[at, 512:640] = turn(jnp.where(wide, k2, v2), t, -1.0, True).astype(bf16)
 
     loads[14].wait()
@@ -1358,9 +1396,6 @@
         for d in range(1, n_dp):
             kv_grads(cols_of(d), keeper(d))
             give(d, 1).start()
-        settle(0)
-        n_late = (EARLY + bounds[1]) // LINE
-        loop(n_late - EARLY // LINE, lambda k: line.launch(k + EARLY // LINE))
     else:
         for j in range(xn1.shape[1] // 256):
             span = slice(256 * j, 256 * j + 256)
@@ -1512,15 +1547,44 @@
     cx = cont_x.reshape(n_cont, width)
     vectors = (ln1_gain, ln1_bias, ln2_gain, ln2_bias)
     states = vmem((3 * (n_prompt // clen + conts), clen, 128), f32)
-    xn1, kv, tab, w_full, wu, wd, wo, o, lse, msgs, gains, qpack = kernel_call(
+    if share:
+        given = (out_weight, up_weight, down_weight)
+    else:
+        out_w = lax.all_gather(out_weight, "dp", axis=1, tiled=True)
+        given = (
+            jnp.concatenate([out_w[:128], jnp.zeros((64, width), bf16), out_w[128:]], 0),
+            lax.all_gather(up_weight, "dp", axis=0, tiled=True),
+            lax.all_gather(down_weight, "dp", axis=1, tiled=True),
+        )
+    outs = [
+        ((n_rows, width), bf16), ((n_rows, 384), bf16), ((tab_rows, 384), f32),
+        ((640, width), bf16),
+        ((n_rows, 256), bf16), ((8 * conts, clen), f32), ((8 * n_ctx, 128), f32),
+        ((8, width), f32),
+        ((n_cont, width), bf16), ((n_cont, width), bf16), ((n_cont, ff), bf16),
+        ((n_cont, width), bf16), ((n_cont, ff), bf16), ((n_cont, width), bf16),
+        ((n_cont, 256), bf16), ((c_split, width), f32), ((16, width), f32),
+        ((n_ctx, packed, 128), bf16),
+    ]
+    out_specs = [HBM_SPEC] * 4 + [VMEM_SPEC] * 14
+    whole_out = vmem((256, width), bf16)
+    extra = []
+    held = [whole_out]
+    if share:
+        outs += [
+            ((EARLY, depth), bf16), ((width, ff), bf16), ((ff, width), bf16), ((256, width), bf16),
+        ]
+        out_specs += [VMEM_SPEC] + [HBM_SPEC] * 2 + [VMEM_SPEC]
+        held = like(*given)
+        extra = [
+            vmem((n_dp - 1, EARLY, depth), bf16), vmem((n_dp - 1, EARLY, depth), bf16),
+            vmem((EARLY, depth), f32), DMA((n_dp - 1,)), DMA((n_dp - 1,)),
+        ]
+    got = kernel_call(
         functools.partial(front_body, n_ctx, n_dp, share, plen, clen, groups, conts),
+        outs,
         [
-            ((n_rows, width), bf16), ((n_rows, 384), bf16), ((tab_rows, 384), f32),
-            ((640, width), bf16), ((width, ff), bf16), ((ff, width), bf16), ((256, width), bf16),
-            ((n_rows, 256), bf16), ((8 * conts, clen), f32), ((8 * n_ctx, 128), f32),
-            ((8, width), f32), ((packed, 128), bf16),
-        ],
-        [
+            vmem((packed, 128), bf16),
             vmem((n_rows, width), bf16), vmem((n_rows, 256), bf16),
             vmem((n_ctx, n_prompt, 384), bf16), vmem((n_cont, 384), bf16),
             vmem((tab_rows, 384), f32), vmem((640, width), bf16),
@@ -1532,58 +1596,35 @@
             DMA((2, n_ctx, groups)), DMA((n_ctx, groups)), DMA((n_ctx - 1,)), DMA((n_ctx - 1,)),
             DMA((n_dp - 1, 4)), DMA((n_dp - 1, 4)), DMA((9,)),
         ]
-        + like(w_t, px, cx, out_weight, up_weight, down_weight)
-        + [DMA((6,))],
-        0,
-        [SMEM_SPEC] + [HBM_SPEC] * 3 + [VMEM_SPEC] * 5 + [HBM_SPEC] * 3,
-        (cont_group, px, cx, w_t, *vectors, valid_mask, out_weight, up_weight, down_weight),
-        "front",
-        [HBM_SPEC] * 6 + [VMEM_SPEC] * 6,
-    )
-    if not share:
-        out_w = lax.all_gather(out_weight, "dp", axis=1, tiled=True)
-        wu = lax.all_gather(up_weight, "dp", axis=0, tiled=True)
-        wd = lax.all_gather(down_weight, "dp", axis=1, tiled=True)
-        wo = jnp.concatenate([out_w[:128], jnp.zeros((64, width), bf16), out_w[128:]], 0)
-
-    outs = [((EARLY, depth), bf16)] if share else []
-    extra = []
-    if share:
-        extra = [
-            vmem((n_dp - 1, EARLY, depth), bf16), vmem((n_dp - 1, EARLY, depth), bf16),
-            vmem((EARLY, depth), f32), DMA((n_dp - 1,)), DMA((n_dp - 1,)),
-        ]
-    got = kernel_call(
-        functools.partial(middle_body, n_ctx, n_dp, share, n_prompt, clen, depth),
-        outs
+        + like(w_t, px, cx)
+        + [DMA((6,)), vmem((width, ff), bf16), vmem((ff, width), bf16)]
+        + held
         + [
-            ((n_cont, width), bf16), ((n_cont, width), bf16), ((n_cont, ff), bf16),
-            ((n_cont, width), bf16), ((n_cont, ff), bf16), ((n_cont, width), bf16),
-            ((n_cont, 256), bf16), ((c_split, width), f32), ((16, width), f32),
-            ((n_ctx, packed, 128), bf16),
-        ],
-        [
             vmem((4, c_split, width), bf16), vmem((c_split, width), bf16),
             vmem((n_cont, ff), f32), vmem((c_split, width), f32),
             vmem((c_split, width), f32), vmem((clen, 128), f32),
-            DMA((7,)), DMA((n_ctx - 1,)), DMA((n_ctx - 1,)),
-            vmem((n_cont, 256), bf16), vmem((256, width), bf16), vmem((c_split, width), bf16),
-            vmem((width, ff), bf16), vmem((ff, width), bf16),
+            DMA((2,)), DMA((n_ctx - 1,)), DMA((n_ctx - 1,)),
         ]
         + TpSum.scratch(c_split, width) * 3
         + share_scratch(c_split) * 4
         + extra,
-        1,
-        [SMEM_SPEC] * 2
-        + [HBM_SPEC] + [VMEM_SPEC] * 2 + [HBM_SPEC] * 4 + [VMEM_SPEC] * 2 + [HBM_SPEC] * 2,
+        0,
+        [SMEM_SPEC] * 3 + [HBM_SPEC] * 3 + [VMEM_SPEC] * 5 + [HBM_SPEC] * 5,
         (
-            layer_ids, dwa_weights, o, qpack, msgs, wo, wu, wd, cx, gains, valid_mask,
+            cont_group, layer_ids, dwa_weights, px, cx, w_t, *vectors, valid_mask, *given,
             cont_hist.reshape(4, n_cont, width), teacher.reshape(n_cont, width),
         ),
-        "middle",
+        "front",
+        out_specs,
     )
-    cont_out, dm, hid, xn2, du, da, do, dh1, stat, qs = got[-10:]
-    g_first = list(got[:-10])
+    xn1, kv, tab, w_full, o, lse, msgs, gains = got[:8]
+    cont_out, dm, hid, xn2, du, da, do, dh1, stat, qs = got[8:18]
+    if share:
+        g_first = [got[18]]
+        wu, wd, wo = got[19:22]
+    else:
+        g_first = []
+        wo, wu, wd = given
 
     grad_rows = 2 * ff + 12 * HEAD_DIM
     outs = [
@@ -1609,7 +1650,7 @@
         ]
         out_specs += [VMEM_SPEC] * 5
         extra = []
-    acc = vmem((n_prompt, 128), f32)
+    acc = vmem((plen, 128 * groups), f32)
     wide = vmem((split, width), bf16)
     tall = vmem((half, width), bf16)
     n_p, n_h = split // CH, half // CH

time: 226 us -> 218 us (0.965)
  Pallas kernels: 225 us -> 216 us
    pallas_call x3 -> x2, Pallas kernels: 218 us -> 209 us  [kernel_call(): pl.pallas_call(body, out_shape=[jax.ShapeDtypeStruct(s, d) for s, d in ou...]
where the time goes in v5:
time: 218 us; the launch traced here: 217 us
  Pallas kernels  216 us (99%)
    pallas_call x2, Pallas kernels, kernel_call(): pl.pallas_call(body, out_shape=[jax.ShapeDtypeStruct(s, d) for s, d in ou...  209 us
    pallas_call x1, Pallas kernels, per_device(): pl.pallas_call(functools.partial(output_body, n_ctx, n_dp, share, ff), ou...  7.01 us

profile of v5, /device:TPU:0, one launch (start us, length us, event | category | flops | bytes accessed | tf_op | source)
XLA Modules:
  0.0 217.3 jit_solution(18434326571839183178)
XLA Ops:
  0.6 110.2 %front.1 = (bf16[1536,768]{1,0:T(8,128)(2,1)}, bf16[1536,384]{1,0:T(8,128)(2,1)}, f32[768,384]{1,0:T(8,128)}, bf16[640,768]{1,0:T(8,128)(2,1)}, bf16[1536,256]{1...) custom-call(s32[2]{0:T(128)} %sel.1, s32[4]{0:T(128)} %ids.5, ...), custom_call_target="tpu_custom_call" | custom-call | bytes 31457280 | tf_op jit(solution)/shard_map/front/pallas_call | solution.py:55
  110.9 99.3 %back.1 = (bf16[1024,768]{1,0:T(8,128)(2,1)}, bf16[1024,768]{1,0:T(8,128)(2,1)}, bf16[512,768]{1,0:T(8,128)(2,1)}, f32[16,768]{1,0:T(8,128)}, bf16[2304,384]{1,0:T(8,128)(2,1)}) custom-call(s32[4]{0:T(128)} %ids.5, f32[5]{0:T(128)} %dwa.3, f32[32,128]{1,0:T(8,128)} %get-tuple-element.55.msgs, bf16[512,256]{1,0:T(8,128)(2,1)} %get-tuple-element.56.do_h, ...), custom_call_target="tpu_custom_call" | custom-call | bytes 31457280 | tf_op jit(solution)/shard_map/back/pallas_call | solution.py:55
  210.2 7.0 %outputs.1 = (bf16[1024,768]{1,0:T(8,128)(2,1)}, bf16[512,768]{1,0:T(8,128)(2,1)}, bf16[1024,768]{1,0:T(8,128)(2,1)}, bf16[512,768]{1,0:T(8,128)(2,1)}, f32[1]{0...) custom-call(s32[4]{0:T(128)} %ids.5, ...), custom_call_target="tpu_custom_call" | custom-call | tf_op jit(solution)/shard_map/outputs/pallas_call | solution.py:1717

commit v6 on v5

--- a/solution.py
+++ b/solution.py
@@ -24,6 +24,8 @@
 CH = 128
 BIG = 256
 LINE = 192
+SUB = 2
+PIECE = LINE // SUB
 EARLY = 2 * LINE
 
 
@@ -146,9 +148,15 @@
     n_ctx, n_dp, share, plen, clen, groups, conts,
     sel, ids, dwa, px_h, cx_h, w_h, g1, b1, g2, b2, valid, wo_h, wu_h, wd_h, hist, teach, *refs,
 ):
-    xn_o, kv_o, tab_o, w_o, o, lse, msgs, gains = refs[:8]
-    middle_outs = refs[8:18]
-    refs = refs[18:]
+    xn_o, kv_o, tab_o, w_o, o_o, lse, msgs, gains = refs[:8]
+    out, *big, da, do, dh1, stat, qs = refs[8:18]
+    o, *kept, ksem = refs[-6:]
+    middle_outs = (out, *kept, da, do, dh1, stat, qs)
+    leave = [
+        pltpu.make_async_copy(s, d, ksem.at[i])
+        for i, (s, d) in enumerate(zip((o, *kept), (o_o, *big)))
+    ]
+    refs = refs[18:-6]
     if share:
         gdn, wu_o, wd_o, wo_o = refs[:4]
         refs = refs[4:]
@@ -517,8 +525,10 @@
     middle_part(
         n_ctx, n_dp, share, n_prompt, clen, depth, rest_of_prompts,
         ids, dwa, o, qpack, msgs, wo_o, wu_f, wd_f, cx, gains, valid, hist, teach,
-        gdn, middle_outs, refs,
+        gdn, middle_outs, refs, leave,
     )
+    for copy in leave:
+        copy.wait()
     for slot in range(n_ctx):
         for g in range(groups):
             @pl.when((slot <= me) & (me < last))
@@ -658,7 +668,7 @@
 
 def middle_part(
     n_ctx, n_dp, share, n_prompt, clen, depth, between,
-    ids, dwa, o, qpack, msgs, wo, wu, wd, cx, gains, valid, hist, teach, gdn, outs, refs,
+    ids, dwa, o, qpack, msgs, wo, wu, wd, cx, gains, valid, hist, teach, gdn, outs, refs, leave,
 ):
     out, dm, hid, xn, du, da, do, dh1, stat, qs = outs
     hc, tc, slope, h1, dy, mask, hsem, s_q, r_q = refs[:9]
@@ -697,6 +707,7 @@
         for d, device in enumerate(others)
     ]
     between()
+    leave[0].start()
     give_xn = Share(xn, home, shares[0:2])
 
     def normed(i):
@@ -737,6 +748,8 @@
     for copy in loads:
         copy.wait()
     onward(normed, give_xn, second)
+    leave[2].start()
+    leave[3].start()
     for copy in moves:
         copy.start()
     give_dm = Share(dm, home, shares[2:4])
@@ -775,6 +788,8 @@
 
     third = TpSum(half, 0, place, s3, back)
     onward(lossy, give_dm, third)
+    leave[1].start()
+    leave[4].start()
     if share:
         gsnd, grcv, gown, s_g, r_g = scratch[29:34]
         gives = []
@@ -836,7 +851,8 @@
 class LineSum:
     @staticmethod
     def scratch(count, width):
-        buffer = pltpu.VMEM((count, LINE, width), bf16)
+        count = count * SUB
+        buffer = pltpu.VMEM((count, PIECE, width), bf16)
         return [buffer, buffer, buffer, DMA((2, count)), DMA((2, count))]
 
     def __init__(self, me, src, dst, scratch):
@@ -850,7 +866,7 @@
         self.twin = {"ctx": 2 - side}
 
     def at(self, k):
-        return rows(k * LINE, LINE)
+        return rows(k * PIECE, PIECE)
 
     def up(self, k):
         return remote(
@@ -870,36 +886,44 @@
     def launch(self, k):
         @pl.when(self.outer)
         def _():
-            self.up(k).start()
+            for s in range(SUB):
+                self.up(k * SUB + s).start()
 
     def meet(self, k):
         @pl.when(self.inner)
         def _():
-            self.up(k).wait_recv()
-            self.pair[k] = (
-                self.src[self.at(k)].astype(f32) + self.got[k].astype(f32)
-            ).astype(bf16)
-            self.cross(k).start()
+            for s in range(SUB):
+                j = k * SUB + s
+                self.up(j).wait_recv()
+                self.pair[j] = (
+                    self.src[self.at(j)].astype(f32) + self.got[j].astype(f32)
+                ).astype(bf16)
+                self.cross(j).start()
 
     def turn(self, k):
         @pl.when(self.inner)
         def _():
-            self.cross(k).wait()
-            total = (self.pair[k].astype(f32) + self.far[k].astype(f32)).astype(bf16)
-            self.pair[k] = total
-            self.down(k).start()
-            self.dst[self.at(k)] = total
+            for s in range(SUB):
+                j = k * SUB + s
+                self.cross(j).wait()
+                total = (self.pair[j].astype(f32) + self.far[j].astype(f32)).astype(bf16)
+                self.pair[j] = total
+                self.down(j).start()
+                self.dst[self.at(j)] = total
 
     def land(self, k):
         @pl.when(self.outer)
         def _():
-            self.up(k).wait_send()
-            self.down(k).wait_recv()
-            self.dst[self.at(k)] = self.got[k]
+            for s in range(SUB):
+                j = k * SUB + s
+                self.up(j).wait_send()
+                self.down(j).wait_recv()
+                self.dst[self.at(j)] = self.got[j]
 
         @pl.when(self.inner)
         def _():
-            self.down(k).wait_send()
+            for s in range(SUB):
+                self.down(k * SUB + s).wait_send()
 
 
 def input_grad_tail(
@@ -991,7 +1015,6 @@
             value += qrcv[d].astype(f32)
         gall[n_line * LINE:n_line * LINE + 3 * HEAD_DIM] = value.astype(bf16)
         line.launch(n_line)
-    prompts_out()
     if share:
         line.turn(0)
         line.meet(6)
@@ -1023,7 +1046,9 @@
     def part(lo, hi):
         loop(hi - lo, lambda i: finish(i + lo))
 
-    part(0, 4)
+    part(0, 2)
+    prompts_out()
+    part(2, 4)
     to_far.wait()
     stats_c[me] = stats_y[0] + stats_y[1]
     to_ctx = [
@@ -1462,9 +1487,13 @@
     p_out_o, c_out_o, p_grad_o, c_grad_o, loss, dwa_g, g1, b1, g2, b2 = refs[n:n + 10]
     refs = refs[n + 10:]
     if share:
-        r_qkv, r_out, r_up, r_down = refs[:4]
+        results = refs[:4]
         refs = refs[4:]
     held, sem = refs[:4], refs[4]
+    if share:
+        g_all, r_qkv, r_out, r_up, r_down, gsem = refs[5:]
+        g_read = pltpu.make_async_copy(parts[0], g_all, gsem.at[4])
+        g_read.start()
     moves = (
         (p_out, p_out_o), (c_out, c_out_o), (p_grad, p_grad_o), (c_grad, c_grad_o)
     )
@@ -1478,6 +1507,31 @@
         copy.start()
     depth = g1.shape[0]
     width = fin.shape[1]
+    for read, copy in zip(reads, copies):
+        read.wait()
+        copy.start()
+    if share:
+        done = [
+            pltpu.make_async_copy(s, r, gsem.at[i])
+            for i, (s, r) in enumerate(zip((r_qkv, r_out, r_up, r_down), results))
+        ]
+        g_read.wait()
+        rest = g_all.at[ff:]
+        r_down[...] = g_all[0:ff].astype(f32)
+        done[3].start()
+        for j in range(ff // depth):
+            r_up[:, j * depth:(j + 1) * depth] = rest[j * depth:(j + 1) * depth].astype(f32)
+        done[2].start()
+        r_out[...] = rest[ff:ff + 192].astype(f32)
+        done[1].start()
+        base = ff + 192
+        r_qkv[1, 0:128] = rest[base:base + 128].astype(f32)
+        r_qkv[2, 0:128] = rest[base + 128:base + 256].astype(f32)
+        r_qkv[1, 128:192] = rest[base + 256:base + 320].astype(f32)
+        r_qkv[2, 128:192] = rest[base + 320:base + 384].astype(f32)
+        r_qkv[0] = rest[base + 384:base + 576].astype(f32)
+        done[0].start()
+        copies = copies + done
     count = msgs[0:1, 0:1]
     for j in range(1, n_ctx):
         count += msgs[8 * j:8 * j + 1, 0:1]
@@ -1504,21 +1558,6 @@
                 here = fin[i:i + 1, d * depth:(d + 1) * depth]
                 piece += jnp.where(lax.axis_index("dp") == d, here, 0.0)
             ref[...] = piece.reshape(depth)
-    for read, copy in zip(reads, copies):
-        read.wait()
-        copy.start()
-    if share:
-        rest = parts[0].at[ff:]
-        r_down[...] = parts[0][0:ff].astype(f32)
-        for j in range(ff // depth):
-            r_up[:, j * depth:(j + 1) * depth] = rest[j * depth:(j + 1) * depth].astype(f32)
-        r_out[...] = rest[ff:ff + 192].astype(f32)
-        base = ff + 192
-        r_qkv[1, 0:128] = rest[base:base + 128].astype(f32)
-        r_qkv[2, 0:128] = rest[base + 128:base + 256].astype(f32)
-        r_qkv[1, 128:192] = rest[base + 256:base + 320].astype(f32)
-        r_qkv[2, 128:192] = rest[base + 320:base + 384].astype(f32)
-        r_qkv[0] = rest[base + 384:base + 576].astype(f32)
     for copy in copies:
         copy.wait()
 
@@ -1566,7 +1605,10 @@
         ((n_cont, 256), bf16), ((c_split, width), f32), ((16, width), f32),
         ((n_ctx, packed, 128), bf16),
     ]
-    out_specs = [HBM_SPEC] * 4 + [VMEM_SPEC] * 14
+    out_specs = (
+        [HBM_SPEC] * 5 + [VMEM_SPEC] * 4 + [HBM_SPEC] * 4 + [VMEM_SPEC] * 5
+    )
+    leaving = [vmem(s, d) for s, d in outs[4:5] + outs[9:13]] + [DMA((5,))]
     whole_out = vmem((256, width), bf16)
     extra = []
     held = [whole_out]
@@ -1607,7 +1649,8 @@
         ]
         + TpSum.scratch(c_split, width) * 3
         + share_scratch(c_split) * 4
-        + extra,
+        + extra
+        + leaving,
         0,
         [SMEM_SPEC] * 3 + [HBM_SPEC] * 3 + [VMEM_SPEC] * 5 + [HBM_SPEC] * 5,
         (
@@ -1710,10 +1753,14 @@
     specs = [SMEM_SPEC] + [VMEM_SPEC] * 2 + [HBM_SPEC] * 4
     args = (layer_ids, msgs, fin, prompt_out, cont_out, grad_p, grad_c)
     if share:
-        outs += [((3, 192, depth), f32), ((192, depth), f32), ((depth, ff), f32), ((ff, depth), f32)]
-        out_specs += [VMEM_SPEC] * 4
+        shapes = [(3, 192, depth), (192, depth), (depth, ff), (ff, depth)]
+        outs += [(s, f32) for s in shapes]
+        out_specs += [HBM_SPEC] * 4
         args += (back[4],)
-        specs += [VMEM_SPEC]
+        specs += [HBM_SPEC]
+        held_grads = like(back[4]) + [vmem(s, f32) for s in shapes] + [DMA((5,))]
+    else:
+        held_grads = []
     done = pl.pallas_call(
         functools.partial(output_body, n_ctx, n_dp, share, ff),
         out_shape=[jax.ShapeDtypeStruct(s, d) for s, d in outs],
@@ -1722,7 +1769,8 @@
         scratch_shapes=[
             vmem((n_prompt, width), bf16), vmem((n_cont, width), bf16),
             vmem((n_prompt, width), bf16), vmem((n_cont, width), bf16), DMA((2, 4)),
-        ],
+        ]
+        + held_grads,
         compiler_params=pltpu.CompilerParams(vmem_limit_bytes=LIMIT),
         name="outputs",
     )(*args)

time: 218 us -> 216 us (level)
  no operation moved by 1% of the time
where the time goes in v6:
time: 216 us
  Pallas kernels  215 us (100%)
    pallas_call x2, Pallas kernels, kernel_call(): pl.pallas_call(body, out_shape=[jax.ShapeDtypeStruct(s, d) for s, d in ou...  208 us
    pallas_call x1, Pallas kernels, per_device(): pl.pallas_call(functools.partial(output_body, n_ctx, n_dp, share, ff), ou...  6.75 us

profile of v6, /device:TPU:0, one launch (start us, length us, event | category | flops | bytes accessed | tf_op | source)
XLA Modules:
  0.0 216.0 jit_solution(15389569756235807488)
XLA Ops:
  0.6 109.2 %front.1 = (bf16[1536,768]{1,0:T(8,128)(2,1)}, bf16[1536,384]{1,0:T(8,128)(2,1)}, f32[768,384]{1,0:T(8,128)}, bf16[640,768]{1,0:T(8,128)(2,1)}, bf16[1536,256]{1...) custom-call(s32[2]{0:T(128)} %sel.1, s32[4]{0:T(128)} %ids.5, ...), custom_call_target="tpu_custom_call" | custom-call | bytes 31457280 | tf_op jit(solution)/shard_map/front/pallas_call | solution.py:57
  109.8 99.3 %back.1 = (bf16[1024,768]{1,0:T(8,128)(2,1)}, bf16[1024,768]{1,0:T(8,128)(2,1)}, bf16[512,768]{1,0:T(8,128)(2,1)}, f32[16,768]{1,0:T(8,128)}, bf16[2304,384]{1,0:T(8,128)(2,1)}) custom-call(s32[4]{0:T(128)} %ids.5, f32[5]{0:T(128)} %dwa.3, f32[32,128]{1,0:T(8,128)} %get-tuple-element.55.msgs, bf16[512,256]{1,0:T(8,128)(2,1)} %get-tuple-element.56.do_h, ...), custom_call_target="tpu_custom_call" | custom-call | bytes 31457280 | tf_op jit(solution)/shard_map/back/pallas_call | solution.py:57
  209.1 6.7 %outputs.1 = (bf16[1024,768]{1,0:T(8,128)(2,1)}, bf16[512,768]{1,0:T(8,128)(2,1)}, bf16[1024,768]{1,0:T(8,128)(2,1)}, bf16[512,768]{1,0:T(8,128)(2,1)}, f32[1]{0...) custom-call(s32[4]{0:T(128)} %ids.5, ...), custom_call_target="tpu_custom_call" | custom-call | tf_op jit(solution)/shard_map/outputs/pallas_call | solution.py:1764

commit v7 on v6

--- a/solution.py
+++ b/solution.py
@@ -929,7 +929,7 @@
 def input_grad_tail(
     n_dp, n_ctx, share, split, c_split, depth,
     dcat, w, px, cx, gains, dh1, stat_in, xn1, grad_p, grad_c, fin,
-    smalls, sums, shares, prompts_out, *q_state,
+    smalls, sums, shares, prompts_out, prompts_done, *q_state,
 ):
     grad, stat, stats_m, stats_y, stats_c, stats_d, s_s, r_s, osem = smalls
     core, mate, across = tp_place()
@@ -1074,6 +1074,7 @@
     if share:
         for k in range(10, n_line + 1):
             line.turn(k)
+    prompts_done()
     loop(total.n, lambda i: give.copy(i, total.row(i)).wait())
     saves = fetch(
         ((grad.at[0:n_prompt], grad_p), (grad.at[n_prompt:n_prompt + n_cont], grad_c)), osem
@@ -1096,16 +1097,17 @@
     wo_h, wu_h, wd_h, px_h, hist_h, xn1_h, w_h, cx_h, dh1_h, stat_in, *refs,
 ):
     if share:
-        g_first, out, grad_p, grad_c, fin, g_sum = refs[:6]
+        g_first, out_o, grad_p, grad_c, fin, g_sum = refs[:6]
         refs = refs[6:]
     else:
-        out, grad_p, grad_c, fin, g_down, g_up, g_out, g_kv, g_q = refs[:9]
+        out_o, grad_p, grad_c, fin, g_down, g_up, g_out, g_kv, g_q = refs[:9]
         refs = refs[9:]
     (
         hid, dm, xn2, du, da, wo, wu, wd, px, hist, lsem,
         dos, sts, dqs, kd, acc_k, acc_v, acc_kd, acc_vd, dq_f, send, recv,
         xp, h1, xn1, flags, do, o, kv, tab, qs, w, cx, dh1, dcat,
     ) = refs[:35]
+    out, refs = refs[-1], refs[:-1]
     snd1, own = refs[35:37]
     s1 = (snd1, refs[37], refs[39], refs[38], own, *refs[40:42])
     s2 = (snd1, refs[42], refs[39], refs[43], own, *refs[44:46])
@@ -1462,6 +1464,12 @@
         loads[15].wait()
         loop(half // CH, mixed)
 
+    leave_out = pltpu.make_async_copy(out, out_o, lsem.at[20])
+
+    def prompts_done():
+        loop(half // CH, lambda i: give_out.copy(i, second.row(i)).wait())
+        leave_out.start()
+
     for copy in loads[16:19]:
         copy.wait()
     if share:
@@ -1471,9 +1479,9 @@
     input_grad_tail(
         n_dp, n_ctx, share, plen, clen, depth,
         dcat, w, px, cx, gains, dh1, stat_in, xn1, grad_p, grad_c, fin,
-        smalls, s3, shares[4:6], prompts_out, *q_state,
+        smalls, s3, shares[4:6], prompts_out, prompts_done, *q_state,
     )
-    loop(half // CH, lambda i: give_out.copy(i, second.row(i)).wait())
+    leave_out.wait()
     for copy in sends:
         copy.wait_send()
 
@@ -1674,7 +1682,7 @@
         ((n_prompt, width), bf16), ((n_prompt, width), bf16), ((n_cont, width), bf16),
         ((16, width), f32),
     ]
-    out_specs = [VMEM_SPEC] + [HBM_SPEC] * 2 + [VMEM_SPEC]
+    out_specs = [HBM_SPEC] * 3 + [VMEM_SPEC]
     if share:
         outs += [((grad_rows, depth), bf16)]
         out_specs += [VMEM_SPEC]
@@ -1707,7 +1715,7 @@
             vmem((n_cont, width), bf16), vmem((n_cont, ff), bf16),
             vmem((n_cont, width), bf16), vmem((256, width), bf16),
             vmem((width, ff), bf16), vmem((ff, width), bf16),
-            vmem((n_prompt, width), bf16), vmem((4, split, width), bf16), DMA((20,)),
+            vmem((n_prompt, width), bf16), vmem((4, split, width), bf16), DMA((21,)),
             vmem((n_ctx, packed, 128), bf16), vmem((n_ctx, 8 * conts, clen), f32),
             vmem((2 * n_ctx, packed, 128), bf16), vmem((n_prompt, 128), bf16),
             acc, acc, acc, acc, vmem((packed, 128), f32),
@@ -1730,7 +1738,8 @@
             vmem((n_dp, 16, width), f32),
             DMA((1 + n_ctx + n_dp,)), DMA((1 + n_ctx + n_dp,)), DMA((2,)),
         ]
-        + extra,
+        + extra
+        + [vmem((n_prompt, width), bf16)],
         2,
         [SMEM_SPEC] * 2
         + [VMEM_SPEC] + [HBM_SPEC] * 2 + [VMEM_SPEC] * 3 + [HBM_SPEC] * 17 + [VMEM_SPEC]

time: 216 us -> 216 us (level)
  no operation moved by 1% of the time
where the time goes in v7:
time: 216 us; the launch traced here: 215 us
  Pallas kernels  215 us (100%)
    pallas_call x2, Pallas kernels, kernel_call(): pl.pallas_call(body, out_shape=[jax.ShapeDtypeStruct(s, d) for s, d in ou...  208 us
    pallas_call x1, Pallas kernels, per_device(): pl.pallas_call(functools.partial(output_body, n_ctx, n_dp, share, ff), ou...  6.75 us

profile of v7, /device:TPU:0, one launch (start us, length us, event | category | flops | bytes accessed | tf_op | source)
XLA Modules:
  0.0 215.5 jit_solution(10215151381528661088)
XLA Ops:
  0.6 109.2 %front.1 = (bf16[1536,768]{1,0:T(8,128)(2,1)}, bf16[1536,384]{1,0:T(8,128)(2,1)}, f32[768,384]{1,0:T(8,128)}, bf16[640,768]{1,0:T(8,128)(2,1)}, bf16[1536,256]{1...) custom-call(s32[2]{0:T(128)} %sel.1, s32[4]{0:T(128)} %ids.5, ...), custom_call_target="tpu_custom_call" | custom-call | bytes 31457280 | tf_op jit(solution)/shard_map/front/pallas_call | solution.py:57
  109.8 98.7 %back.1 = (bf16[1024,768]{1,0:T(8,128)(2,1)}, bf16[1024,768]{1,0:T(8,128)(2,1)}, bf16[512,768]{1,0:T(8,128)(2,1)}, f32[16,768]{1,0:T(8,128)}, bf16[2304,384]{1,0:T(8,128)(2,1)}) custom-call(s32[4]{0:T(128)} %ids.5, f32[5]{0:T(128)} %dwa.3, f32[32,128]{1,0:T(8,128)} %get-tuple-element.55.msgs, bf16[512,256]{1,0:T(8,128)(2,1)} %get-tuple-element.56.do_h, ...), custom_call_target="tpu_custom_call" | custom-call | bytes 31457280 | tf_op jit(solution)/shard_map/back/pallas_call | solution.py:57
  208.5 6.7 %outputs.1 = (bf16[1024,768]{1,0:T(8,128)(2,1)}, bf16[512,768]{1,0:T(8,128)(2,1)}, bf16[1024,768]{1,0:T(8,128)(2,1)}, bf16[512,768]{1,0:T(8,128)(2,1)}, f32[1]{0...) custom-call(s32[4]{0:T(128)} %ids.5, ...), custom_call_target="tpu_custom_call" | custom-call | tf_op jit(solution)/shard_map/outputs/pallas_call | solution.py:1773
